TPU v7x, 32 devices: a whole 2x2x4 slice. The times are simulated.
32 devices in a mesh: dp: 8 (over z, y), tp: 4 (over x, core).
Axes of the slice: x: 2, y: 2, z: 4, core: 2. Of those that a mesh axis runs over, the one named last changes fastest.
Arguments:
- hidden_in: float32 [2048, 2048], P('dp'), may hold values from -6 to 6
- cotangent: float32 [2048, 2048], P('dp'), may hold values from -6 to 6
- segment_ids: int32 [8, 256], P('dp'), may hold values from 0 to 3, never falling along the last dimension, each value on 1 to 128 neighbouring positions
- expert_ids: int32 [2048, 8], P('dp'), may hold values from 0 to 63, all different within a row; in each aligned block of 256 rows (0 to 255, 256 to 511, ...) at most 48 rows name the same one
- first_gain: bfloat16 [2048], P('dp'), may hold values from 0.5 to 1.5
- query_weight: bfloat16 [2048, 2048], P('dp', 'tp'), may hold values from -4 to 4
- key_weight: bfloat16 [2048, 2048], P('dp', 'tp'), may hold values from -4 to 4
- value_weight: bfloat16 [2048, 2048], P('dp', 'tp'), may hold values from -0.125 to 0.125
- output_weight: bfloat16 [2048, 2048], P('tp', 'dp'), may hold values from -0.375 to 0.375
- query_gain: bfloat16 [16, 128], P('tp', 'dp'), may hold values from 0.5 to 1.5
- key_gain: bfloat16 [16, 128], P('tp', 'dp'), may hold values from 0.5 to 1.5
- second_gain: bfloat16 [2048], P('dp'), may hold values from 0.5 to 1.5
- router_weight: bfloat16 [2048, 64], P('dp'), may hold values from -0.0625 to 0.0625
- gate_weight: bfloat16 [64, 2048, 1024], P('dp', None, 'tp'), may hold values from -0.125 to 0.125
- up_weight: bfloat16 [64, 2048, 1024], P('dp', None, 'tp'), may hold values from -0.125 to 0.125
- down_weight: bfloat16 [64, 1024, 2048], P('dp', 'tp'), may hold values from -6 to 6
Outputs:
- hidden_out: float32 [2048, 2048], P('dp')
- grad_hidden: float32 [2048, 2048], P('dp')
- grad_first_gain: float32 [2048], P('dp')
- grad_query: float32 [2048, 2048], P('dp', 'tp')
- grad_key: float32 [2048, 2048], P('dp', 'tp')
- grad_value: float32 [2048, 2048], P('dp', 'tp')
- grad_output: float32 [2048, 2048], P('tp', 'dp')
- grad_query_gain: float32 [16, 128], P('tp', 'dp')
- grad_key_gain: float32 [16, 128], P('tp', 'dp')
- grad_second_gain: float32 [2048], P('dp')
- grad_router: float32 [2048, 64], P('dp')
- grad_gate: float32 [64, 2048, 1024], P('dp', None, 'tp')
- grad_up: float32 [64, 2048, 1024], P('dp', None, 'tp')
- grad_down: float32 [64, 1024, 2048], P('dp', 'tp')
Inputs may be any that keep to these rules, and one draw needn't show every extreme that they name: `expert_ids`: each row names 8 different experts. Within one sequence no expert is named by more than 48 rows, a bound that some block reaches. `segment_ids`: within each sequence the numbers never fall; each document has 1 to 128 tokens and some document has exactly 128.
All inputs are finite; a program needn't handle non-finite values.
Results may differ from a plain program's by a relative error of at most 0.017.
Values may be sent and summed in bfloat16 or wider, within the bound.
No kernel may reach another device: no remote copies, remote signals or barrier semaphores. Data moves between devices by JAX's collectives and lax.ppermute only.
A program may use at most 384 MiB of HBM per device.

v0:
```python
import math

import jax
import jax.numpy as jnp
from jax import lax
from jax.sharding import PartitionSpec as P

D = 2048
HD = 128
E = 64
TOPK = 8
CAP = 48


epsilon = 1e-05


def rms_scale(values):
    return lax.rsqrt(jnp.mean(values * values, axis=-1, keepdims=True) + epsilon)


def rms_back(values, scale, scaled_grad):
    return scale * scaled_grad - values * scale**3 * jnp.mean(
        scaled_grad * values, axis=-1, keepdims=True
    )


def rope_tables(length, head_size):
    half_size = head_size // 2
    inverse = 10000.0 ** (-2.0 * jnp.arange(half_size, dtype=jnp.float32) / head_size)
    angles = jnp.arange(length, dtype=jnp.float32)[:, None] * inverse[None, :]
    return (jnp.cos(angles)[:, None, :], jnp.sin(angles)[:, None, :])


def rotate(values, cosine, sine_table):
    half_size = values.shape[-1] // 2
    leading, second = (values[..., :half_size], values[..., half_size:])
    return jnp.concatenate(
        [leading * cosine - second * sine_table, second * cosine + leading * sine_table], axis=-1
    )


def unrotate(values, cosine, sine_table):
    half_size = values.shape[-1] // 2
    leading, second = (values[..., :half_size], values[..., half_size:])
    return jnp.concatenate(
        [leading * cosine + second * sine_table, second * cosine - leading * sine_table], axis=-1
    )


def allowed_mask(segments):
    position = jnp.arange(segments.shape[0], dtype=jnp.int32)
    return (position[None, :] <= position[:, None]) & (segments[:, None] == segments[None, :])


def score_table(queries, key_rows, segments):
    score_scale = 1.0 / math.sqrt(queries.shape[-1])
    scores = (
        jnp.einsum("qhd,khd->hqk", queries, key_rows, preferred_element_type=jnp.float32)
        * score_scale
    )
    allowed = allowed_mask(segments)[None]
    return (jnp.where(allowed, scores, -1e30), allowed, score_scale)


def attend_local(queries, key_rows, value_rows, segments):
    scores, allowed, score_scale = score_table(queries, key_rows, segments)
    largest = jnp.max(scores, axis=-1, keepdims=True)
    denominator = jnp.sum(
        jnp.where(allowed, jnp.exp(scores - largest), 0.0), axis=-1, keepdims=True
    )
    log_total = largest + jnp.log(denominator)
    weights = jnp.where(allowed, jnp.exp(scores - log_total), 0.0).astype(jnp.bfloat16)
    mixture = jnp.einsum("hqk,khd->qhd", weights, value_rows, preferred_element_type=jnp.float32)
    return (mixture.astype(jnp.bfloat16), log_total)


def attend_local_back(queries, key_rows, value_rows, segments, log_total, grad_mixture):
    scores, allowed, score_scale = score_table(queries, key_rows, segments)
    full_probs = jnp.where(allowed, jnp.exp(scores - log_total), 0.0)
    low_probs = full_probs.astype(jnp.bfloat16)
    grad_values = jnp.einsum(
        "hqk,qhd->khd", low_probs, grad_mixture, preferred_element_type=jnp.float32
    )
    grad_attn = jnp.einsum(
        "qhd,khd->hqk", grad_mixture, value_rows, preferred_element_type=jnp.float32
    )
    row_dot = jnp.sum(full_probs * grad_attn, axis=-1, keepdims=True)
    grad_scores = (full_probs * (grad_attn - row_dot) * score_scale).astype(jnp.bfloat16)
    grad_queries = jnp.einsum(
        "hqk,khd->qhd", grad_scores, key_rows, preferred_element_type=jnp.float32
    )
    grad_keys = jnp.einsum("hqk,qhd->khd", grad_scores, queries, preferred_element_type=jnp.float32)
    return (grad_queries, grad_keys, grad_values)


def slot_table(expert_ids, experts, capacity):
    flat_ids = expert_ids.reshape(-1)
    assignments = flat_ids.shape[0]
    matches = (flat_ids[:, None] == jnp.arange(experts, dtype=jnp.int32)[None, :]).astype(jnp.int32)
    earlier = jnp.sum((jnp.cumsum(matches, axis=0) - matches) * matches, axis=1)
    places = flat_ids * capacity + earlier
    slot_owner = (
        jnp.full((experts * capacity,), assignments, jnp.int32)
        .at[places]
        .set(jnp.arange(assignments, dtype=jnp.int32))
    )
    return (slot_owner, places.reshape(expert_ids.shape))


def rounded_wide(values):
    return lax.optimization_barrier(values.astype(jnp.bfloat16)).astype(jnp.float32)


def per_device(
    hidden_in,
    cotangent,
    segment_ids,
    expert_ids,
    first_gain,
    query_weight,
    key_weight,
    value_weight,
    output_weight,
    query_gain,
    key_gain,
    second_gain,
    router_weight,
    gate_weight,
    up_weight,
    down_weight,
):
    data_size = lax.axis_size("dp")
    tensor_size = lax.axis_size("tp")
    seq_len, width = hidden_in.shape
    gathered = (
        lax.all_gather(query_weight, "dp", axis=0, tiled=True),
        lax.all_gather(key_weight, "dp", axis=0, tiled=True),
        lax.all_gather(value_weight, "dp", axis=0, tiled=True),
        lax.all_gather(output_weight, "dp", axis=1, tiled=True),
        lax.all_gather(router_weight, "dp", axis=0, tiled=True),
        lax.all_gather(first_gain, "dp", axis=0, tiled=True),
        lax.all_gather(second_gain, "dp", axis=0, tiled=True),
        lax.all_gather(query_gain, "dp", axis=1, tiled=True),
        lax.all_gather(key_gain, "dp", axis=1, tiled=True),
    )
    (
        query_full,
        key_full,
        value_full,
        output_full,
        router_full,
        gain_one,
        gain_two,
        query_gains,
        key_gains,
    ) = gathered
    gain_one = gain_one.astype(jnp.float32)
    gain_two = gain_two.astype(jnp.float32)
    heads_local = query_full.shape[1] // HD
    query_gains = query_gains.astype(jnp.float32).reshape(-1)
    key_gains = key_gains.astype(jnp.float32).reshape(-1)
    segments = segment_ids[0]
    first_scale = rms_scale(hidden_in)
    normed_one = (hidden_in * first_scale * gain_one).astype(jnp.bfloat16)
    queries = jnp.dot(normed_one, query_full, preferred_element_type=jnp.float32)
    key_proj = jnp.dot(normed_one, key_full, preferred_element_type=jnp.float32)
    value_proj = jnp.dot(normed_one, value_full, preferred_element_type=jnp.float32).astype(
        jnp.bfloat16
    )
    query_squares, key_squares = lax.psum(
        (jnp.sum(queries * queries, axis=-1), jnp.sum(key_proj * key_proj, axis=-1)), "tp"
    )
    query_scale = lax.rsqrt(query_squares[:, None] / D + epsilon)
    key_scale = lax.rsqrt(key_squares[:, None] / D + epsilon)
    query_normed = queries * query_scale * query_gains
    key_normed = key_proj * key_scale * key_gains
    cosine, sine_table = rope_tables(seq_len, HD)
    query_rot = rotate(query_normed.reshape(seq_len, heads_local, HD), cosine, sine_table).astype(
        jnp.bfloat16
    )
    key_rot = rotate(key_normed.reshape(seq_len, heads_local, HD), cosine, sine_table).astype(
        jnp.bfloat16
    )
    value_heads = value_proj.reshape(seq_len, heads_local, HD)
    attended_heads, log_total = attend_local(query_rot, key_rot, value_heads, segments)
    attended = attended_heads.reshape(seq_len, heads_local * HD)
    middle = hidden_in + lax.psum(
        jnp.dot(attended, output_full, preferred_element_type=jnp.float32), "tp"
    )
    second_scale = rms_scale(middle)
    normed_two = (middle * second_scale * gain_two).astype(jnp.bfloat16)
    logits = jnp.dot(normed_two, router_full, preferred_element_type=jnp.float32)
    router_probs = jax.nn.softmax(logits, axis=-1)
    chosen = expert_ids[:, :, None] == jnp.arange(E, dtype=jnp.int32)[None, None, :]
    mix_weights = jnp.sum(jnp.where(chosen, router_probs[:, None, :], 0.0), axis=-1)
    slot_owner, places = slot_table(expert_ids, E, CAP)
    local_experts = E // data_size
    share_size = CAP // tensor_size
    owner_table = slot_owner.reshape(E, CAP)
    normed_pad = jnp.concatenate([normed_two, jnp.zeros((1, width), jnp.bfloat16)], axis=0)
    weighted_grads = (
        (mix_weights[:, :, None] * cotangent[:, None, :])
        .astype(jnp.bfloat16)
        .reshape(seq_len * TOPK, width)
    )
    weighted_pad = jnp.concatenate([weighted_grads, jnp.zeros((1, width), jnp.bfloat16)], axis=0)
    own_owners = lax.dynamic_slice_in_dim(
        owner_table, lax.axis_index("tp") * share_size, share_size, 1
    )
    own_rows = normed_pad[own_owners // TOPK].reshape(data_size, local_experts, share_size, width)
    own_grads = weighted_pad[own_owners].reshape(data_size, local_experts, share_size, width)
    arrived_rows, arrived_grads = (
        lax.all_to_all(own_rows, "dp", split_axis=0, concat_axis=0, tiled=True),
        lax.all_to_all(own_grads, "dp", split_axis=0, concat_axis=0, tiled=True),
    )
    received, grad_received = (
        lax.all_gather(arrived_rows, "tp", axis=2, tiled=True),
        lax.all_gather(arrived_grads, "tp", axis=2, tiled=True),
    )
    gate_act = jnp.einsum(
        "secd,edf->secf", received, gate_weight, preferred_element_type=jnp.float32
    )
    up_act = jnp.einsum("secd,edf->secf", received, up_weight, preferred_element_type=jnp.float32)
    hidden_act = (jax.nn.silu(gate_act) * up_act).astype(jnp.bfloat16)
    part_sum = jnp.einsum(
        "secf,efd->secd", hidden_act, down_weight, preferred_element_type=jnp.float32
    )
    quarter_sum = lax.psum_scatter(rounded_wide(part_sum), "tp", scatter_dimension=2, tiled=True)
    returned = lax.all_to_all(quarter_sum, "dp", split_axis=0, concat_axis=0, tiled=True).reshape(
        E * share_size, width
    )
    row_index = places // CAP * share_size + places % share_size
    keep = places % CAP // share_size == lax.axis_index("tp")
    moe_part = jnp.zeros((seq_len, width), jnp.float32)
    grad_mix_cols = []
    for pick_index in range(TOPK):
        picked = jnp.where(
            keep[:, pick_index : pick_index + 1], returned[row_index[:, pick_index]], 0.0
        )
        moe_part = moe_part + mix_weights[:, pick_index : pick_index + 1] * picked
        grad_mix_cols.append(jnp.sum(cotangent * picked, axis=-1))
    hidden_out = middle + lax.psum(moe_part, "tp")
    grad_mix_part = jnp.stack(grad_mix_cols, axis=1)
    grad_hidden_act = jnp.einsum(
        "secd,efd->secf", grad_received, down_weight, preferred_element_type=jnp.float32
    )
    grad_down = jnp.einsum(
        "secf,secd->efd", hidden_act, grad_received, preferred_element_type=jnp.float32
    )
    sigmoid_gate = jax.nn.sigmoid(gate_act)
    grad_gate_act = (
        grad_hidden_act * up_act * sigmoid_gate * (1.0 + gate_act * (1.0 - sigmoid_gate))
    ).astype(jnp.bfloat16)
    grad_up_act = (grad_hidden_act * gate_act * sigmoid_gate).astype(jnp.bfloat16)
    grad_gate = jnp.einsum(
        "secd,secf->edf", received, grad_gate_act, preferred_element_type=jnp.float32
    )
    grad_up = jnp.einsum(
        "secd,secf->edf", received, grad_up_act, preferred_element_type=jnp.float32
    )
    grad_input_sum = jnp.einsum(
        "secf,edf->secd", grad_gate_act, gate_weight, preferred_element_type=jnp.float32
    )
    grad_input_sum = grad_input_sum + jnp.einsum(
        "secf,edf->secd", grad_up_act, up_weight, preferred_element_type=jnp.float32
    )
    grad_quarter = lax.psum_scatter(
        rounded_wide(grad_input_sum), "tp", scatter_dimension=2, tiled=True
    )
    grad_back = lax.all_to_all(grad_quarter, "dp", split_axis=0, concat_axis=0, tiled=True).reshape(
        E * share_size, width
    )
    grad_normed_part = jnp.zeros((seq_len, width), jnp.float32)
    for pick_index in range(TOPK):
        grad_normed_part = grad_normed_part + jnp.where(
            keep[:, pick_index : pick_index + 1], grad_back[row_index[:, pick_index]], 0.0
        )
    grad_probs = jnp.sum(jnp.where(chosen, grad_mix_part[:, :, None], 0.0), axis=1)
    grad_logits_part = router_probs * (
        grad_probs - jnp.sum(router_probs * grad_probs, axis=-1, keepdims=True)
    )
    grad_normed_part = grad_normed_part + jnp.dot(
        grad_logits_part, router_full.astype(jnp.float32).T, precision=lax.Precision.HIGHEST
    )
    grad_normed_two, grad_logits = lax.psum((grad_normed_part, grad_logits_part), "tp")
    grad_router = jnp.dot(
        normed_two.astype(jnp.float32).T, grad_logits, precision=lax.Precision.HIGHEST
    )
    grad_second_gain = jnp.sum(grad_normed_two * middle * second_scale, axis=0)
    grad_middle = cotangent + rms_back(middle, second_scale, grad_normed_two * gain_two)
    grad_middle_low = grad_middle.astype(jnp.bfloat16)
    grad_output = jnp.dot(attended.T, grad_middle_low, preferred_element_type=jnp.float32)
    grad_attended = jnp.dot(
        grad_middle_low, output_full.T, preferred_element_type=jnp.float32
    ).astype(jnp.bfloat16)
    grad_query_rot, grad_key_rot, grad_values = attend_local_back(
        query_rot,
        key_rot,
        value_heads,
        segments,
        log_total,
        grad_attended.reshape(seq_len, heads_local, HD),
    )
    grad_query_normed = unrotate(grad_query_rot, cosine, sine_table).reshape(seq_len, -1)
    grad_key_normed = unrotate(grad_key_rot, cosine, sine_table).reshape(seq_len, -1)
    grad_query_gain = jnp.sum(grad_query_normed * queries * query_scale, axis=0).reshape(
        heads_local, HD
    )
    grad_key_gain = jnp.sum(grad_key_normed * key_proj * key_scale, axis=0).reshape(heads_local, HD)
    query_scaled_grad = grad_query_normed * query_gains
    key_scaled_grad = grad_key_normed * key_gains
    query_inner, key_inner = lax.psum(
        (
            jnp.sum(query_scaled_grad * queries, axis=-1),
            jnp.sum(key_scaled_grad * key_proj, axis=-1),
        ),
        "tp",
    )
    grad_queries = (
        query_scale * query_scaled_grad - queries * query_scale**3 * (query_inner[:, None] / D)
    ).astype(jnp.bfloat16)
    grad_keys = (
        key_scale * key_scaled_grad - key_proj * key_scale**3 * (key_inner[:, None] / D)
    ).astype(jnp.bfloat16)
    grad_values_low = grad_values.reshape(seq_len, -1).astype(jnp.bfloat16)
    grad_query = jnp.dot(normed_one.T, grad_queries, preferred_element_type=jnp.float32)
    grad_key = jnp.dot(normed_one.T, grad_keys, preferred_element_type=jnp.float32)
    grad_value = jnp.dot(normed_one.T, grad_values_low, preferred_element_type=jnp.float32)
    grad_normed_local = jnp.dot(grad_queries, query_full.T, preferred_element_type=jnp.float32)
    grad_normed_local = grad_normed_local + jnp.dot(
        grad_keys, key_full.T, preferred_element_type=jnp.float32
    )
    grad_normed_local = grad_normed_local + jnp.dot(
        grad_values_low, value_full.T, preferred_element_type=jnp.float32
    )
    grad_normed_one = lax.psum(grad_normed_local, "tp")
    grad_first_gain = jnp.sum(grad_normed_one * hidden_in * first_scale, axis=0)
    grad_hidden = grad_middle + rms_back(hidden_in, first_scale, grad_normed_one * gain_one)
    summed = (
        lax.psum_scatter(grad_query, "dp", scatter_dimension=0, tiled=True),
        lax.psum_scatter(grad_key, "dp", scatter_dimension=0, tiled=True),
        lax.psum_scatter(grad_value, "dp", scatter_dimension=0, tiled=True),
        lax.psum_scatter(grad_output, "dp", scatter_dimension=1, tiled=True),
        lax.psum_scatter(grad_router, "dp", scatter_dimension=0, tiled=True),
        lax.psum_scatter(grad_first_gain, "dp", scatter_dimension=0, tiled=True),
        lax.psum_scatter(grad_second_gain, "dp", scatter_dimension=0, tiled=True),
        lax.psum_scatter(grad_query_gain, "dp", scatter_dimension=1, tiled=True),
        lax.psum_scatter(grad_key_gain, "dp", scatter_dimension=1, tiled=True),
    )
    (
        grad_query,
        grad_key,
        grad_value,
        grad_output,
        grad_router,
        grad_first_gain,
        grad_second_gain,
        grad_query_gain,
        grad_key_gain,
    ) = summed
    return (
        hidden_out,
        grad_hidden,
        grad_first_gain,
        grad_query,
        grad_key,
        grad_value,
        grad_output,
        grad_query_gain,
        grad_key_gain,
        grad_second_gain,
        grad_router,
        grad_gate,
        grad_up,
        grad_down,
    )


def solution(mesh):
    return jax.shard_map(
        per_device,
        mesh=mesh,
        in_specs=(
            P("dp", None),
            P("dp", None),
            P("dp", None),
            P("dp", None),
            P("dp"),
            P("dp", "tp"),
            P("dp", "tp"),
            P("dp", "tp"),
            P("tp", "dp"),
            P("tp", "dp"),
            P("tp", "dp"),
            P("dp"),
            P("dp", None),
            P("dp", None, "tp"),
            P("dp", None, "tp"),
            P("dp", "tp", None),
        ),
        out_specs=(
            P("dp", None),
            P("dp", None),
            P("dp"),
            P("dp", "tp"),
            P("dp", "tp"),
            P("dp", "tp"),
            P("tp", "dp"),
            P("tp", "dp"),
            P("tp", "dp"),
            P("dp"),
            P("dp", None),
            P("dp", None, "tp"),
            P("dp", None, "tp"),
            P("dp", "tp", None),
        ),
        check_vma=False,
    )
```

profile of v0, /device:TPU:0, one launch (start us, length us, event | category | flops | bytes accessed | tf_op | source)
XLA Modules:
  0.0 2340.1 jit_solution(4034197804295648224)
XLA Ops:
  10.8 22.3 all-gather
  35.5 16.4 all-gather.1
  52.5 18.3 all-gather.2
  77.7 16.5 all-gather.3
  94.2 34.6 %reduce-window.6 = s32[64,16,128]{2,1,0:T(8,128)} reduce-window(s32[64,16,128]{2,1,0:T(8,128)} %fusion.69, s32[]{:T(128)} %constant.89.clone.1), window={size=1x1x128 pad=0_0x0_0x127_0}, to_apply=%region_12.13 | reduce-window | flops 16646144 | bytes 1048580 | tf_op jit(solution)/shard_map/reduce-window
  170.5 43.3 %all-gather.17.cloned.1.call-done = bf16[512,2048]{1,0:T(8,128)(2,1)} async-done(((bf16[512,256]{1,0:T(8,128)(2,1)}), bf16[512,2048]{1,0:T(8,128)(2,1)}) %all-gather.17.cloned.1.call-update) | async-done | bytes 2097168 | tf_op jit(solution)/shard_map/all_gather | solution.py:140
  227.7 39.4 %all-reduce.12.cloned.1.call-done = f32[256,2048]{1,0:T(8,128)} async-done(((f32[256,2048]{1,0:T(8,128)}), f32[256,2048]{1,0:T(8,128)}) %all-reduce.12.cloned.1.call-update) | async-done | bytes 2097168 | tf_op jit(solution)/shard_map/psum | solution.py:188
  285.0 76.0 %all_to_all.20 = bf16[8,8,12,2048]{3,1,2,0:T(8,128)(2,1)S(1)} all-to-all(bf16[8,8,12,2048]{3,1,2,0:T(8,128)(2,1)S(1)} %copy.213), channel_id=1, replica_groups=mesh['dp'=8,'tp'=4] {'dp'}, dimensions={0} | all-to-all | bytes 6291456 | tf_op jit(solution)/shard_map/all_to_all | solution.py:214
  363.1 80.5 %all-gather.19.cloned.1.call-done = bf16[8,8,48,2048]{3,1,0,2:T(8,128)(2,1)} async-done(((bf16[8,8,12,2048]{3,1,0,2:T(8,128)(2,1)}), bf16[8,8,48,2048]{3,1,0,2:T(8,128)(2,1)}) %all-gather.19.cloned.1.call-update) | async-done | bytes 12582928 | tf_op jit(solution)/shard_map/all_gather | solution.py:218
  459.5 28.7 %fusion.42 = (bf16[8,8,48,256]{3,2,0,1:T(8,128)(2,1)}, f32[8,8,48,256]{3,2,1,0:T(8,128)}) fusion(f32[8,8,48,256]{3,2,1,0:T(8,128)} %fusion.13, bf16[8,2048,256]{2,1,0:T(8,128)(2,1)} %param.30, bf16[8,8,48,2048]{3,1,0,2:T(8,128)(2,1)} %all-gather.19.cloned.1.call-done), kind=kOutput, calls=%fused_computation.57 | convolution fusion | flops 3225944064 | bytes 28835840 | tf_op jit(solution)/shard_map/secd,edf->secf/dot_general | solution.py:224
  500.2 16.9 copy.217
  517.2 180.6 %reduce-scatter.14.cloned.1.call-done = f32[8,8,12,2048]{3,1,0,2:T(8,128)} async-done(((f32[8,8,48,2048]{3,1,0,2:T(8,128)}), f32[8,8,12,2048]{3,1,0,2:T(8,128)}) %reduce-scatter.14.cloned.1.call-update) | async-done | bytes 6291472 | tf_op jit(solution)/shard_map/reduce_scatter | solution.py:229
  710.6 157.8 %all_gather.41 = bf16[2048,64]{0,1:T(8,128)(2,1)S(1)} all-gather(bf16[256,64]{0,1:T(8,128)(2,1)S(1)} %copy-done.62), channel_id=1, replica_groups=mesh['dp'=8,'tp'=4] {'dp'}, dimensions={0}, use_global_device_ids=true | all-gather | bytes 294912 | tf_op jit(solution)/shard_map/all_gather | solution.py:141
  978.4 68.4 %all_to_all.21 = bf16[8,8,12,2048]{3,1,2,0:T(8,128)(2,1)S(1)} all-to-all(bf16[8,8,12,2048]{3,1,2,0:T(8,128)(2,1)S(1)} %copy.221), channel_id=1, replica_groups=mesh['dp'=8,'tp'=4] {'dp'}, dimensions={0} | all-to-all | bytes 6291456 | tf_op jit(solution)/shard_map/all_to_all | solution.py:215
  1049.0 80.3 %all-gather.21.cloned.1.call-done = bf16[8,8,48,2048]{3,1,0,2:T(8,128)(2,1)} async-done(((bf16[8,8,12,2048]{3,1,0,2:T(8,128)(2,1)}), bf16[8,8,48,2048]{3,1,0,2:T(8,128)(2,1)}) %all-gather.21.cloned.1.call-update) | async-done | bytes 12582928 | tf_op jit(solution)/shard_map/all_gather | solution.py:219
  1129.3 17.5 fusion.39
  1162.5 20.0 fusion.2
  1182.5 16.9 copy.224
  1199.5 180.6 %reduce-scatter.16.cloned.1.call-done = f32[8,8,12,2048]{3,1,0,2:T(8,128)} async-done(((f32[8,8,48,2048]{3,1,0,2:T(8,128)}), f32[8,8,12,2048]{3,1,0,2:T(8,128)}) %reduce-scatter.16.cloned.1.call-update) | async-done | bytes 6291472 | tf_op jit(solution)/shard_map/reduce_scatter | solution.py:268
  1392.0 138.1 %all-to-all-done.3 = f32[8,8,12,2048]{3,1,2,0:T(8,128)} async-done(((f32[8,8,12,2048]{3,1,2,0:T(8,128)}), f32[8,8,12,2048]{3,1,2,0:T(8,128)}, u32[]{:S(2)}, u32[]{:S(2)}) %all-to-all-start.3) | async-done | bytes 6291488 | tf_op jit(solution)/shard_map/all_to_all | solution.py:271
  1615.3 40.8 %all-reduce.14.cloned.1.call-done = f32[256,2048]{1,0:T(8,128)} async-done(((f32[256,2048]{1,0:T(8,128)}), f32[256,2048]{1,0:T(8,128)}) %all-reduce.14.cloned.1.call-update) | async-done | bytes 2097168 | tf_op jit(solution)/shard_map/psum | solution.py:286
  1684.3 86.1 %all-reduce.16.cloned.1.call-done = (f32[256,2048]{1,0:T(8,128)}, f32[256,2048]{1,0:T(8,128)}, f32[256,64]{0,1:T(8,128)}) async-done(((f32[256,2048]{1,0:T(8,128)}, f32[256,2048]{1,0:T(8,128)}, f32[256,64]{0,1:T(8,128)}), (f32[256,2048]{1,0:T(8,128)}, f32[256,2048]{1,0:T(8,128)}, f32[256,64]{0,1:T(8,128)})) %all-reduce.16.cloned.1.call-update) | async-done | bytes 4259856 | tf_op jit(solution)/shard_map/psum | solution.py:243
  1787.3 25.0 %fusion.26 = f32[8,2048,256]{2,1,0:T(8,128)} fusion(bf16[8,8,48,256]{3,2,0,1:T(8,128)(2,1)S(1)} %copy-done.33, bf16[8,8,48,2048]{3,1,0,2:T(8,128)(2,1)} %all-gather.19.cloned.1.call-done), kind=kOutput, calls=%fused_computation.46 | convolution fusion | flops 3221225472 | bytes 30932992 | tf_op jit(solution)/shard_map/secd,secf->edf/dot_general | solution.py:256
  1812.3 25.0 %fusion.29 = f32[8,2048,256]{2,1,0:T(8,128)} fusion(bf16[8,8,48,256]{3,2,0,1:T(8,128)(2,1)S(1)} %copy-done.21, bf16[8,8,48,2048]{3,1,0,2:T(8,128)(2,1)} %all-gather.19.cloned.1.call-done), kind=kOutput, calls=%fused_computation.47 | convolution fusion | flops 3221225472 | bytes 30932992 | tf_op jit(solution)/shard_map/secd,secf->edf/dot_general | solution.py:259
  1837.3 37.6 %fusion.32 = f32[8,256,2048]{2,1,0:T(8,128)} fusion(bf16[8,8,48,256]{3,2,0,1:T(8,128)(2,1)S(1)} %copy-done.34, bf16[8,8,48,2048]{3,1,0,2:T(8,128)(2,1)} %all-gather.21.cloned.1.call-done), kind=kOutput, calls=%fused_computation.48 | convolution fusion | flops 3221225472 | bytes 30932992 | tf_op jit(solution)/shard_map/secf,secd->efd/dot_general | solution.py:248
  1876.2 23.3 reduce-scatter.30.cloned.1.call-done
  1905.6 35.4 %all-reduce.4 = (f32[2048]{0:T(1024)S(1)}, f32[2048]{0:T(1024)S(1)}) all-reduce(f32[2048]{0:T(1024)S(1)} %get-tuple-element.16, f32[2048]{0:T(1024)S(1)} %get-tuple-element.14), channel_id=4, replica_groups=mesh['dp'=8,'tp'=4] {'dp'}, use_global_device_ids=true, to_apply=%region_39.40.clone | all-reduce | flops 4096 | bytes 32768
  1946.4 18.8 reduce-scatter.26.cloned.1.call-done
  1965.2 91.0 %reduce-scatter.18.cloned.1.call-done = f32[256,512]{1,0:T(8,128)} async-done(((f32[2048,512]{1,0:T(8,128)}), f32[256,512]{1,0:T(8,128)}) %reduce-scatter.18.cloned.1.call-update) | async-done | bytes 524304 | tf_op jit(solution)/shard_map/reduce_scatter | solution.py:341
  2056.2 92.2 %reduce-scatter.20.cloned.1.call-done = f32[256,512]{1,0:T(8,128)} async-done(((f32[2048,512]{1,0:T(8,128)}), f32[256,512]{1,0:T(8,128)}) %reduce-scatter.20.cloned.1.call-update) | async-done | bytes 524304 | tf_op jit(solution)/shard_map/reduce_scatter | solution.py:342
  2148.3 91.7 %reduce-scatter.22.cloned.1.call-done = f32[256,512]{1,0:T(8,128)} async-done(((f32[2048,512]{1,0:T(8,128)}), f32[256,512]{1,0:T(8,128)}) %reduce-scatter.22.cloned.1.call-update) | async-done | bytes 524304 | tf_op jit(solution)/shard_map/reduce_scatter | solution.py:343
  2240.1 92.7 %reduce-scatter.24.cloned.1.call-done = f32[512,256]{1,0:T(8,128)} async-done(((f32[512,2048]{1,0:T(8,128)}), f32[512,256]{1,0:T(8,128)}) %reduce-scatter.24.cloned.1.call-update) | async-done | bytes 524304 | tf_op jit(solution)/shard_map/reduce_scatter | solution.py:344
  (358 shorter events, 410.8 us)
Async XLA Ops:
  7.2 129.3 %all-gather.13.cloned.1.call-start = ((), (), s32[]{:S(2)}) async-start(), calls=%async_computation.14 | async-start | bytes 2359296 | tf_op jit(solution)/shard_map/all_gather | solution.py:137
  8.0 65.2 %copy-start = (f32[256,2048]{1,0:T(8,128)S(1)}, f32[256,2048]{1,0:T(8,128)}, u32[]{:S(2)}) copy-start(f32[256,2048]{1,0:T(8,128)} %param.16) | copy-start | bytes 6291460
  8.0 132.2 %all-gather.15.cloned.1.call-start = ((), (), s32[]{:S(2)}) async-start(), calls=%async_computation.15 | async-start | bytes 2359296 | tf_op jit(solution)/shard_map/all_gather | solution.py:138
  8.7 158.2 %all-gather.11.cloned.1.call-start = ((), (), s32[]{:S(2)}) async-start(), calls=%async_computation.13 | async-start | bytes 2359296 | tf_op jit(solution)/shard_map/all_gather | solution.py:139
  9.5 204.3 %all-gather.17.cloned.1.call-start = ((), (), s32[]{:S(2)}) async-start(), calls=%async_computation.16 | async-start | bytes 2359296 | tf_op jit(solution)/shard_map/all_gather | solution.py:140
  10.0 257.1 %all-reduce.12.cloned.1.call-start = ((), (), s32[]{:S(2)}) async-start(), calls=%async_computation.17 | async-start | bytes 4194304 | tf_op jit(solution)/shard_map/psum | solution.py:188
  71.3 93.1 %copy-start.35 = (f32[256,64]{1,0:T(8,128)}, f32[256,64]{1,0:T(8,128)S(1)}, u32[]{:S(2)}) copy-start(f32[256,64]{1,0:T(8,128)S(1)} %get-tuple-element.97) | copy-start | bytes 196612
  71.3 93.1 %copy-start.37 = (f32[256,64]{1,0:T(8,128)}, f32[256,64]{1,0:T(8,128)S(1)}, u32[]{:S(2)}) copy-start(f32[256,64]{1,0:T(8,128)S(1)} %get-tuple-element.98) | copy-start | bytes 196612
  74.1 92.9 %copy-start.4 = (bf16[256,2048]{1,0:T(8,128)(2,1)}, bf16[256,2048]{1,0:T(8,128)(2,1)S(1)}, u32[]{:S(2)}) copy-start(bf16[256,2048]{1,0:T(8,128)(2,1)S(1)} %multiply_convert_fusion.1) | copy-start | bytes 3145732
  76.3 75.6 %copy-start.59 = (f32[128,4]{0,1:T(4,128)}, f32[128,4]{0,1:T(4,128)S(1)}, u32[]{:S(2)}) copy-start(f32[128,4]{0,1:T(4,128)S(1)} %reshape.467) | copy-start | bytes 6148
  77.1 80.5 %copy-start.57 = (f32[128,4]{0,1:T(4,128)}, f32[128,4]{0,1:T(4,128)S(1)}, u32[]{:S(2)}) copy-start(f32[128,4]{0,1:T(4,128)S(1)} %reshape.468) | copy-start | bytes 6148
  94.2 175.5 %copy-start.55 = (f32[8,1,256]{2,1,0:T(1,128)}, f32[8,1,256]{2,1,0:T(1,128)S(1)}, u32[]{:S(2)}) copy-start(f32[8,1,256]{2,1,0:T(1,128)S(1)} %convert_element_type.122) | copy-start | bytes 24580
  217.4 226.2 %all-gather.19.cloned.1.call-start = ((), (), s32[]{:S(2)}) async-start(), calls=%async_computation.18 | async-start | bytes 15728640 | tf_op jit(solution)/shard_map/all_gather | solution.py:218
  270.6 598.6 %copy-start.10 = (bf16[256,2048]{1,0:T(8,128)(2,1)}, bf16[256,2048]{1,0:T(8,128)(2,1)S(1)}, u32[]{:S(2)}) copy-start(bf16[256,2048]{1,0:T(8,128)(2,1)S(1)} %multiply_convert_fusion) | copy-start | bytes 3145732
  363.1 334.7 %reduce-scatter.14.cloned.1.call-start = ((), (), s32[]{:S(2)}) async-start(), calls=%async_computation.19 | async-start | bytes 31457280 | tf_op jit(solution)/shard_map/reduce_scatter | solution.py:229
  704.1 165.6 %all-to-all-start.1 = ((f32[8,8,12,2048]{3,1,2,0:T(8,128)}), f32[8,8,12,2048]{3,1,2,0:T(8,128)}, u32[]{:S(2)}, u32[]{:S(2)}) async-start(f32[8,8,12,2048]{3,1,2,0:T(8,128)} %copy.218), calls=%async_computation.2 | async-start | bytes 12582912 | tf_op jit(solution)/shard_map/all_to_all | solution.py:230
  709.7 419.6 %all-gather.21.cloned.1.call-start = ((), (), s32[]{:S(2)}) async-start(), calls=%async_computation.20 | async-start | bytes 15728640 | tf_op jit(solution)/shard_map/all_gather | solution.py:219
  1049.0 331.1 %reduce-scatter.16.cloned.1.call-start = ((), (), s32[]{:S(2)}) async-start(), calls=%async_computation.21 | async-start | bytes 31457280 | tf_op jit(solution)/shard_map/reduce_scatter | solution.py:268
  1386.3 143.8 %all-to-all-start.3 = ((f32[8,8,12,2048]{3,1,2,0:T(8,128)}), f32[8,8,12,2048]{3,1,2,0:T(8,128)}, u32[]{:S(2)}, u32[]{:S(2)}) async-start(f32[8,8,12,2048]{3,1,2,0:T(8,128)} %copy.225), calls=%async_computation.5 | async-start | bytes 12582912 | tf_op jit(solution)/shard_map/all_to_all | solution.py:271
  1391.8 264.3 %all-reduce.14.cloned.1.call-start = ((), (), s32[]{:S(2)}) async-start(), calls=%async_computation.22 | async-start | bytes 4194304 | tf_op jit(solution)/shard_map/psum | solution.py:286
  1392.0 207.0 %copy-start.51 = (f32[256,64]{0,1:T(8,128)}, f32[256,64]{0,1:T(8,128)S(1)}, u32[]{:S(2)}) copy-start(f32[256,64]{0,1:T(8,128)S(1)} %subtract_multiply_fusion) | copy-start | bytes 196612
  1606.5 164.0 %all-reduce.16.cloned.1.call-start = ((), (), s32[]{:S(2)}) async-start(), calls=%async_computation.30 | async-start | bytes 8519680 | tf_op jit(solution)/shard_map/psum | solution.py:243
  1682.6 87.8 %copy-start.11 = (bf16[256,2048]{1,0:T(8,128)(2,1)S(1)}, bf16[256,2048]{1,0:T(8,128)(2,1)}, u32[]{:S(2)}) copy-start(bf16[256,2048]{1,0:T(8,128)(2,1)} %copy-done.10) | copy-start | bytes 3145732
  1682.6 90.1 %copy-start.5 = (bf16[256,2048]{1,0:T(8,128)(2,1)S(1)}, bf16[256,2048]{1,0:T(8,128)(2,1)}, u32[]{:S(2)}) copy-start(bf16[256,2048]{1,0:T(8,128)(2,1)} %copy-done.4) | copy-start | bytes 3145732
  1682.6 90.1 %copy-start.25 = (bf16[256,512]{1,0:T(8,128)(2,1)S(1)}, bf16[256,512]{1,0:T(8,128)(2,1)}, u32[]{:S(2)}) copy-start(bf16[256,512]{1,0:T(8,128)(2,1)} %copy-done.24) | copy-start | bytes 786436
  1682.7 192.2 %reduce-scatter.28.cloned.1.call-start = ((), (), s32[]{:S(2)}) async-start(), calls=%async_computation.28 | async-start | bytes 73728
  1683.5 216.1 %reduce-scatter.30.cloned.1.call-start = ((), (), s32[]{:S(2)}) async-start(), calls=%async_computation.29 | async-start | bytes 73728
  1684.3 280.9 %reduce-scatter.26.cloned.1.call-start = ((), (), s32[]{:S(2)}) async-start(), calls=%async_computation.27 | async-start | bytes 589824 | tf_op jit(solution)/shard_map/reduce_scatter | solution.py:345
  1772.7 283.4 %reduce-scatter.18.cloned.1.call-start = ((), (), s32[]{:S(2)}) async-start(), calls=%async_computation.23 | async-start | bytes 4718592 | tf_op jit(solution)/shard_map/reduce_scatter | solution.py:341
  1775.5 372.8 %reduce-scatter.20.cloned.1.call-start = ((), (), s32[]{:S(2)}) async-start(), calls=%async_computation.24 | async-start | bytes 4718592 | tf_op jit(solution)/shard_map/reduce_scatter | solution.py:342
  1778.3 461.8 %reduce-scatter.22.cloned.1.call-start = ((), (), s32[]{:S(2)}) async-start(), calls=%async_computation.25 | async-start | bytes 4718592 | tf_op jit(solution)/shard_map/reduce_scatter | solution.py:343
  1781.1 551.7 %reduce-scatter.24.cloned.1.call-start = ((), (), s32[]{:S(2)}) async-start(), calls=%async_computation.26 | async-start | bytes 4718592 | tf_op jit(solution)/shard_map/reduce_scatter | solution.py:344
  (72 other events, 791.4 us)
Sparse Core Ops, SparseCore 0:
  10.2 52.0 all-gather.12
  64.4 47.2 all-gather.14
  113.8 48.3 all-gather.10
  164.1 49.5 all-gather.16
  217.5 49.5 all-reduce.11
  363.2 80.3 all-gather.18
  517.3 180.4 reduce-scatter.13
  1049.1 80.1 all-gather.20
  1199.6 180.4 reduce-scatter.15
  1606.6 49.4 all-reduce.13
  1682.8 87.6 all-reduce.15
  1774.0 61.3 reduce-scatter.27
  1839.2 60.2 reduce-scatter.29
  1903.7 61.4 reduce-scatter.25
  1969.2 86.8 reduce-scatter.17
  2060.7 87.6 reduce-scatter.19
  2152.4 87.6 reduce-scatter.21
  2244.5 88.1 reduce-scatter.23
where the time goes:
time: 2350 us; the launch traced here: 2340 us
  waiting for transfers between devices  1280 us (54%)
  blocking collectives  423 us (18%)
  local copies, waits for them, and re-layouts  272 us (12%)
  matrix products  242 us (10%)
  other arithmetic  91.9 us (4%)
    reduce_scatter x1, waiting for transfers between devices, per_device(): lax.psum_scatter(rounded_wide(part_sum), 'tp', scatter_dimension=2, tiled...  181 us
    reduce_scatter x1, waiting for transfers between devices, per_device(): lax.psum_scatter(rounded_wide(grad_input_sum), 'tp', scatter_dimension=2,...  181 us
    all_gather x1, blocking collectives, per_device(): lax.all_gather(router_weight, 'dp', axis=0, tiled=True)  158 us
    all_to_all x1, waiting for transfers between devices, per_device(): lax.all_to_all(grad_quarter, 'dp', split_axis=0, concat_axis=0, tiled=True)  138 us
    reduce_scatter x1, waiting for transfers between devices, per_device(): lax.psum_scatter(grad_output, 'dp', scatter_dimension=1, tiled=True)  92.7 us
    reduce_scatter x1, waiting for transfers between devices, per_device(): lax.psum_scatter(grad_key, 'dp', scatter_dimension=0, tiled=True)  92.2 us
    reduce_scatter x1, waiting for transfers between devices, per_device(): lax.psum_scatter(grad_value, 'dp', scatter_dimension=0, tiled=True)  91.7 us
    reduce_scatter x1, waiting for transfers between devices, per_device(): lax.psum_scatter(grad_query, 'dp', scatter_dimension=0, tiled=True)  91 us
  transfers between devices with their start and end apart: 20, of which 15 were waited for; matrix products, arithmetic and copies ran while one was open for 9% of the time, Pallas kernels for 0%

commit v1 on v0

v1 whole, which is shorter than its diff:
```python
import math

import jax
import jax.numpy as jnp
from jax import lax
from jax.experimental import pallas as pl
from jax.experimental.pallas import tpu as pltpu
from jax.sharding import PartitionSpec as P

D = 2048
HD = 128
E = 64
TOPK = 8
CAP = 48
EXTRA = 2 * E

bf16 = jnp.bfloat16
f32 = jnp.float32

epsilon = 1e-05


def hop(values, move):
    dp, tp = lax.axis_size("dp"), lax.axis_size("tp")
    pairs = []
    for a in range(dp):
        for b in range(tp):
            c, e = move(a, b)
            pairs.append((a * tp + b, c * tp + e))
    return lax.ppermute(values, ("dp", "tp"), pairs)


def over_z(values, steps=1):
    half = lax.axis_size("dp") // 2
    return hop(values, lambda a, b: ((a // 2 + steps) % half * 2 + a % 2, b))


def over_y(values):
    return hop(values, lambda a, b: (a ^ 1, b))


def over_x(values):
    return hop(values, lambda a, b: (a, b ^ 2))


def over_core(values):
    return hop(values, lambda a, b: (a, b ^ 1))


def gather_dp(values):
    half = lax.axis_size("dp") // 2
    line = [values]
    for _ in range(half - 1):
        line.append(over_z(line[-1]))
    return line + [over_y(v) for v in line]


def gather_all(values):
    line = gather_dp(values)
    both = [(v, over_x(v)) for v in line]
    return [(a, over_core(a), b, over_core(b)) for a, b in both]


def absolute_dp(pieces):
    dp = lax.axis_size("dp")
    half = dp // 2
    me = lax.axis_index("dp")
    stack = jnp.stack(pieces).reshape((2, half) + pieces[0].shape)
    stack = jnp.where(me % 2 == 1, stack[::-1], stack)[:, ::-1]
    twice = jnp.concatenate([stack, stack], axis=1)
    turned = lax.dynamic_slice_in_dim(twice, half - 1 - me // 2, half, 1)
    return jnp.swapaxes(turned, 0, 1).reshape((dp,) + pieces[0].shape)


def absolute_tp(pieces, axis=0):
    me = lax.axis_index("tp")
    first = [jnp.where(me % 2 == 1, pieces[i ^ 1], pieces[i]) for i in range(4)]
    second = [jnp.where(me // 2 == 1, first[i ^ 2], first[i]) for i in range(4)]
    return jnp.concatenate(second, axis=axis)


def gather_tp(values):
    other = over_x(values)
    return [values, over_core(values), other, over_core(other)]


def added(*terms):
    total = terms[0].astype(f32)
    for term in terms[1:]:
        total = total + term.astype(f32)
    return total


def scatter_tp(values):
    tp = lax.axis_size("tp")
    me = lax.axis_index("tp")
    share = values.shape[0] // tp
    values = values.astype(bf16)
    part = [lax.dynamic_slice_in_dim(values, (me ^ q) * share, share, 0) for q in range(4)]
    mine = over_core(part[1])
    far = over_core(part[3])
    return added(part[0], mine, over_x(added(part[2], far).astype(bf16)))


def scatter_all(parts):
    half = lax.axis_size("dp") // 2
    share = parts[0].shape[0] // (2 * half)
    mine, far = over_core(parts[1]), over_core(parts[3])
    from_x = over_x(added(parts[2], far).astype(bf16))
    total = added(parts[0], mine, from_x)
    near = total[: half * share]
    from_y = over_y(total[half * share :].astype(bf16))
    line = near + from_y.astype(f32)
    moving = line[(half - 1) * share :]
    for dz in reversed(range(half - 1)):
        moving = line[dz * share : (dz + 1) * share] + over_z(moving.astype(bf16), -1).astype(f32)
    return moving


def chosen_slots(table):
    experts, tokens = table.shape
    place = lax.broadcasted_iota(jnp.int32, (experts, CAP, tokens), 1)
    hit = place == table[:, None, :]
    return jnp.where(hit, 1.0, 0.0).astype(bf16).reshape(experts * CAP, tokens)


def rows_of_slots(pieces, table):
    sequences, experts, tokens = table.shape
    flat = [piece for group in pieces for piece in group]
    share, width = flat[0].shape
    groups = len(flat) // sequences

    def kernel(table_ref, *refs):
        sources, (out_ref, buffer, arrived) = refs[: len(flat)], refs[len(flat) :]
        step = pl.program_id(0)

        @pl.when(step == 0)
        def _():
            for i, source in enumerate(sources):
                pltpu.make_async_copy(
                    source, buffer.at[i // groups, pl.ds(i % groups * share, share)], arrived.at[i]
                ).start()

        for i in range(groups):
            pltpu.make_async_copy(
                sources[i], buffer.at[step, pl.ds(i * share, share)], arrived.at[step * groups + i]
            ).wait()
        picked = jnp.dot(chosen_slots(table_ref[0]), buffer[step], preferred_element_type=f32)
        out_ref[...] = picked.astype(bf16).reshape(experts, CAP, width)

    return pl.pallas_call(
        kernel,
        grid=(sequences,),
        in_specs=[pl.BlockSpec((1, experts, tokens), lambda s: (s, 0, 0))]
        + [pl.BlockSpec(memory_space=pl.ANY)] * len(flat),
        out_specs=pl.BlockSpec((experts, CAP, width), lambda s: (0, s, 0)),
        out_shape=jax.ShapeDtypeStruct((experts, sequences * CAP, width), bf16),
        scratch_shapes=[
            pltpu.VMEM((sequences, tokens, width), bf16),
            pltpu.SemaphoreType.DMA((len(flat),)),
        ],
        compiler_params=pltpu.CompilerParams(vmem_limit_bytes=48 << 20),
        cost_estimate=pl.CostEstimate(
            flops=2 * experts * CAP * sequences * tokens * width,
            bytes_accessed=2 * sequences * (tokens + experts * CAP) * width,
            transcendentals=0,
        ),
        name="rows_of_slots",
    )(table, *flat)


def tokens_of_slots(rows, table):
    sequences, experts, tokens = table.shape
    width = rows.shape[-1]
    share = tokens // 4

    def kernel(table_ref, rows_ref, *outs):
        picked = chosen_slots(table_ref[0])
        total = lax.dot_general(
            picked,
            rows_ref[...].reshape(experts * CAP, width),
            (((0,), (0,)), ((), ())),
            preferred_element_type=f32,
        ).astype(bf16)
        for q, out in enumerate(outs):
            out[...] = total[q * share : (q + 1) * share]

    return pl.pallas_call(
        kernel,
        grid=(sequences,),
        in_specs=[
            pl.BlockSpec((1, experts, tokens), lambda s: (s, 0, 0)),
            pl.BlockSpec((experts, CAP, width), lambda s: (0, s, 0)),
        ],
        out_specs=[pl.BlockSpec((share, width), lambda s: (s, 0))] * 4,
        out_shape=[jax.ShapeDtypeStruct((sequences * share, width), bf16)] * 4,
        compiler_params=pltpu.CompilerParams(vmem_limit_bytes=48 << 20),
        cost_estimate=pl.CostEstimate(
            flops=2 * experts * CAP * sequences * tokens * width,
            bytes_accessed=2 * sequences * (tokens + experts * CAP) * width,
            transcendentals=0,
        ),
        name="tokens_of_slots",
    )(table, rows)


def dot_last(a, b):
    return lax.dot_general(a, b, (((1,), (1,)), ((), ())), preferred_element_type=f32)


def dot_first(a, b):
    return lax.dot_general(a, b, (((0,), (0,)), ((), ())), preferred_element_type=f32)


def per_expert(kernel, experts, ins, outs, flops, name, scalars=()):
    whole = lambda shape: pl.BlockSpec((1,) + tuple(shape[1:]), lambda e: (e, 0, 0))
    in_specs = [pl.BlockSpec(memory_space=pltpu.SMEM)] * len(scalars)
    moved = 0
    for array, block in ins:
        in_specs.append(pl.BlockSpec((1,) + block, lambda e: (e, 0, 0)))
        moved += experts * math.prod(block) * array.dtype.itemsize
    moved += sum(math.prod(o.shape) * o.dtype.itemsize for o in outs)
    return pl.pallas_call(
        kernel,
        grid=(experts,),
        in_specs=in_specs,
        out_specs=[whole(o.shape) for o in outs],
        out_shape=list(outs),
        compiler_params=pltpu.CompilerParams(vmem_limit_bytes=48 << 20),
        cost_estimate=pl.CostEstimate(flops=flops, bytes_accessed=moved, transcendentals=0),
        name=name,
    )(*scalars, *[array for array, _ in ins])


def grad_of_hidden(cot_rows, down_weight):
    experts, rows, width = cot_rows.shape
    hidden = down_weight.shape[1]

    def kernel(cot_ref, down_ref, out_ref):
        out_ref[0] = dot_last(cot_ref[0], down_ref[0])

    return per_expert(
        kernel,
        experts,
        [(cot_rows, (rows, width)), (down_weight, (hidden, width))],
        [jax.ShapeDtypeStruct((experts, rows, hidden), f32)],
        2 * experts * rows * width * hidden,
        "grad_of_hidden",
    )[0]


def expert_step(x_rows, gate_weight, up_weight, hidden_grad, first_expert):
    experts, rows, wide = x_rows.shape
    width, hidden = gate_weight.shape[1:]

    def kernel(base_ref, x_ref, gate_ref, up_ref, grad_ref, back_ref, act_ref, gate_grad_ref, up_grad_ref):
        mine = base_ref[0] + pl.program_id(0)
        x = x_ref[0, :, :width]
        lane = lax.broadcasted_iota(jnp.int32, (rows, EXTRA), 1)
        probs = x_ref[0, :, width:].astype(f32)
        mix = jnp.sum(
            jnp.where((lane == mine) | (lane == mine + E), probs, 0.0), axis=1, keepdims=True
        )
        gate_act = jnp.dot(x, gate_ref[0], preferred_element_type=f32)
        up_act = jnp.dot(x, up_ref[0], preferred_element_type=f32)
        raw = grad_ref[0]
        sig = jax.nn.sigmoid(gate_act)
        silu = gate_act * sig
        act = silu * up_act
        grad_mix = jnp.sum(act * raw, axis=1, keepdims=True)
        act_ref[0] = (mix * act).astype(bf16)
        weighted = mix * raw
        gate_grad = (weighted * up_act * sig * (1.0 + gate_act * (1.0 - sig))).astype(bf16)
        up_grad = (weighted * silu).astype(bf16)
        gate_grad_ref[0] = gate_grad
        up_grad_ref[0] = up_grad
        back_ref[0, :, :width] = (
            dot_last(gate_grad, gate_ref[0]) + dot_last(up_grad, up_ref[0])
        ).astype(bf16)
        coarse = grad_mix.astype(bf16).astype(f32)
        fine = grad_mix - coarse
        back_ref[0, :, width:] = jnp.where(
            lane == mine, coarse, jnp.where(lane == mine + E, fine, 0.0)
        ).astype(bf16)

    small = jax.ShapeDtypeStruct((experts, rows, hidden), bf16)
    return per_expert(
        kernel,
        experts,
        [
            (x_rows, (rows, wide)),
            (gate_weight, (width, hidden)),
            (up_weight, (width, hidden)),
            (hidden_grad, (rows, hidden)),
        ],
        [jax.ShapeDtypeStruct((experts, rows, wide), bf16), small, small, small],
        8 * experts * rows * width * hidden,
        "expert_step",
        (first_expert,),
    )


def expert_out(act, down_weight):
    experts, rows, hidden = act.shape
    width = down_weight.shape[2]

    def kernel(act_ref, down_ref, out_ref):
        out_ref[0] = jnp.dot(act_ref[0], down_ref[0], preferred_element_type=f32).astype(bf16)

    return per_expert(
        kernel,
        experts,
        [(act, (rows, hidden)), (down_weight, (hidden, width))],
        [jax.ShapeDtypeStruct((experts, rows, width), bf16)],
        2 * experts * rows * width * hidden,
        "expert_out",
    )[0]


def expert_weight_grads(x_rows, cot_rows, act, gate_grad, up_grad, width):
    experts, rows, hidden = act.shape

    def kernel(x_ref, cot_ref, act_ref, gate_ref, up_ref, gate_out, up_out, down_out):
        gate_out[0] = dot_first(x_ref[0], gate_ref[0])
        up_out[0] = dot_first(x_ref[0], up_ref[0])
        down_out[0] = dot_first(act_ref[0], cot_ref[0])

    return per_expert(
        kernel,
        experts,
        [
            (x_rows, (rows, width)),
            (cot_rows, (rows, width)),
            (act, (rows, hidden)),
            (gate_grad, (rows, hidden)),
            (up_grad, (rows, hidden)),
        ],
        [
            jax.ShapeDtypeStruct((experts, width, hidden), f32),
            jax.ShapeDtypeStruct((experts, width, hidden), f32),
            jax.ShapeDtypeStruct((experts, hidden, width), f32),
        ],
        6 * experts * rows * width * hidden,
        "expert_weight_grads",
    )


def rms_scale(values):
    return lax.rsqrt(jnp.mean(values * values, axis=-1, keepdims=True) + epsilon)


def rms_back(values, scale, scaled_grad):
    return scale * scaled_grad - values * scale**3 * jnp.mean(
        scaled_grad * values, axis=-1, keepdims=True
    )


def rope_tables(length, head_size):
    half_size = head_size // 2
    inverse = 10000.0 ** (-2.0 * jnp.arange(half_size, dtype=jnp.float32) / head_size)
    angles = jnp.arange(length, dtype=jnp.float32)[:, None] * inverse[None, :]
    return (jnp.cos(angles)[:, None, :], jnp.sin(angles)[:, None, :])


def rotate(values, cosine, sine_table):
    half_size = values.shape[-1] // 2
    leading, second = (values[..., :half_size], values[..., half_size:])
    return jnp.concatenate(
        [leading * cosine - second * sine_table, second * cosine + leading * sine_table], axis=-1
    )


def unrotate(values, cosine, sine_table):
    half_size = values.shape[-1] // 2
    leading, second = (values[..., :half_size], values[..., half_size:])
    return jnp.concatenate(
        [leading * cosine + second * sine_table, second * cosine - leading * sine_table], axis=-1
    )


def allowed_mask(segments):
    position = jnp.arange(segments.shape[0], dtype=jnp.int32)
    return (position[None, :] <= position[:, None]) & (segments[:, None] == segments[None, :])


def score_table(queries, key_rows, segments):
    score_scale = 1.0 / math.sqrt(queries.shape[-1])
    scores = (
        jnp.einsum("qhd,khd->hqk", queries, key_rows, preferred_element_type=jnp.float32)
        * score_scale
    )
    allowed = allowed_mask(segments)[None]
    return (jnp.where(allowed, scores, -1e30), allowed, score_scale)


def attend_local(queries, key_rows, value_rows, segments):
    scores, allowed, score_scale = score_table(queries, key_rows, segments)
    largest = jnp.max(scores, axis=-1, keepdims=True)
    denominator = jnp.sum(
        jnp.where(allowed, jnp.exp(scores - largest), 0.0), axis=-1, keepdims=True
    )
    log_total = largest + jnp.log(denominator)
    weights = jnp.where(allowed, jnp.exp(scores - log_total), 0.0).astype(jnp.bfloat16)
    mixture = jnp.einsum("hqk,khd->qhd", weights, value_rows, preferred_element_type=jnp.float32)
    return (mixture.astype(jnp.bfloat16), log_total)


def attend_local_back(queries, key_rows, value_rows, segments, log_total, grad_mixture):
    scores, allowed, score_scale = score_table(queries, key_rows, segments)
    full_probs = jnp.where(allowed, jnp.exp(scores - log_total), 0.0)
    low_probs = full_probs.astype(jnp.bfloat16)
    grad_values = jnp.einsum(
        "hqk,qhd->khd", low_probs, grad_mixture, preferred_element_type=jnp.float32
    )
    grad_attn = jnp.einsum(
        "qhd,khd->hqk", grad_mixture, value_rows, preferred_element_type=jnp.float32
    )
    row_dot = jnp.sum(full_probs * grad_attn, axis=-1, keepdims=True)
    grad_scores = (full_probs * (grad_attn - row_dot) * score_scale).astype(jnp.bfloat16)
    grad_queries = jnp.einsum(
        "hqk,khd->qhd", grad_scores, key_rows, preferred_element_type=jnp.float32
    )
    grad_keys = jnp.einsum("hqk,qhd->khd", grad_scores, queries, preferred_element_type=jnp.float32)
    return (grad_queries, grad_keys, grad_values)


def coarse_and_fine(values):
    coarse = lax.reduce_precision(values, 8, 7)
    return jnp.concatenate([coarse, values - coarse], axis=-1).astype(bf16)


def slot_tables(expert_ids, local_experts):
    data_size, tensor_size = lax.axis_size("dp"), lax.axis_size("tp")
    ids = jnp.stack(gather_dp(expert_ids.T))
    sequences, top, tokens = ids.shape
    share = tokens // tensor_size
    ids = absolute_tp([ids[:, :, q * share : (q + 1) * share] for q in range(4)], axis=2)
    mine = lax.axis_index("dp") * local_experts + jnp.arange(local_experts, dtype=jnp.int32)
    named = jnp.any(ids[:, None] == mine[None, :, None, None], axis=2)
    position = jnp.arange(tokens, dtype=jnp.int32)
    before = (position[:, None] < position[None, :]).astype(bf16)
    slot = jnp.einsum("set,tu->seu", named.astype(bf16), before, preferred_element_type=f32)
    return jnp.where(named, slot.astype(jnp.int32), -1)


def slabs_of(values):
    dp = lax.axis_size("dp")
    half = dp // 2
    me = lax.axis_index("dp")
    slab = values.shape[1] // dp
    got = []
    for dy in range(2):
        for dz in range(half):
            target = (me // 2 + dz) % half * 2 + (me % 2 ^ dy)
            part = lax.dynamic_slice_in_dim(values, target * slab, slab, 1)
            if dy or dz:
                part = hop(
                    part,
                    lambda a, b, dy=dy, dz=dz: ((a // 2 + dz) % half * 2 + (a % 2 ^ dy), b),
                )
            got.append(part)
    return absolute_tp(gather_tp(jnp.stack(got)), axis=1)


def per_device(
    hidden_in,
    cotangent,
    segment_ids,
    expert_ids,
    first_gain,
    query_weight,
    key_weight,
    value_weight,
    output_weight,
    query_gain,
    key_gain,
    second_gain,
    router_weight,
    gate_weight,
    up_weight,
    down_weight,
):
    data_size = lax.axis_size("dp")
    tensor_size = lax.axis_size("tp")
    seq_len, width = hidden_in.shape
    share = seq_len // tensor_size
    me_dp, me_tp = lax.axis_index("dp"), lax.axis_index("tp")
    own = lambda values: lax.dynamic_slice_in_dim(values, me_tp * share, share, 0)
    local_experts = E // data_size

    table = slot_tables(expert_ids, local_experts)

    rows_full = lambda pieces: absolute_dp(pieces).reshape(width, -1)
    query_full = rows_full(gather_dp(query_weight))
    key_full = rows_full(gather_dp(key_weight))
    value_full = rows_full(gather_dp(value_weight))
    output_full = jnp.swapaxes(absolute_dp(gather_dp(output_weight)), 0, 1).reshape(
        output_weight.shape[0], width
    )
    small = jnp.concatenate(
        [
            router_weight.reshape(-1),
            first_gain,
            second_gain,
            query_gain.reshape(-1),
            key_gain.reshape(-1),
        ]
    )
    small = absolute_dp(gather_dp(small))
    slab = width // data_size
    cut = slab * E
    router_full = small[:, :cut].reshape(width, E)
    gain_one = small[:, cut : cut + slab].reshape(-1).astype(f32)
    gain_two = small[:, cut + slab : cut + 2 * slab].reshape(-1).astype(f32)
    heads_local = query_gain.shape[0]
    piece = heads_local * query_gain.shape[1]
    cut = cut + 2 * slab
    spread = lambda v: jnp.swapaxes(v.reshape(data_size, heads_local, -1), 0, 1).reshape(-1).astype(f32)
    query_gains = spread(small[:, cut : cut + piece])
    key_gains = spread(small[:, cut + piece : cut + 2 * piece])

    cot_own = own(cotangent)
    cot_rows = rows_of_slots(gather_all(cot_own.astype(bf16)), table)
    hidden_grad = grad_of_hidden(cot_rows, down_weight)

    segments = segment_ids[0]
    first_scale = rms_scale(hidden_in)
    normed_one = (hidden_in * first_scale * gain_one).astype(jnp.bfloat16)
    queries = jnp.dot(normed_one, query_full, preferred_element_type=jnp.float32)
    key_proj = jnp.dot(normed_one, key_full, preferred_element_type=jnp.float32)
    value_proj = jnp.dot(normed_one, value_full, preferred_element_type=jnp.float32).astype(
        jnp.bfloat16
    )
    query_squares, key_squares = lax.psum(
        (jnp.sum(queries * queries, axis=-1), jnp.sum(key_proj * key_proj, axis=-1)), "tp"
    )
    query_scale = lax.rsqrt(query_squares[:, None] / D + epsilon)
    key_scale = lax.rsqrt(key_squares[:, None] / D + epsilon)
    query_normed = queries * query_scale * query_gains
    key_normed = key_proj * key_scale * key_gains
    cosine, sine_table = rope_tables(seq_len, HD)
    query_rot = rotate(query_normed.reshape(seq_len, heads_local, HD), cosine, sine_table).astype(
        jnp.bfloat16
    )
    key_rot = rotate(key_normed.reshape(seq_len, heads_local, HD), cosine, sine_table).astype(
        jnp.bfloat16
    )
    value_heads = value_proj.reshape(seq_len, heads_local, HD)
    attended_heads, log_total = attend_local(query_rot, key_rot, value_heads, segments)
    attended = attended_heads.reshape(seq_len, heads_local * HD)
    middle = own(hidden_in) + scatter_tp(
        jnp.dot(attended, output_full, preferred_element_type=jnp.float32)
    )
    second_scale = rms_scale(middle)
    normed_two = (middle * second_scale * gain_two).astype(jnp.bfloat16)
    logits = jnp.dot(normed_two, router_full, preferred_element_type=jnp.float32)
    router_probs = jax.nn.softmax(logits, axis=-1)

    x_pieces = gather_all(jnp.concatenate([normed_two, coarse_and_fine(router_probs)], axis=1))
    x_rows = rows_of_slots(x_pieces, table)
    first_expert = (me_dp * local_experts).astype(jnp.int32).reshape(1)
    back_rows, act, gate_grad, up_grad = expert_step(
        x_rows, gate_weight, up_weight, hidden_grad, first_expert
    )
    back = scatter_all(tokens_of_slots(back_rows, table))
    moe = scatter_all(tokens_of_slots(expert_out(act, down_weight), table))
    grad_gate, grad_up, grad_down = expert_weight_grads(
        x_rows, cot_rows, act, gate_grad, up_grad, width
    )
    hidden_out = absolute_tp(gather_tp(middle + moe))

    grad_probs = back[:, width : width + E] + back[:, width + E :]
    grad_logits = router_probs * (
        grad_probs - jnp.sum(router_probs * grad_probs, axis=-1, keepdims=True)
    )
    grad_normed_two = back[:, :width] + jnp.dot(
        grad_logits, router_full.astype(jnp.float32).T, precision=lax.Precision.HIGHEST
    )
    grad_router = jnp.dot(
        normed_two.astype(jnp.float32).T, grad_logits, precision=lax.Precision.HIGHEST
    )
    grad_second_gain = jnp.sum(grad_normed_two * middle * second_scale, axis=0)
    grad_middle = cot_own + rms_back(middle, second_scale, grad_normed_two * gain_two)
    grad_middle_low = grad_middle.astype(jnp.bfloat16)
    grad_middle_all = absolute_tp(gather_tp(grad_middle_low))
    grad_attended = jnp.dot(
        grad_middle_all, output_full.T, preferred_element_type=jnp.float32
    ).astype(jnp.bfloat16)
    grad_query_rot, grad_key_rot, grad_values = attend_local_back(
        query_rot,
        key_rot,
        value_heads,
        segments,
        log_total,
        grad_attended.reshape(seq_len, heads_local, HD),
    )
    grad_query_normed = unrotate(grad_query_rot, cosine, sine_table).reshape(seq_len, -1)
    grad_key_normed = unrotate(grad_key_rot, cosine, sine_table).reshape(seq_len, -1)
    grad_query_gain = jnp.sum(grad_query_normed * queries * query_scale, axis=0).reshape(
        heads_local, HD
    )
    grad_key_gain = jnp.sum(grad_key_normed * key_proj * key_scale, axis=0).reshape(heads_local, HD)
    query_scaled_grad = grad_query_normed * query_gains
    key_scaled_grad = grad_key_normed * key_gains
    query_inner, key_inner = lax.psum(
        (
            jnp.sum(query_scaled_grad * queries, axis=-1),
            jnp.sum(key_scaled_grad * key_proj, axis=-1),
        ),
        "tp",
    )
    grad_queries = (
        query_scale * query_scaled_grad - queries * query_scale**3 * (query_inner[:, None] / D)
    ).astype(jnp.bfloat16)
    grad_keys = (
        key_scale * key_scaled_grad - key_proj * key_scale**3 * (key_inner[:, None] / D)
    ).astype(jnp.bfloat16)
    grad_values_low = grad_values.reshape(seq_len, -1).astype(jnp.bfloat16)

    stacked = lambda v: jnp.stack(gather_dp(v)).reshape(-1, v.shape[1])
    flat = lambda v: v.reshape(-1, v.shape[2])
    one_slab = flat(slabs_of(own(normed_one)))
    middle_slab = flat(slabs_of(grad_middle_low))
    grad_output = dot_first(stacked(attended), middle_slab)
    grad_query = dot_first(one_slab, stacked(grad_queries))
    grad_key = dot_first(one_slab, stacked(grad_keys))
    grad_value = dot_first(one_slab, stacked(grad_values_low))

    grad_normed_local = dot_last(grad_queries, query_full)
    grad_normed_local = grad_normed_local + dot_last(grad_keys, key_full)
    grad_normed_local = grad_normed_local + dot_last(grad_values_low, value_full)
    grad_normed_one = scatter_tp(grad_normed_local)
    hidden_own = own(hidden_in)
    scale_own = own(first_scale)
    grad_first_gain = jnp.sum(grad_normed_one * hidden_own * scale_own, axis=0)
    grad_hidden = absolute_tp(
        gather_tp(grad_middle + rms_back(hidden_own, scale_own, grad_normed_one * gain_one))
    )

    tokenwise = lax.psum_scatter(
        jnp.concatenate([grad_router.T, grad_first_gain[None], grad_second_gain[None]]),
        "dp",
        scatter_dimension=1,
        tiled=True,
    )
    tokenwise = lax.psum(tokenwise, "tp")
    grad_router = tokenwise[:E].T
    grad_first_gain = tokenwise[E]
    grad_second_gain = tokenwise[E + 1]
    headwise = lax.psum_scatter(
        jnp.concatenate([grad_query_gain, grad_key_gain]), "dp", scatter_dimension=1, tiled=True
    )
    return (
        hidden_out,
        grad_hidden,
        grad_first_gain,
        grad_query,
        grad_key,
        grad_value,
        grad_output,
        headwise[:heads_local],
        headwise[heads_local:],
        grad_second_gain,
        grad_router,
        grad_gate,
        grad_up,
        grad_down,
    )


def solution(mesh):
    return jax.shard_map(
        per_device,
        mesh=mesh,
        in_specs=(
            P("dp", None),
            P("dp", None),
            P("dp", None),
            P("dp", None),
            P("dp"),
            P("dp", "tp"),
            P("dp", "tp"),
            P("dp", "tp"),
            P("tp", "dp"),
            P("tp", "dp"),
            P("tp", "dp"),
            P("dp"),
            P("dp", None),
            P("dp", None, "tp"),
            P("dp", None, "tp"),
            P("dp", "tp", None),
        ),
        out_specs=(
            P("dp", None),
            P("dp", None),
            P("dp"),
            P("dp", "tp"),
            P("dp", "tp"),
            P("dp", "tp"),
            P("tp", "dp"),
            P("tp", "dp"),
            P("tp", "dp"),
            P("dp"),
            P("dp", None),
            P("dp", None, "tp"),
            P("dp", None, "tp"),
            P("dp", "tp", None),
        ),
        check_vma=False,
    )
```

time: 2350 us -> 904 us (0.38)
  waiting for transfers between devices: 1280 us -> 413 us
  blocking collectives: 423 us -> 12.8 us
  matrix products: 242 us -> 24.2 us
  local copies, waits for them, and re-layouts: 272 us -> 117 us
  starting transfers between devices: 11.9 us -> 147 us
  Pallas kernels: 0 us -> 112 us
  other arithmetic: 91.9 us -> 50 us
    reduce_scatter x7 -> x1, waiting for transfers between devices: 748 us -> 0.02 us  [per_device(): lax.psum_scatter(jnp.concatenate([grad_router.T, grad_first_gain[None], g...]
    ppermute x0 -> x181, waiting for transfers between devices: none -> 339 us  [hop(): return lax.ppermute(values, ('dp', 'tp'), pairs)]
    all_gather x5 -> x0, blocking collectives: 231 us -> none  [the longest x1 158 us: per_device(): lax.all_gather(router_weight, 'dp', axis=0, tiled=True)]
    dot_general x18 -> x10, matrix products: 220 us -> 12.8 us  [the longest x4 6.11 us: dot_first(): lax.dot_general(a, b, (((0,), (0,)), ((), ())), preferred_element_type=f32)]
    all_gather x6 -> x0, waiting for transfers between devices: 204 us -> none  [the longest x1 80.5 us: per_device(): lax.all_gather(arrived_rows, 'tp', axis=2, tiled=True)]
    ppermute x0 -> x181, starting transfers between devices: none -> 147 us  [hop(): return lax.ppermute(values, ('dp', 'tp'), pairs)]
    all_to_all x2 -> x0, blocking collectives: 144 us -> none  [the longest x1 76 us: per_device(): lax.all_to_all(own_rows, 'dp', split_axis=0, concat_axis=0, tiled=True)]
    psum x3 -> x1, waiting for transfers between devices: 166 us -> 25.8 us  [per_device(): tokenwise = lax.psum(tokenwise, 'tp')]
  transfers between devices with their start and end apart: 20 -> 184, of which waited for: 15 -> 81; matrix products, arithmetic and copies ran while one was open for 9% -> 19% of each run, Pallas kernels for 0% -> 13%
where the time goes in v1:
time: 904 us; the launch traced here: 893 us
  waiting for transfers between devices  413 us (46%)
  starting transfers between devices  147 us (16%)
  local copies, waits for them, and re-layouts  117 us (13%)
  Pallas kernels  112 us (12%)
  other arithmetic  50 us (6%)
  matrix products  24.2 us (3%)
  between operations  16.5 us (2%)
  blocking collectives  12.8 us (1%)
    ppermute x181, waiting for transfers between devices, hop(): return lax.ppermute(values, ('dp', 'tp'), pairs)  339 us
    ppermute x181, starting transfers between devices, hop(): return lax.ppermute(values, ('dp', 'tp'), pairs)  147 us
    pallas_call x4, Pallas kernels, per_expert(): pl.pallas_call(kernel, grid=(experts,), in_specs=in_specs, out_specs=[who...  72.1 us
    unnamed x363, local copies, waits for them, and re-layouts  69.1 us
    unnamed x4, waiting for transfers between devices  48.3 us
    psum x1, waiting for transfers between devices, per_device(): tokenwise = lax.psum(tokenwise, 'tp')  25.8 us
    pallas_call x2, Pallas kernels, tokens_of_slots(): pl.pallas_call(kernel, grid=(sequences,), in_specs=[pl.BlockSpec((1, expe...  22.8 us
  transfers between devices with their start and end apart: 184, of which 81 were waited for; matrix products, arithmetic and copies ran while one was open for 19% of the time, Pallas kernels for 13%

profile of v1, /device:TPU:0, one launch (start us, length us, event | category | flops | bytes accessed | tf_op | source)
XLA Modules:
  0.0 892.8 jit_solution(9090824561309182279)
XLA Ops:
  95.9 4.9 collective-permute-done.18
  118.5 4.9 collective-permute-done.26
  130.5 7.8 collective-permute-done.11
  183.2 5.8 all-reduce.1
  226.4 5.0 collective-permute-done.79.refs_4_
  332.2 8.2 rows_of_slots.3.cot_ref
  342.0 10.7 %grad_of_hidden.1.grad_ref = f32[8,384,256]{2,1,0:T(8,128)S(1)} custom-call(bf16[8,384,2048]{2,1,0:T(8,128)(2,1)} %rows_of_slots.3.cot_ref, bf16[8,256,2048]{2,1,0:T(8,128)(2,1)} %down_ref.3), custom_call_target="tpu_custom_call" | custom-call | flops 3221225472 | bytes 24117248 | tf_op jit(solution)/shard_map/grad_of_hidden/pallas_call | solution.py:223
  362.3 9.3 %rows_of_slots.2.x_ref = bf16[8,384,2176]{2,1,0:T(8,128)(2,1)} custom-call(s32[8,8,256]{2,1,0:T(8,128)S(1)} %fusion.16.table_ref, bf16[64,2176]{1,0:T(8,128)(2,1)S(1)} %concatenate.71.refs_0_, bf16[64,2176]{1,0:T(8,128)(2,1)S(1)} %collective-permute-done.45.refs_1_, bf16[64,2176]{1,0:T(8,128)(2,1)S(1)} %collective-permute-done.46.refs_2_, ...), custom_call_target="tpu_custom_call" | custom-call | flops 3422552064 | bytes 22282240 | tf_op jit(solution)/shard_map/rows_of_slots/pallas_call | solution.py:151
  371.5 21.9 %expert_step.1 = (bf16[8,384,2176]{2,1,0:T(8,128)(2,1)}, bf16[8,384,256]{2,1,0:T(8,128)(2,1)S(1)}, bf16[8,384,256]{2,1,0:T(8,128)(2,1)S(1)}, bf16[8,384,256]{2,1,0:T(8,128)(2,1)S(1)}) custom-call(s32[1]{0:T(128)} %bitcast.62.base_ref, bf16[8,384,2176]{2,1,0:T(8,128)(2,1)} %rows_of_slots.2.x_ref, bf16[8,2048,256]{2,1,0:T(8,128)(2,1)} %gate_ref.1, ...), custom_call_target="tpu_custom_call" | custom-call | flops 12884901888 | bytes 51380224 | tf_op jit(solution)/shard_map/expert_step/pallas_call | solution.py:223
  393.5 11.6 %tokens_of_slots.3 = (bf16[512,2176]{1,0:T(8,128)(2,1)S(1)}, bf16[512,2176]{1,0:T(8,128)(2,1)S(1)}, bf16[512,2176]{1,0:T(8,128)(2,1)}, bf16[512,2176]{1,0:T(8,128)(2,1)}) custom-call(s32[8,8,256]{2,1,0:T(8,128)S(1)} %fusion.16.table_ref, bf16[8,384,2176]{2,1,0:T(8,128)(2,1)} %get-tuple-element.34.rows_ref), custom_call_target="tpu_custom_call" | custom-call | flops 3422552064 | bytes 22282240 | tf_op jit(solution)/shard_map/tokens_of_slots/pallas_call | solution.py:188
  414.7 11.5 %expert_out.1.rows_ref = bf16[8,384,2048]{2,1,0:T(8,128)(2,1)} custom-call(bf16[8,384,256]{2,1,0:T(8,128)(2,1)S(1)} %get-tuple-element.29.act_ref, bf16[8,256,2048]{2,1,0:T(8,128)(2,1)} %down_ref.3), custom_call_target="tpu_custom_call" | custom-call | flops 3221225472 | bytes 22544384 | tf_op jit(solution)/shard_map/expert_out/pallas_call | solution.py:223
  426.2 11.2 %tokens_of_slots.2 = (bf16[512,2048]{1,0:T(8,128)(2,1)S(1)}, bf16[512,2048]{1,0:T(8,128)(2,1)S(1)}, bf16[512,2048]{1,0:T(8,128)(2,1)}, bf16[512,2048]{1,0:T(8,128)(2,1)}) custom-call(s32[8,8,256]{2,1,0:T(8,128)S(1)} %fusion.16.table_ref, bf16[8,384,2048]{2,1,0:T(8,128)(2,1)} %expert_out.1.rows_ref), custom_call_target="tpu_custom_call" | custom-call | flops 3221225472 | bytes 20971520 | tf_op jit(solution)/shard_map/tokens_of_slots/pallas_call | solution.py:188
  438.1 8.1 collective-permute-done.140
  452.4 7.9 collective-permute-done.164
  460.4 9.1 %collective-permute-done.165 = bf16[256,512]{0,1:T(8,128)(2,1)S(1)} collective-permute-done((bf16[256,512]{0,1:T(8,128)(2,1)S(1)}, bf16[256,512]{0,1:T(8,128)(2,1)S(1)}, u32[]{:S(2)}, u32[]{:S(2)}) %collective-permute-start.165) | collective-permute-done | bytes 262176 | tf_op jit(solution)/shard_map/ppermute | solution.py:30
  479.5 5.9 collective-permute-done.168
  487.5 12.8 %collective-permute-done.119 = bf16[512,2176]{1,0:T(8,128)(2,1)S(1)} collective-permute-done((bf16[512,2176]{1,0:T(8,128)(2,1)S(1)}, bf16[512,2176]{1,0:T(8,128)(2,1)S(1)}, u32[]{:S(2)}, u32[]{:S(2)}) %collective-permute-start.119) | collective-permute-done | bytes 2228256 | tf_op jit(solution)/shard_map/ppermute | solution.py:30
  502.3 42.0 %collective-permute-done.109 = bf16[512,2048]{1,0:T(8,128)(2,1)S(1)} collective-permute-done((bf16[512,2048]{1,0:T(8,128)(2,1)}, bf16[512,2048]{1,0:T(8,128)(2,1)S(1)}, u32[]{:S(2)}, u32[]{:S(2)}) %collective-permute-start.109) | collective-permute-done | bytes 2097184 | tf_op jit(solution)/shard_map/ppermute | solution.py:30
  551.2 18.7 %collective-permute-done.110 = bf16[256,2048]{1,0:T(8,128)(2,1)S(1)} collective-permute-done((bf16[256,2048]{1,0:T(8,128)(2,1)S(1)}, bf16[256,2048]{1,0:T(8,128)(2,1)S(1)}, u32[]{:S(2)}, u32[]{:S(2)}) %collective-permute-start.110) | collective-permute-done | bytes 1048608 | tf_op jit(solution)/shard_map/ppermute | solution.py:30
  574.6 6.6 collective-permute-done.111
  604.9 5.1 collective-permute-start.177
  633.6 28.0 %expert_weight_grads.1 = (f32[8,2048,256]{2,1,0:T(8,128)}, f32[8,2048,256]{2,1,0:T(8,128)}, f32[8,256,2048]{2,1,0:T(8,128)}) custom-call(bf16[8,384,2176]{2,1,0:T(8,128)(2,1)} %rows_of_slots.2.x_ref, bf16[8,384,2048]{2,1,0:T(8,128)(2,1)} %rows_of_slots.3.cot_ref, bf16[8,384,256]{2,1,0:T(8,128)(2,1)S(1)} %get-tuple-element.29.act_ref, ...), custom_call_target="tpu_custom_call" | custom-call | flops 9663676416 | bytes 80216064 | tf_op jit(solution)/shard_map/expert_weight_grads/pallas_call | solution.py:223
  672.8 6.9 all-reduce
  692.3 48.2 %reduce-scatter.7.cloned.1.call-done = f32[16,8]{1,0:T(8,128)} async-done(((f32[128,8]{1,0:T(8,128)}), f32[16,8]{1,0:T(8,128)}) %reduce-scatter.7.cloned.1.call-update) | async-done | bytes 528
  768.2 7.8 collective-permute-done.151
  776.0 7.6 collective-permute-done.144
  783.7 7.3 collective-permute-done.158
  799.1 6.4 collective-permute-done.154
  816.3 7.0 collective-permute-done.148
  832.5 4.8 collective-permute-done.162
  838.6 9.9 %collective-permute-done.156 = bf16[256,512]{1,0:T(8,128)(2,1)S(1)} collective-permute-done((bf16[256,512]{1,0:T(8,128)(2,1)S(1)}, bf16[256,512]{1,0:T(8,128)(2,1)S(1)}, u32[]{:S(2)}, u32[]{:S(2)}) %collective-permute-start.156) | collective-permute-done | bytes 262176 | tf_op jit(solution)/shard_map/ppermute | solution.py:30
  857.4 25.8 %all-reduce.4.cloned.1.call-done = f32[66,256]{1,0:T(8,128)} async-done(((f32[66,256]{1,0:T(8,128)}), f32[66,256]{1,0:T(8,128)}) %all-reduce.4.cloned.1.call-update) | async-done | bytes 67600 | tf_op jit(solution)/shard_map/psum | solution.py:646
  (868 shorter events, 487.2 us)
Async XLA Ops:
  7.2 733.3 %reduce-scatter.7.cloned.1.call-start = ((), (), s32[]{:S(2)}) async-start(), calls=%async_computation.4 | async-start | bytes 73728
  15.9 123.1 %collective-permute-start.38 = (s32[8,256]{1,0:T(8,128)}, s32[8,256]{1,0:T(8,128)}, u32[]{:S(2)}, u32[]{:S(2)}) collective-permute-start(s32[8,256]{1,0:T(8,128)} %bitcast.350), channel_id=1, source_target_pairs={{0,8},{1,9},{2,10},{3,11},{4,12},{5,13},{6,14},{7,15},{8,16},{9,17... | collective-permute-start | bytes 24584 | tf_op jit(solution)/shard_map/ppermute | solution.py:30
  37.1 185.1 %collective-permute-start.41 = (s32[8,256]{1,0:T(8,128)S(1)}, s32[8,256]{1,0:T(8,128)S(1)}, u32[]{:S(2)}, u32[]{:S(2)}) collective-permute-start(s32[8,256]{1,0:T(8,128)S(1)} %bitcast.351), channel_id=1, source_target_pairs={{0,4},{1,5},{2,6},{3,7},{4,0},{5,1},{6,2},{7,3},{8,12},{9,13},{10,... | collective-permute-start | bytes 24584 | tf_op jit(solution)/shard_map/ppermute | solution.py:30
  38.8 54.9 %collective-permute-start.17 = (bf16[256,512]{1,0:T(8,128)(2,1)}, bf16[256,512]{1,0:T(8,128)(2,1)}, u32[]{:S(2)}, u32[]{:S(2)}) collective-permute-start(bf16[256,512]{1,0:T(8,128)(2,1)} %param.21), channel_id=1, source_target_pairs={{0,4},{1,5},{2,6},{3,7},{4,0},{5,1},{6,2},{7,3},{8,12},{9,13},{10,... | collective-permute-start | bytes 786440 | tf_op jit(solution)/shard_map/ppermute | solution.py:30
  139.0 87.1 %collective-permute-start.91 = (bf16[64,2048]{1,0:T(8,128)(2,1)S(1)}, bf16[64,2048]{1,0:T(8,128)(2,1)S(1)}, u32[]{:S(2)}, u32[]{:S(2)}) collective-permute-start(bf16[64,2048]{1,0:T(8,128)(2,1)S(1)} %dynamic-slice_convert_fusion.refs_0_), channel_id=1, source_target_pairs={{0,4},{1,5},{2,6},{3,7},{4,0},{5,1},{6,2},{7,3},{8,12},{9,13},{10,... | collective-permute-start | bytes 786440 | tf_op jit(solution)/shard_map/ppermute | solution.py:30
  156.5 66.1 %collective-permute-start.42 = (s32[8,256]{1,0:T(8,128)}, s32[8,256]{1,0:T(8,128)S(1)}, u32[]{:S(2)}, u32[]{:S(2)}) collective-permute-start(s32[8,256]{1,0:T(8,128)} %collective-permute-done.38), channel_id=1, source_target_pairs={{0,4},{1,5},{2,6},{3,7},{4,0},{5,1},{6,2},{7,3},{8,12},{9,13},{10,... | collective-permute-start | bytes 24584 | tf_op jit(solution)/shard_map/ppermute | solution.py:30
  158.6 44.3 %collective-permute-start.40 = (s32[8,256]{1,0:T(8,128)S(1)}, s32[8,256]{1,0:T(8,128)S(1)}, u32[]{:S(2)}, u32[]{:S(2)}) collective-permute-start(s32[8,256]{1,0:T(8,128)S(1)} %collective-permute-done.39), channel_id=1, source_target_pairs={{0,8},{1,9},{2,10},{3,11},{4,12},{5,13},{6,14},{7,15},{8,16},{9,17... | collective-permute-start | bytes 24584 | tf_op jit(solution)/shard_map/ppermute | solution.py:30
  354.4 83.0 %collective-permute-start.139 = (bf16[64,256]{1,0:T(8,128)(2,1)S(1)}, bf16[64,256]{1,0:T(8,128)(2,1)S(1)}, u32[]{:S(2)}, u32[]{:S(2)}) collective-permute-start(bf16[64,256]{1,0:T(8,128)(2,1)S(1)} %copy-done.97), channel_id=1, source_target_pairs={{0,28},{1,29},{2,30},{3,31},{4,24},{5,25},{6,26},{7,27},{8,4},{9,5... | collective-permute-start | bytes 98312 | tf_op jit(solution)/shard_map/ppermute | solution.py:30
  356.2 57.8 %collective-permute-start.138 = (bf16[64,256]{1,0:T(8,128)(2,1)S(1)}, bf16[64,256]{1,0:T(8,128)(2,1)S(1)}, u32[]{:S(2)}, u32[]{:S(2)}) collective-permute-start(bf16[64,256]{1,0:T(8,128)(2,1)S(1)} %copy-done.98), channel_id=1, source_target_pairs={{0,20},{1,21},{2,22},{3,23},{4,16},{5,17},{6,18},{7,19},{8,28},{9,... | collective-permute-start | bytes 98312 | tf_op jit(solution)/shard_map/ppermute | solution.py:30
  356.5 57.5 %collective-permute-start.137 = (bf16[64,256]{1,0:T(8,128)(2,1)S(1)}, bf16[64,256]{1,0:T(8,128)(2,1)S(1)}, u32[]{:S(2)}, u32[]{:S(2)}) collective-permute-start(bf16[64,256]{1,0:T(8,128)(2,1)S(1)} %copy-done.99), channel_id=1, source_target_pairs={{0,12},{1,13},{2,14},{3,15},{4,8},{5,9},{6,10},{7,11},{8,20},{9,21... | collective-permute-start | bytes 98312 | tf_op jit(solution)/shard_map/ppermute | solution.py:30
  359.4 45.7 %collective-permute-start.134 = (bf16[64,256]{1,0:T(8,128)(2,1)S(1)}, bf16[64,256]{1,0:T(8,128)(2,1)S(1)}, u32[]{:S(2)}, u32[]{:S(2)}) collective-permute-start(bf16[64,256]{1,0:T(8,128)(2,1)S(1)} %copy-done.102), channel_id=1, source_target_pairs={{0,16},{1,17},{2,18},{3,19},{4,20},{5,21},{6,22},{7,23},{8,24},{9,... | collective-permute-start | bytes 98312 | tf_op jit(solution)/shard_map/ppermute | solution.py:30
  361.6 43.5 %collective-permute-start.133 = (bf16[64,256]{1,0:T(8,128)(2,1)S(1)}, bf16[64,256]{1,0:T(8,128)(2,1)S(1)}, u32[]{:S(2)}, u32[]{:S(2)}) collective-permute-start(bf16[64,256]{1,0:T(8,128)(2,1)S(1)} %copy-done.103), channel_id=1, source_target_pairs={{0,8},{1,9},{2,10},{3,11},{4,12},{5,13},{6,14},{7,15},{8,16},{9,17... | collective-permute-start | bytes 98312 | tf_op jit(solution)/shard_map/ppermute | solution.py:30
  405.1 41.6 %collective-permute-start.118 = (bf16[512,2176]{1,0:T(8,128)(2,1)}, bf16[512,2176]{1,0:T(8,128)(2,1)}, u32[]{:S(2)}, u32[]{:S(2)}) collective-permute-start(bf16[512,2176]{1,0:T(8,128)(2,1)} %get-tuple-element.38), channel_id=1, source_target_pairs={{0,1},{1,0},{2,3},{3,2},{4,5},{5,4},{6,7},{7,6},{8,9},{9,8},{10,11... | collective-permute-start | bytes 6684680 | tf_op jit(solution)/shard_map/ppermute | solution.py:30
  437.4 32.5 %collective-permute-start.108 = (bf16[512,2048]{1,0:T(8,128)(2,1)}, bf16[512,2048]{1,0:T(8,128)(2,1)S(1)}, u32[]{:S(2)}, u32[]{:S(2)}) collective-permute-start(bf16[512,2048]{1,0:T(8,128)(2,1)} %get-tuple-element.33), channel_id=1, source_target_pairs={{0,1},{1,0},{2,3},{3,2},{4,5},{5,4},{6,7},{7,6},{8,9},{9,8},{10,11... | collective-permute-start | bytes 6291464 | tf_op jit(solution)/shard_map/ppermute | solution.py:30
  446.2 40.5 %collective-permute-start.117 = (bf16[512,2176]{1,0:T(8,128)(2,1)S(1)}, bf16[512,2176]{1,0:T(8,128)(2,1)S(1)}, u32[]{:S(2)}, u32[]{:S(2)}) collective-permute-start(bf16[512,2176]{1,0:T(8,128)(2,1)S(1)} %get-tuple-element.36), channel_id=1, source_target_pairs={{0,1},{1,0},{2,3},{3,2},{4,5},{5,4},{6,7},{7,6},{8,9},{9,8},{10,11... | collective-permute-start | bytes 6684680 | tf_op jit(solution)/shard_map/ppermute | solution.py:30
  448.9 51.4 %collective-permute-start.119 = (bf16[512,2176]{1,0:T(8,128)(2,1)S(1)}, bf16[512,2176]{1,0:T(8,128)(2,1)S(1)}, u32[]{:S(2)}, u32[]{:S(2)}) collective-permute-start(bf16[512,2176]{1,0:T(8,128)(2,1)S(1)} %add_convert_fusion), channel_id=1, source_target_pairs={{0,2},{1,3},{2,0},{3,1},{4,6},{5,7},{6,4},{7,5},{8,10},{9,11},{10,... | collective-permute-start | bytes 6684680 | tf_op jit(solution)/shard_map/ppermute | solution.py:30
  472.1 72.2 %collective-permute-start.109 = (bf16[512,2048]{1,0:T(8,128)(2,1)}, bf16[512,2048]{1,0:T(8,128)(2,1)S(1)}, u32[]{:S(2)}, u32[]{:S(2)}) collective-permute-start(bf16[512,2048]{1,0:T(8,128)(2,1)} %add_convert_fusion.1), channel_id=1, source_target_pairs={{0,2},{1,3},{2,0},{3,1},{4,6},{5,7},{6,4},{7,5},{8,10},{9,11},{10,... | collective-permute-start | bytes 6291464 | tf_op jit(solution)/shard_map/ppermute | solution.py:30
  486.7 59.3 %collective-permute-start.170 = (bf16[256,512]{0,1:T(8,128)(2,1)S(1)}, bf16[256,512]{0,1:T(8,128)(2,1)S(1)}, u32[]{:S(2)}, u32[]{:S(2)}) collective-permute-start(bf16[256,512]{0,1:T(8,128)(2,1)S(1)} %collective-permute-done.166), channel_id=1, source_target_pairs={{0,4},{1,5},{2,6},{3,7},{4,0},{5,1},{6,2},{7,3},{8,12},{9,13},{10,... | collective-permute-start | bytes 786440 | tf_op jit(solution)/shard_map/ppermute | solution.py:30
  501.2 45.5 %collective-permute-start.120 = (bf16[256,2176]{1,0:T(8,128)(2,1)S(1)}, bf16[256,2176]{1,0:T(8,128)(2,1)S(1)}, u32[]{:S(2)}, u32[]{:S(2)}) collective-permute-start(bf16[256,2176]{1,0:T(8,128)(2,1)S(1)} %slice.281), channel_id=1, source_target_pairs={{0,4},{1,5},{2,6},{3,7},{4,0},{5,1},{6,2},{7,3},{8,12},{9,13},{10,... | collective-permute-start | bytes 3342344 | tf_op jit(solution)/shard_map/ppermute | solution.py:30
  604.6 59.3 %collective-permute-start.126 = (bf16[64,2048]{1,0:T(8,128)(2,1)S(1)}, bf16[64,2048]{1,0:T(8,128)(2,1)S(1)}, u32[]{:S(2)}, u32[]{:S(2)}) collective-permute-start(bf16[64,2048]{1,0:T(8,128)(2,1)S(1)} %get-tuple-element.62), channel_id=1, source_target_pairs={{0,1},{1,0},{2,3},{3,2},{4,5},{5,4},{6,7},{7,6},{8,9},{9,8},{10,11... | collective-permute-start | bytes 786440 | tf_op jit(solution)/shard_map/ppermute | solution.py:30
  661.6 102.3 %collective-permute-start.116 = (f32[64,2048]{1,0:T(8,128)}, f32[64,2048]{1,0:T(8,128)}, u32[]{:S(2)}, u32[]{:S(2)}) collective-permute-start(f32[64,2048]{1,0:T(8,128)} %get-tuple-element.105), channel_id=1, source_target_pairs={{0,1},{1,0},{2,3},{3,2},{4,5},{5,4},{6,7},{7,6},{8,9},{9,8},{10,11... | collective-permute-start | bytes 1572872 | tf_op jit(solution)/shard_map/ppermute | solution.py:30
  662.1 97.8 %collective-permute-start.114 = (f32[64,2048]{1,0:T(8,128)}, f32[64,2048]{1,0:T(8,128)}, u32[]{:S(2)}, u32[]{:S(2)}) collective-permute-start(f32[64,2048]{1,0:T(8,128)} %get-tuple-element.105), channel_id=1, source_target_pairs={{0,2},{1,3},{2,0},{3,1},{4,6},{5,7},{6,4},{7,5},{8,10},{9,11},{10,... | collective-permute-start | bytes 1572872 | tf_op jit(solution)/shard_map/ppermute | solution.py:30
  663.8 78.8 %collective-permute-start.180 = (bf16[8,64,256]{2,1,0:T(8,128)(2,1)}, bf16[8,64,256]{2,1,0:T(8,128)(2,1)}, u32[]{:S(2)}, u32[]{:S(2)}) collective-permute-start(bf16[8,64,256]{2,1,0:T(8,128)(2,1)} %constant_dynamic-update-slice_fusion.18), channel_id=1, source_target_pairs={{0,1},{1,0},{2,3},{3,2},{4,5},{5,4},{6,7},{7,6},{8,9},{9,8},{10,11... | collective-permute-start | bytes 786440 | tf_op jit(solution)/shard_map/ppermute | solution.py:30
  663.9 80.2 %collective-permute-start.179 = (bf16[8,64,256]{2,1,0:T(8,128)(2,1)}, bf16[8,64,256]{2,1,0:T(8,128)(2,1)}, u32[]{:S(2)}, u32[]{:S(2)}) collective-permute-start(bf16[8,64,256]{2,1,0:T(8,128)(2,1)} %collective-permute-done.178), channel_id=1, source_target_pairs={{0,1},{1,0},{2,3},{3,2},{4,5},{5,4},{6,7},{7,6},{8,9},{9,8},{10,11... | collective-permute-start | bytes 786440 | tf_op jit(solution)/shard_map/ppermute | solution.py:30
  680.6 175.3 %reduce-scatter.5.cloned.1.call-start = ((), (), s32[]{:S(2)}) async-start(), calls=%async_computation.2 | async-start | bytes 663552 | tf_op jit(solution)/shard_map/reduce_scatter | solution.py:640
  691.7 55.8 %collective-permute-start.150 = (bf16[256,512]{1,0:T(8,128)(2,1)}, bf16[256,512]{1,0:T(8,128)(2,1)S(1)}, u32[]{:S(2)}, u32[]{:S(2)}) collective-permute-start(bf16[256,512]{1,0:T(8,128)(2,1)} %get-tuple-element.57), channel_id=1, source_target_pairs={{0,8},{1,9},{2,10},{3,11},{4,12},{5,13},{6,14},{7,15},{8,16},{9,17... | collective-permute-start | bytes 786440 | tf_op jit(solution)/shard_map/ppermute | solution.py:30
  757.6 71.7 %collective-permute-start.160 = (bf16[256,512]{1,0:T(8,128)(2,1)}, bf16[256,512]{1,0:T(8,128)(2,1)}, u32[]{:S(2)}, u32[]{:S(2)}) collective-permute-start(bf16[256,512]{1,0:T(8,128)(2,1)} %copy.177), channel_id=1, source_target_pairs={{0,4},{1,5},{2,6},{3,7},{4,0},{5,1},{6,2},{7,3},{8,12},{9,13},{10,... | collective-permute-start | bytes 786440 | tf_op jit(solution)/shard_map/ppermute | solution.py:30
  759.8 36.7 %collective-permute-start.153 = (bf16[256,512]{1,0:T(8,128)(2,1)}, bf16[256,512]{1,0:T(8,128)(2,1)}, u32[]{:S(2)}, u32[]{:S(2)}) collective-permute-start(bf16[256,512]{1,0:T(8,128)(2,1)} %get-tuple-element.57), channel_id=1, source_target_pairs={{0,4},{1,5},{2,6},{3,7},{4,0},{5,1},{6,2},{7,3},{8,12},{9,13},{10,... | collective-permute-start | bytes 786440 | tf_op jit(solution)/shard_map/ppermute | solution.py:30
  760.4 53.4 %collective-permute-start.146 = (bf16[256,512]{1,0:T(8,128)(2,1)}, bf16[256,512]{1,0:T(8,128)(2,1)}, u32[]{:S(2)}, u32[]{:S(2)}) collective-permute-start(bf16[256,512]{1,0:T(8,128)(2,1)} %get-tuple-element.59), channel_id=1, source_target_pairs={{0,4},{1,5},{2,6},{3,7},{4,0},{5,1},{6,2},{7,3},{8,12},{9,13},{10,... | collective-permute-start | bytes 786440 | tf_op jit(solution)/shard_map/ppermute | solution.py:30
  763.8 119.4 %all-reduce.4.cloned.1.call-start = ((), (), s32[]{:S(2)}) async-start(), calls=%async_computation.3 | async-start | bytes 147456 | tf_op jit(solution)/shard_map/psum | solution.py:646
  791.0 40.2 %collective-permute-start.161 = (bf16[256,512]{1,0:T(8,128)(2,1)S(1)}, bf16[256,512]{1,0:T(8,128)(2,1)S(1)}, u32[]{:S(2)}, u32[]{:S(2)}) collective-permute-start(bf16[256,512]{1,0:T(8,128)(2,1)S(1)} %copy-done.86), channel_id=1, source_target_pairs={{0,4},{1,5},{2,6},{3,7},{4,0},{5,1},{6,2},{7,3},{8,12},{9,13},{10,... | collective-permute-start | bytes 786440 | tf_op jit(solution)/shard_map/ppermute | solution.py:30
  813.7 41.8 %collective-permute-start.132 = (f32[64,2048]{1,0:T(8,128)S(1)}, f32[64,2048]{1,0:T(8,128)S(1)}, u32[]{:S(2)}, u32[]{:S(2)}) collective-permute-start(f32[64,2048]{1,0:T(8,128)S(1)} %subtract_add_fusion), channel_id=1, source_target_pairs={{0,1},{1,0},{2,3},{3,2},{4,5},{5,4},{6,7},{7,6},{8,9},{9,8},{10,11... | collective-permute-start | bytes 1572872 | tf_op jit(solution)/shard_map/ppermute | solution.py:30
  (293 other events, 5457.3 us)
Sparse Core Ops, SparseCore 0:
  680.7 59.8 reduce-scatter.6
  763.9 66.3 reduce-scatter.4
  856.0 27.1 all-reduce.3

commit v2 on v1

v2 whole, which is shorter than its diff:
```python
import math

import jax
import jax.numpy as jnp
from jax import lax
from jax.experimental import pallas as pl
from jax.experimental.pallas import tpu as pltpu
from jax.sharding import PartitionSpec as P

D = 2048
HD = 128
E = 64
TOPK = 8
CAP = 48
EXTRA = 2 * E

bf16 = jnp.bfloat16
f32 = jnp.float32

epsilon = 1e-05


def hop(values, move):
    dp, tp = lax.axis_size("dp"), lax.axis_size("tp")
    pairs = []
    for a in range(dp):
        for b in range(tp):
            c, e = move(a, b)
            pairs.append((a * tp + b, c * tp + e))
    return lax.ppermute(values, ("dp", "tp"), pairs)


def over_z(values, steps=1):
    half = lax.axis_size("dp") // 2
    return hop(values, lambda a, b: ((a // 2 + steps) % half * 2 + a % 2, b))


def over_y(values):
    return hop(values, lambda a, b: (a ^ 1, b))


def over_x(values):
    return hop(values, lambda a, b: (a, b ^ 2))


def over_core(values):
    return hop(values, lambda a, b: (a, b ^ 1))


def gather_dp(values):
    half = lax.axis_size("dp") // 2
    line = [values]
    for _ in range(half - 1):
        line.append(over_z(line[-1]))
    return line + [over_y(v) for v in line]


def gather_all(values):
    line = gather_dp(values)
    both = [(v, over_x(v)) for v in line]
    return [(a, over_core(a), b, over_core(b)) for a, b in both]


def absolute_dp(pieces):
    dp = lax.axis_size("dp")
    half = dp // 2
    me = lax.axis_index("dp")
    backwards = [(half - 1 - i) % half for i in range(2 * half - 1)]
    near = jnp.stack([pieces[dz] for dz in backwards])
    far = jnp.stack([pieces[half + dz] for dz in backwards])
    start = half - 1 - me // 2
    near = lax.dynamic_slice_in_dim(near, start, half, 0)
    far = lax.dynamic_slice_in_dim(far, start, half, 0)
    odd = me % 2 == 1
    both = jnp.stack([jnp.where(odd, far, near), jnp.where(odd, near, far)], axis=1)
    return both.reshape((dp,) + pieces[0].shape)


def absolute_tp(pieces, axis=0):
    me = lax.axis_index("tp")
    first = [jnp.where(me % 2 == 1, pieces[i ^ 1], pieces[i]) for i in range(4)]
    second = [jnp.where(me // 2 == 1, first[i ^ 2], first[i]) for i in range(4)]
    return jnp.concatenate(second, axis=axis)


def gather_tp(values):
    other = over_x(values)
    return [values, over_core(values), other, over_core(other)]


def added(*terms):
    total = terms[0].astype(f32)
    for term in terms[1:]:
        total = total + term.astype(f32)
    return total


def scatter_tp(parts):
    mine, far = over_core(parts[1]), over_core(parts[3])
    return parts[0], mine, over_x(added(parts[2], far).astype(bf16))


def after(values, *others):
    return lax.optimization_barrier((values,) + others)[0]


def scatter_near(parts, wait=()):
    first = after(parts[1], *wait) if wait else parts[1]
    mine, far = over_core(first), over_core(parts[3])
    crossing = added(parts[2], far).astype(bf16)
    return added(parts[0], mine, over_x(crossing)), crossing


def scatter_line(near, far_line, between=()):
    half = lax.axis_size("dp") // 2
    share = near.shape[0] // half
    between = list(between)
    gate = lambda values: after(values, *between.pop(0)) if between else values
    line = near + over_y(gate(far_line.astype(bf16))).astype(f32)
    moving = line[(half - 1) * share :]
    for dz in reversed(range(1, half - 1)):
        moving = gate(moving.astype(bf16))
        moving = line[dz * share : (dz + 1) * share] + over_z(moving, -1).astype(f32)
    return line[:share], over_z(gate(moving.astype(bf16)), -1)


def owner(pos):
    half = lax.axis_size("dp") // 2
    me = lax.axis_index("dp")
    return (me // 2 - pos % half) % half * 2 + (me % 2 ^ pos // half)


def reduce_dp(values):
    dp = lax.axis_size("dp")
    half = dp // 2
    slab = values.shape[1] // dp
    part = [lax.dynamic_slice_in_dim(values, owner(i) * slab, slab, 1) for i in range(dp)]
    line = jnp.stack(part[:half]) + over_y(jnp.stack(part[half:]))
    moving = line[half - 1]
    for dz in reversed(range(half - 1)):
        moving = line[dz] + over_z(moving, -1)
    return moving


def reduce_tp(values):
    values = values + over_core(values)
    return values + over_x(values)


def chosen_slots(table):
    experts, tokens = table.shape
    place = lax.broadcasted_iota(jnp.int32, (experts, CAP, tokens), 1)
    hit = place == table[:, None, :]
    return jnp.where(hit, 1.0, 0.0).astype(bf16).reshape(experts * CAP, tokens)


def rows_of_slots(pieces, table):
    sequences, experts, tokens = table.shape
    flat = [piece for group in pieces for piece in group]
    share, width = flat[0].shape
    groups = len(flat) // sequences

    def kernel(table_ref, *refs):
        sources, (out_ref, buffer, arrived) = refs[: len(flat)], refs[len(flat) :]
        step = pl.program_id(0)

        @pl.when(step == 0)
        def _():
            for i, source in enumerate(sources):
                pltpu.make_async_copy(
                    source, buffer.at[i // groups, pl.ds(i % groups * share, share)], arrived.at[i]
                ).start()

        for i in range(groups):
            pltpu.make_async_copy(
                sources[i], buffer.at[step, pl.ds(i * share, share)], arrived.at[step * groups + i]
            ).wait()
        picked = jnp.dot(chosen_slots(table_ref[0]), buffer[step], preferred_element_type=f32)
        out_ref[...] = picked.astype(bf16).reshape(experts, CAP, width)

    return pl.pallas_call(
        kernel,
        grid=(sequences,),
        in_specs=[pl.BlockSpec((1, experts, tokens), lambda s: (s, 0, 0))]
        + [pl.BlockSpec(memory_space=pl.ANY)] * len(flat),
        out_specs=pl.BlockSpec((experts, CAP, width), lambda s: (0, s, 0)),
        out_shape=jax.ShapeDtypeStruct((experts, sequences * CAP, width), bf16),
        scratch_shapes=[
            pltpu.VMEM((sequences, tokens, width), bf16),
            pltpu.SemaphoreType.DMA((len(flat),)),
        ],
        compiler_params=pltpu.CompilerParams(vmem_limit_bytes=48 << 20),
        cost_estimate=pl.CostEstimate(
            flops=2 * experts * CAP * sequences * tokens * width,
            bytes_accessed=2 * sequences * (tokens + experts * CAP) * width,
            transcendentals=0,
        ),
        name="rows_of_slots",
    )(table, *flat)


def tokens_of_slots(rows, table):
    sequences, experts, tokens = table.shape
    width = rows.shape[-1]
    share = tokens // 4

    def kernel(table_ref, rows_ref, *outs):
        picked = chosen_slots(table_ref[0])
        total = lax.dot_general(
            picked,
            rows_ref[...].reshape(experts * CAP, width),
            (((0,), (0,)), ((), ())),
            preferred_element_type=f32,
        ).astype(bf16)
        for q, out in enumerate(outs):
            out[...] = total[q * share : (q + 1) * share]

    return pl.pallas_call(
        kernel,
        grid=(sequences,),
        in_specs=[
            pl.BlockSpec((1, experts, tokens), lambda s: (s, 0, 0)),
            pl.BlockSpec((experts, CAP, width), lambda s: (0, s, 0)),
        ],
        out_specs=[pl.BlockSpec((share, width), lambda s: (s, 0))] * 4,
        out_shape=[jax.ShapeDtypeStruct((sequences * share, width), bf16)] * 4,
        compiler_params=pltpu.CompilerParams(vmem_limit_bytes=48 << 20),
        cost_estimate=pl.CostEstimate(
            flops=2 * experts * CAP * sequences * tokens * width,
            bytes_accessed=2 * sequences * (tokens + experts * CAP) * width,
            transcendentals=0,
        ),
        name="tokens_of_slots",
    )(table, rows)


def dot_last(a, b):
    return lax.dot_general(a, b, (((1,), (1,)), ((), ())), preferred_element_type=f32)


def dot_first(a, b):
    return lax.dot_general(a, b, (((0,), (0,)), ((), ())), preferred_element_type=f32)


def per_expert(kernel, experts, ins, outs, flops, name, scalars=()):
    whole = lambda shape: pl.BlockSpec((1,) + tuple(shape[1:]), lambda e: (e, 0, 0))
    in_specs = [pl.BlockSpec(memory_space=pltpu.SMEM)] * len(scalars)
    moved = 0
    for array, block in ins:
        in_specs.append(pl.BlockSpec((1,) + block, lambda e: (e, 0, 0)))
        moved += experts * math.prod(block) * array.dtype.itemsize
    moved += sum(math.prod(o.shape) * o.dtype.itemsize for o in outs)
    return pl.pallas_call(
        kernel,
        grid=(experts,),
        in_specs=in_specs,
        out_specs=[whole(o.shape) for o in outs],
        out_shape=list(outs),
        compiler_params=pltpu.CompilerParams(vmem_limit_bytes=48 << 20),
        cost_estimate=pl.CostEstimate(flops=flops, bytes_accessed=moved, transcendentals=0),
        name=name,
    )(*scalars, *[array for array, _ in ins])


def grad_of_hidden(cot_rows, down_weight):
    experts, rows, width = cot_rows.shape
    hidden = down_weight.shape[1]

    def kernel(cot_ref, down_ref, out_ref):
        out_ref[0] = dot_last(cot_ref[0], down_ref[0])

    return per_expert(
        kernel,
        experts,
        [(cot_rows, (rows, width)), (down_weight, (hidden, width))],
        [jax.ShapeDtypeStruct((experts, rows, hidden), f32)],
        2 * experts * rows * width * hidden,
        "grad_of_hidden",
    )[0]


def expert_step(x_rows, gate_weight, up_weight, hidden_grad, first_expert):
    experts, rows, wide = x_rows.shape
    width, hidden = gate_weight.shape[1:]

    def kernel(base_ref, x_ref, gate_ref, up_ref, grad_ref, back_ref, act_ref, gate_grad_ref, up_grad_ref):
        mine = base_ref[0] + pl.program_id(0)
        x = x_ref[0, :, :width]
        lane = lax.broadcasted_iota(jnp.int32, (rows, EXTRA), 1)
        probs = x_ref[0, :, width:].astype(f32)
        mix = jnp.sum(
            jnp.where((lane == mine) | (lane == mine + E), probs, 0.0), axis=1, keepdims=True
        )
        gate_act = jnp.dot(x, gate_ref[0], preferred_element_type=f32)
        up_act = jnp.dot(x, up_ref[0], preferred_element_type=f32)
        raw = grad_ref[0]
        sig = jax.nn.sigmoid(gate_act)
        silu = gate_act * sig
        act = silu * up_act
        grad_mix = jnp.sum(act * raw, axis=1, keepdims=True)
        act_ref[0] = (mix * act).astype(bf16)
        weighted = mix * raw
        gate_grad = (weighted * up_act * sig * (1.0 + gate_act * (1.0 - sig))).astype(bf16)
        up_grad = (weighted * silu).astype(bf16)
        gate_grad_ref[0] = gate_grad
        up_grad_ref[0] = up_grad
        back_ref[0, :, :width] = (
            dot_last(gate_grad, gate_ref[0]) + dot_last(up_grad, up_ref[0])
        ).astype(bf16)
        coarse = grad_mix.astype(bf16).astype(f32)
        fine = grad_mix - coarse
        back_ref[0, :, width:] = jnp.where(
            lane == mine, coarse, jnp.where(lane == mine + E, fine, 0.0)
        ).astype(bf16)

    small = jax.ShapeDtypeStruct((experts, rows, hidden), bf16)
    return per_expert(
        kernel,
        experts,
        [
            (x_rows, (rows, wide)),
            (gate_weight, (width, hidden)),
            (up_weight, (width, hidden)),
            (hidden_grad, (rows, hidden)),
        ],
        [jax.ShapeDtypeStruct((experts, rows, wide), bf16), small, small, small],
        8 * experts * rows * width * hidden,
        "expert_step",
        (first_expert,),
    )


def expert_out(act, down_weight):
    experts, rows, hidden = act.shape
    width = down_weight.shape[2]

    def kernel(act_ref, down_ref, out_ref):
        out_ref[0] = jnp.dot(act_ref[0], down_ref[0], preferred_element_type=f32).astype(bf16)

    return per_expert(
        kernel,
        experts,
        [(act, (rows, hidden)), (down_weight, (hidden, width))],
        [jax.ShapeDtypeStruct((experts, rows, width), bf16)],
        2 * experts * rows * width * hidden,
        "expert_out",
    )[0]


def expert_weight_grad(left, right, name):
    experts = left[0].shape[0]
    rows = sum(half.shape[1] for half in left)
    width, columns = min(left[0].shape[2], D), min(right[0].shape[2], D)

    def kernel(a_ref, b_ref, c_ref, d_ref, out_ref):
        out_ref[0] = dot_first(
            jnp.concatenate([a_ref[0], b_ref[0]]), jnp.concatenate([c_ref[0], d_ref[0]])
        )

    return per_expert(
        kernel,
        experts,
        [(half, (half.shape[1], width)) for half in left]
        + [(half, (half.shape[1], columns)) for half in right],
        [jax.ShapeDtypeStruct((experts, width, columns), f32)],
        2 * experts * rows * width * columns,
        name,
    )[0]


def kernel_call(kernel, name, scalars, ins, outs, flops, scratch=()):
    moved = sum(a.size * a.dtype.itemsize for a in ins)
    moved += sum(math.prod(o.shape) * o.dtype.itemsize for o in outs)
    return pl.pallas_call(
        kernel,
        in_specs=[pl.BlockSpec(memory_space=pltpu.SMEM)] * len(scalars)
        + [pl.BlockSpec(memory_space=pltpu.VMEM)] * len(ins),
        out_specs=[pl.BlockSpec(memory_space=pltpu.VMEM)] * len(outs),
        out_shape=list(outs),
        scratch_shapes=list(scratch),
        compiler_params=pltpu.CompilerParams(vmem_limit_bytes=48 << 20),
        cost_estimate=pl.CostEstimate(flops=flops, bytes_accessed=moved, transcendentals=0),
        name=name,
    )(*scalars, *ins)


def shape_of(shape, dtype):
    return jax.ShapeDtypeStruct(shape, dtype)


def project(x_slabs, pieces, places, dtype, other=None):
    _, tokens, _ = x_slabs.shape
    columns = pieces[0].shape[1]

    def kernel(place_ref, x_ref, *refs):
        out_ref = refs[len(pieces) + (other is not None)]
        total = None
        for i in range(len(pieces)):
            part = jnp.dot(x_ref[place_ref[i]], refs[i][...], preferred_element_type=f32)
            total = part if total is None else total + part
        out_ref[...] = total.astype(dtype)
        if other is not None:
            first = refs[len(pieces)][...]
            lane = lax.broadcasted_iota(jnp.int32, (tokens, 128), 1)
            refs[-1][...] = jnp.where(
                lane < 64,
                jnp.sum(first * first, axis=1, keepdims=True),
                jnp.sum(total * total, axis=1, keepdims=True),
            )

    outs = [shape_of((tokens, columns), dtype)]
    extra = []
    if other is not None:
        outs.append(shape_of((tokens, 128), f32))
        extra = [other]
    return kernel_call(
        kernel, "project", [places], [x_slabs, *pieces, *extra], outs, 2 * x_slabs.size * columns
    )


def turned(values):
    return pltpu.roll(values, HD // 2, 1)


def attend(queries, key_proj, squares, values, gains, tables, bias, pieces, places):
    tokens, columns = queries.shape
    heads = columns // HD
    dp = len(pieces)
    slab = pieces[0].shape[1]
    share = tokens // 4
    lanes = 128 // heads

    def kernel(place_ref, q_ref, k_ref, sq_ref, v_ref, gain_ref, table_ref, bias_ref, *refs):
        weights = refs[:dp]
        q_out, k_out, log_out, att_out = refs[dp : dp + 4]
        parts, scratch = refs[dp + 4 : dp + 8], refs[dp + 8]
        cosine, sine = table_ref[0], table_ref[1]
        bias_value = bias_ref[...]
        lane = lax.broadcasted_iota(jnp.int32, (tokens, 128), 1)
        q_scale = lax.rsqrt(sq_ref[:, 0:1] / D + epsilon)
        k_scale = lax.rsqrt(sq_ref[:, 64:65] / D + epsilon)
        logs = jnp.zeros((tokens, 128), f32)
        for h in range(heads):
            cut = slice(h * HD, (h + 1) * HD)
            q = q_ref[:, cut] * q_scale * gain_ref[0:1, cut]
            k = k_ref[:, cut] * k_scale * gain_ref[1:2, cut]
            q = (q * cosine + turned(q) * sine).astype(bf16)
            k = (k * cosine + turned(k) * sine).astype(bf16)
            q_out[:, cut] = q
            k_out[:, cut] = k
            scores = dot_last(q, k) * (1.0 / math.sqrt(HD)) + bias_value
            largest = jnp.max(scores, axis=1, keepdims=True)
            raised = jnp.exp(scores - largest)
            total = jnp.sum(raised, axis=1, keepdims=True)
            logs = jnp.where(lane // lanes == h, largest + jnp.log(total), logs)
            probs = (raised / total).astype(bf16)
            att_out[:, cut] = jnp.dot(probs, v_ref[:, cut], preferred_element_type=f32).astype(bf16)
        log_out[...] = logs
        attended = att_out[...]
        for i in range(dp):
            scratch[place_ref[i]] = jnp.dot(
                attended, weights[i][...], preferred_element_type=f32
            ).astype(bf16)
        for q, part in enumerate(parts):
            start = pl.multiple_of((place_ref[dp] ^ q) * share, share)
            for i in range(dp):
                part[:, i * slab : (i + 1) * slab] = scratch[i, pl.ds(start, share), :]

    low = shape_of((tokens, columns), bf16)
    return kernel_call(
        kernel,
        "attend",
        [places],
        [queries, key_proj, squares, values, gains, tables, bias, *pieces],
        [low, low, shape_of((tokens, 128), f32), low] + [shape_of((share, slab * dp), bf16)] * 4,
        4 * tokens * tokens * columns + 2 * tokens * columns * slab * dp,
        [pltpu.VMEM((dp, tokens, slab), bf16)],
    )


def route(terms, hidden, gain, router):
    share, width = hidden.shape

    def kernel(a_ref, b_ref, c_ref, hidden_ref, gain_ref, router_ref, middle_ref, x_ref, probs_ref):
        middle = hidden_ref[...] + added(a_ref[...], b_ref[...], c_ref[...])
        middle_ref[...] = middle
        scale = lax.rsqrt(jnp.mean(middle * middle, axis=1, keepdims=True) + epsilon)
        normed = (middle * scale * gain_ref[...]).astype(bf16)
        x_ref[:, :width] = normed
        logits = dot_last(normed, router_ref[...])
        raised = jnp.exp(logits - jnp.max(logits, axis=1, keepdims=True))
        probs = raised / (0.5 * jnp.sum(raised, axis=1, keepdims=True))
        probs_ref[...] = probs
        coarse = probs.astype(bf16).astype(f32)
        lane = lax.broadcasted_iota(jnp.int32, probs.shape, 1)
        x_ref[:, width:] = jnp.where(lane < E, coarse, probs - coarse).astype(bf16)

    return kernel_call(
        kernel,
        "route",
        [],
        [*terms, hidden, gain, router],
        [
            shape_of((share, width), f32),
            shape_of((share, width + EXTRA), bf16),
            shape_of((share, EXTRA), f32),
        ],
        2 * share * width * EXTRA,
    )


def route_back(terms, middle, x_piece, probs, cotangent, gain, router):
    share, width = middle.shape

    def kernel(a_ref, b_ref, middle_ref, x_ref, probs_ref, cot_ref, gain_ref, router_ref, *outs):
        grad_ref, low_ref, router_out, gain_out = outs
        pair = added(a_ref[:, width:], b_ref[:, width:])
        grad_probs = pair + pltpu.roll(pair, E, 1)
        probs = probs_ref[...]
        inner = 0.5 * jnp.sum(probs * grad_probs, axis=1, keepdims=True)
        grad_logits = probs * (grad_probs - inner)
        middle = middle_ref[...]
        scale = lax.rsqrt(jnp.mean(middle * middle, axis=1, keepdims=True) + epsilon)
        lane = lax.broadcasted_iota(jnp.int32, probs.shape, 1)
        once = jnp.where(lane < E, grad_logits, 0.0)
        normed_grad = added(a_ref[:, :width], b_ref[:, :width]) + lax.dot_general(
            once,
            router_ref[...].astype(f32),
            (((1,), (0,)), ((), ())),
            precision=lax.Precision.HIGHEST,
            preferred_element_type=f32,
        )
        router_out[...] = lax.dot_general(
            once,
            x_ref[:, :width].astype(f32),
            (((0,), (0,)), ((), ())),
            precision=lax.Precision.HIGHEST,
            preferred_element_type=f32,
        )
        gain_out[...] = jnp.sum(normed_grad * middle * scale, axis=0, keepdims=True)
        scaled = normed_grad * gain_ref[...]
        grad = (
            cot_ref[...]
            + scale * scaled
            - middle * (scale * scale * scale) * jnp.mean(scaled * middle, axis=1, keepdims=True)
        )
        grad_ref[...] = grad
        low_ref[...] = grad.astype(bf16)

    return kernel_call(
        kernel,
        "route_back",
        [],
        [*terms, middle, x_piece, probs, cotangent, gain, router],
        [
            shape_of((share, width), f32),
            shape_of((share, width), bf16),
            shape_of((EXTRA, width), f32),
            shape_of((1, width), f32),
        ],
        24 * share * width * EXTRA,
    )


def attend_back(low_pieces, pieces, places, q_rot, k_rot, values, logs, queries, key_proj, squares, gains, tables, bias):
    tokens, columns = queries.shape
    heads = columns // HD
    dp = len(pieces)
    slab = pieces[0].shape[1]
    share = tokens // 4
    lanes = 128 // heads

    def kernel(place_ref, *refs):
        lows, weights = refs[:4], refs[4 : 4 + dp]
        qr_ref, kr_ref, v_ref, log_ref, q_ref, k_ref, sq_ref, gain_ref, table_ref, bias_ref = refs[
            4 + dp : 14 + dp
        ]
        gv_ref, gq_ref, gk_ref, inner_ref, gains_ref, scratch = refs[14 + dp :]
        for q, low in enumerate(lows):
            start = pl.multiple_of((place_ref[dp] ^ q) * share, share)
            for i in range(dp):
                scratch[i, pl.ds(start, share), :] = low[:, i * slab : (i + 1) * slab]
        total = None
        for i in range(dp):
            part = dot_last(scratch[place_ref[i]], weights[i][...])
            total = part if total is None else total + part
        grad_att = total.astype(bf16)
        cosine, sine = table_ref[0], table_ref[1]
        bias_value = bias_ref[...]
        q_scale = lax.rsqrt(sq_ref[:, 0:1] / D + epsilon)
        k_scale = lax.rsqrt(sq_ref[:, 64:65] / D + epsilon)
        q_inner = jnp.zeros((tokens, 1), f32)
        k_inner = jnp.zeros((tokens, 1), f32)
        for h in range(heads):
            cut = slice(h * HD, (h + 1) * HD)
            qr, kr, v, grad = qr_ref[:, cut], kr_ref[:, cut], v_ref[:, cut], grad_att[:, cut]
            scores = dot_last(qr, kr) * (1.0 / math.sqrt(HD)) + bias_value
            probs = jnp.exp(scores - log_ref[:, h * lanes : h * lanes + 1])
            gv_ref[:, cut] = dot_first(probs.astype(bf16), grad).astype(bf16)
            grad_probs = dot_last(grad, v)
            dots = jnp.sum(probs * grad_probs, axis=1, keepdims=True)
            grad_scores = (probs * (grad_probs - dots) * (1.0 / math.sqrt(HD))).astype(bf16)
            gq = jnp.dot(grad_scores, kr, preferred_element_type=f32)
            gk = dot_first(grad_scores, qr)
            gq = gq * cosine - turned(gq) * sine
            gk = gk * cosine - turned(gk) * sine
            q, k = q_ref[:, cut], k_ref[:, cut]
            gains_ref[0:1, cut] = jnp.sum(gq * q * q_scale, axis=0, keepdims=True)
            gains_ref[1:2, cut] = jnp.sum(gk * k * k_scale, axis=0, keepdims=True)
            gq = gq * gain_ref[0:1, cut]
            gk = gk * gain_ref[1:2, cut]
            gq_ref[:, cut] = gq
            gk_ref[:, cut] = gk
            q_inner = q_inner + jnp.sum(gq * q, axis=1, keepdims=True)
            k_inner = k_inner + jnp.sum(gk * k, axis=1, keepdims=True)
        lane = lax.broadcasted_iota(jnp.int32, (tokens, 128), 1)
        inner_ref[...] = jnp.where(lane < 64, q_inner, k_inner)

    return kernel_call(
        kernel,
        "attend_back",
        [places],
        [*low_pieces, *pieces, q_rot, k_rot, values, logs, queries, key_proj, squares, gains, tables, bias],
        [
            shape_of((tokens, columns), bf16),
            shape_of((tokens, columns), f32),
            shape_of((tokens, columns), f32),
            shape_of((tokens, 128), f32),
            shape_of((2, columns), f32),
        ],
        10 * tokens * tokens * columns + 2 * tokens * columns * slab * dp,
        [pltpu.VMEM((dp, tokens, slab), bf16)],
    )


def norm_back(gq, gk, queries, key_proj, squares, inner):
    tokens, columns = queries.shape

    def kernel(gq_ref, gk_ref, q_ref, k_ref, sq_ref, inner_ref, q_out, k_out):
        for i, (grad, value, out) in enumerate(((gq_ref, q_ref, q_out), (gk_ref, k_ref, k_out))):
            scale = lax.rsqrt(sq_ref[:, 64 * i : 64 * i + 1] / D + epsilon)
            mean = inner_ref[:, 64 * i : 64 * i + 1] / D
            out[...] = (
                scale * grad[...] - value[...] * (scale * scale * scale) * mean
            ).astype(bf16)

    low = shape_of((tokens, columns), bf16)
    return kernel_call(
        kernel, "norm_back", [], [gq, gk, queries, key_proj, squares, inner], [low, low], 0
    )


def project_back(grads, weights, places):
    tokens, columns = grads[0].shape
    dp = len(weights[0])
    slab = weights[0][0].shape[0]
    share = tokens // 4
    flat = [piece for pieces in weights for piece in pieces]

    def kernel(place_ref, *refs):
        values = [ref[...] for ref in refs[: len(grads)]]
        pieces = refs[len(grads) : len(grads) + len(flat)]
        parts, scratch = refs[len(grads) + len(flat) : -1], refs[-1]
        for i in range(dp):
            total = None
            for j, value in enumerate(values):
                part = dot_last(value, pieces[j * dp + i][...])
                total = part if total is None else total + part
            scratch[place_ref[i]] = total.astype(bf16)
        for q, part in enumerate(parts):
            start = pl.multiple_of((place_ref[dp] ^ q) * share, share)
            for i in range(dp):
                part[:, i * slab : (i + 1) * slab] = scratch[i, pl.ds(start, share), :]

    return kernel_call(
        kernel,
        "project_back",
        [places],
        [*grads, *flat],
        [shape_of((share, slab * dp), bf16)] * 4,
        2 * len(grads) * tokens * columns * slab * dp,
        [pltpu.VMEM((dp, tokens, slab), bf16)],
    )


def hidden_back(terms, hidden, grad_middle, gain):
    share, width = hidden.shape

    def kernel(a_ref, b_ref, c_ref, hidden_ref, grad_ref, gain_ref, out_ref, gain_out):
        normed_grad = added(a_ref[...], b_ref[...], c_ref[...])
        hidden = hidden_ref[...]
        scale = lax.rsqrt(jnp.mean(hidden * hidden, axis=1, keepdims=True) + epsilon)
        gain_out[...] = jnp.sum(normed_grad * hidden * scale, axis=0, keepdims=True)
        scaled = normed_grad * gain_ref[...]
        out_ref[...] = (
            grad_ref[...]
            + scale * scaled
            - hidden * (scale * scale * scale) * jnp.mean(scaled * hidden, axis=1, keepdims=True)
        )

    return kernel_call(
        kernel,
        "hidden_back",
        [],
        [*terms, hidden, grad_middle, gain],
        [shape_of((share, width), f32), shape_of((1, width), f32)],
        0,
    )


def token_product(slabs, whole, places, slab_first):
    sequences, share, slab = slabs[0].shape
    tokens, columns = whole[0].shape

    def kernel(place_ref, *refs):
        parts, wholes, out_ref, scratch = refs[:4], refs[4:-2], refs[-2], refs[-1]
        for q, part in enumerate(parts):
            start = pl.multiple_of((place_ref[sequences] ^ q) * share, share)
            scratch[:, pl.ds(start, share), :] = part[...]
        total = None
        for i in range(sequences):
            pair = (scratch[i], wholes[i][...])
            part = dot_first(*pair) if slab_first else dot_first(*pair[::-1])
            total = part if total is None else total + part
        out_ref[...] = total

    return kernel_call(
        kernel,
        "token_product",
        [places],
        [*slabs, *whole],
        [shape_of((slab, columns) if slab_first else (columns, slab), f32)],
        2 * sequences * tokens * slab * columns,
        [pltpu.VMEM((sequences, tokens, slab), bf16)],
    )[0]


def rope_tables(length, head_size):
    half_size = head_size // 2
    inverse = 10000.0 ** (-2.0 * jnp.arange(half_size, dtype=jnp.float32) / head_size)
    angles = jnp.arange(length, dtype=jnp.float32)[:, None] * inverse[None, :]
    cosine, sine = jnp.cos(angles), jnp.sin(angles)
    return jnp.stack(
        [jnp.concatenate([cosine, cosine], axis=1), jnp.concatenate([-sine, sine], axis=1)]
    )


def score_bias(segments):
    position = jnp.arange(segments.shape[0], dtype=jnp.int32)
    allowed = (position[None, :] <= position[:, None]) & (segments[:, None] == segments[None, :])
    return jnp.where(allowed, 0.0, -1e30).astype(f32)


def slot_tables(expert_ids, local_experts):
    data_size, tensor_size = lax.axis_size("dp"), lax.axis_size("tp")
    ids = jnp.stack(gather_dp(expert_ids.T))
    sequences, top, tokens = ids.shape
    share = tokens // tensor_size
    ids = absolute_tp([ids[:, :, q * share : (q + 1) * share] for q in range(4)], axis=2)
    mine = lax.axis_index("dp") * local_experts + jnp.arange(local_experts, dtype=jnp.int32)
    named = jnp.any(ids[:, None] == mine[None, :, None, None], axis=2)
    position = jnp.arange(tokens, dtype=jnp.int32)
    before = (position[:, None] < position[None, :]).astype(bf16)
    slot = jnp.einsum("set,tu->seu", named.astype(bf16), before, preferred_element_type=f32)
    return jnp.where(named, slot.astype(jnp.int32), -1)


def slabs_of(values):
    dp = lax.axis_size("dp")
    half = dp // 2
    me = lax.axis_index("dp")
    slab = values.shape[1] // dp
    got = []
    for dy in range(2):
        for dz in range(half):
            target = (me // 2 + dz) % half * 2 + (me % 2 ^ dy)
            part = lax.dynamic_slice_in_dim(values, target * slab, slab, 1)
            if dy or dz:
                part = hop(
                    part,
                    lambda a, b, dy=dy, dz=dz: ((a // 2 + dz) % half * 2 + (a % 2 ^ dy), b),
                )
            got.append(part)
    return gather_tp(jnp.stack(got))


def per_device(
    hidden_in,
    cotangent,
    segment_ids,
    expert_ids,
    first_gain,
    query_weight,
    key_weight,
    value_weight,
    output_weight,
    query_gain,
    key_gain,
    second_gain,
    router_weight,
    gate_weight,
    up_weight,
    down_weight,
):
    data_size = lax.axis_size("dp")
    tensor_size = lax.axis_size("tp")
    half = data_size // 2
    seq_len, width = hidden_in.shape
    share = seq_len // tensor_size
    slab = width // data_size
    me_dp, me_tp = lax.axis_index("dp"), lax.axis_index("tp")
    own = lambda values: lax.dynamic_slice_in_dim(values, me_tp * share, share, 0)
    local_experts = E // data_size
    first_expert = (me_dp * local_experts).astype(jnp.int32).reshape(1)
    places = jnp.concatenate([owner(jnp.arange(data_size, dtype=jnp.int32)), me_tp[None]]).astype(
        jnp.int32
    )

    hidden_own, cot_own = own(hidden_in), own(cotangent)
    small = jnp.concatenate(
        [
            router_weight.T.reshape(-1),
            first_gain,
            second_gain,
            query_gain.reshape(-1),
            key_gain.reshape(-1),
        ]
    )
    small = absolute_dp(gather_dp(small))
    cot_pieces = gather_all(cot_own.astype(bf16))
    query_pieces = gather_dp(after(query_weight, cot_pieces[1][0]))
    key_pieces = gather_dp(after(key_weight, query_pieces[1]))
    value_pieces = gather_dp(after(value_weight, key_pieces[1]))
    output_pieces = gather_dp(after(output_weight, value_pieces[1]))
    cut = slab * E
    router = jnp.swapaxes(small[:, :cut].reshape(data_size, E, slab), 0, 1).reshape(E, width)
    router = jnp.concatenate([router, router])
    gain_one = small[:, cut : cut + slab].reshape(1, width).astype(f32)
    gain_two = small[:, cut + slab : cut + 2 * slab].reshape(1, width).astype(f32)
    heads_local = query_gain.shape[0]
    piece = query_gain.size
    cut = cut + 2 * slab
    spread = lambda v: jnp.swapaxes(v.reshape(data_size, heads_local, -1), 0, 1).reshape(-1).astype(f32)
    gains = jnp.stack(
        [spread(small[:, cut : cut + piece]), spread(small[:, cut + piece : cut + 2 * piece])]
    )

    table = slot_tables(expert_ids, local_experts)
    tables = rope_tables(seq_len, HD)
    bias = score_bias(segment_ids[0])

    halves = []
    for pick in (slice(0, half), slice(half, None)):
        cot_rows = rows_of_slots(cot_pieces[pick], table[pick])
        halves.append((pick, cot_rows, grad_of_hidden(cot_rows, down_weight)))

    first_scale = lax.rsqrt(jnp.mean(hidden_in * hidden_in, axis=-1, keepdims=True) + epsilon)
    normed_one = (hidden_in * first_scale * gain_one).astype(bf16)
    x_slabs = jnp.swapaxes(normed_one.reshape(seq_len, data_size, slab), 0, 1)
    (queries,) = project(x_slabs, query_pieces, places, f32)
    key_proj, squares = project(x_slabs, key_pieces, places, f32, queries)
    (values,) = project(x_slabs, value_pieces, places, bf16)
    squares = reduce_tp(squares)
    q_rot, k_rot, logs, attended, *parts = attend(
        queries, key_proj, squares, values, gains, tables, bias, output_pieces, places
    )
    middle, x_piece, probs = route(scatter_tp(parts), hidden_own, gain_two, router)

    x_pieces = gather_all(after(x_piece, halves[0][2], halves[1][2]))
    attended_pieces = gather_dp(after(attended, x_pieces[-1][0]))
    one_slabs = slabs_of(after(own(normed_one), x_pieces[-1][0]))
    near, saved, crossed = [], [], []
    for pick, cot_rows, hidden_grad in halves:
        x_rows = rows_of_slots(x_pieces[pick], table[pick])
        back_rows, act, gate_grad, up_grad = expert_step(
            x_rows, gate_weight, up_weight, hidden_grad, first_expert
        )
        saved.append((x_rows, cot_rows, act, gate_grad, up_grad))
        total, crossing = scatter_near(tokens_of_slots(back_rows, table[pick]))
        near.append(total)
        crossed.append(crossing)
    saved = [list(arrays) for arrays in zip(*saved)]
    outs = [expert_out(after(act, crossed[1]), down_weight) for act in saved[2]]
    sums = [
        tokens_of_slots(rows, table[pick]) for rows, (pick, _, _) in zip(outs, halves, strict=True)
    ]
    back = scatter_line(*near, [outs[:1], outs[1:], sums[0], sums[1]])

    grad_middle, grad_low, router_sum, gain_sum = route_back(
        back, middle, x_piece, probs, cot_own, gain_two, router
    )
    low_pieces = gather_tp(grad_low)
    grad_gate = expert_weight_grad([after(v, grad_low) for v in saved[0]], saved[3], "grad_gate")
    grad_values, gq, gk, inner, gain_sums = attend_back(
        [after(low_pieces[0], grad_gate)] + low_pieces[1:], output_pieces, places, q_rot, k_rot, values, logs, queries,
        key_proj, squares, gains, tables, bias,
    )
    value_grads = gather_dp(grad_values)
    inner = reduce_tp(inner)
    grad_queries, grad_keys = norm_back(gq, gk, queries, key_proj, squares, inner)
    query_grads = gather_dp(after(grad_queries, value_grads[1]))
    key_grads = gather_dp(after(grad_keys, query_grads[1]))
    parts = project_back(
        [grad_queries, grad_keys, grad_values], [query_pieces, key_pieces, value_pieces], places
    )
    grad_hidden, first_sum = hidden_back(scatter_tp(parts), hidden_own, grad_middle, gain_one)
    grad_hidden = absolute_tp(gather_tp(grad_hidden))

    moe_near = [scatter_near(part, (inner,))[0] for part in sums]
    moe = scatter_line(*moe_near)
    hidden_out = absolute_tp(gather_tp(middle + added(*moe)))
    token_sums = jnp.concatenate([router_sum[:E], gain_sum, first_sum])
    token_sums = reduce_tp(reduce_dp(token_sums))
    middle_slabs = slabs_of(after(grad_low, inner))
    head_sums = reduce_dp(gain_sums.reshape(2 * heads_local, HD))
    grad_up = expert_weight_grad([after(v, parts[0]) for v in saved[0]], saved[4], "grad_up")
    grad_down = expert_weight_grad([after(v, parts[0]) for v in saved[2]], saved[1], "grad_down")
    grad_output = token_product(middle_slabs, attended_pieces, places, False)
    grad_value = token_product(one_slabs, value_grads, places, True)
    grad_query = token_product(one_slabs, query_grads, places, True)
    grad_key = token_product(one_slabs, key_grads, places, True)
    return (
        hidden_out,
        grad_hidden,
        token_sums[E + 1],
        grad_query,
        grad_key,
        grad_value,
        grad_output,
        head_sums[:heads_local],
        head_sums[heads_local:],
        token_sums[E],
        token_sums[:E].T,
        grad_gate,
        grad_up,
        grad_down,
    )


def solution(mesh):
    return jax.shard_map(
        per_device,
        mesh=mesh,
        in_specs=(
            P("dp", None),
            P("dp", None),
            P("dp", None),
            P("dp", None),
            P("dp"),
            P("dp", "tp"),
            P("dp", "tp"),
            P("dp", "tp"),
            P("tp", "dp"),
            P("tp", "dp"),
            P("tp", "dp"),
            P("dp"),
            P("dp", None),
            P("dp", None, "tp"),
            P("dp", None, "tp"),
            P("dp", "tp", None),
        ),
        out_specs=(
            P("dp", None),
            P("dp", None),
            P("dp"),
            P("dp", "tp"),
            P("dp", "tp"),
            P("dp", "tp"),
            P("tp", "dp"),
            P("tp", "dp"),
            P("tp", "dp"),
            P("dp"),
            P("dp", None),
            P("dp", None, "tp"),
            P("dp", None, "tp"),
            P("dp", "tp", None),
        ),
        check_vma=False,
    )
```

time: 904 us -> 742 us (0.82)
  waiting for transfers between devices: 413 us -> 275 us
  Pallas kernels: 112 us -> 185 us
  local copies, waits for them, and re-layouts: 117 us -> 65.3 us
  starting transfers between devices: 147 us -> 171 us
  matrix products: 24.2 us -> 0.79 us
  other arithmetic: 50 us -> 31.3 us
  between operations: 16.5 us -> 3.56 us
  blocking collectives: 12.8 us -> 0 us
    ppermute x181 -> x201, waiting for transfers between devices: 339 us -> 275 us  [hop(): return lax.ppermute(values, ('dp', 'tp'), pairs)]
    unnamed x4 -> x0, waiting for transfers between devices: 48.3 us -> none
    pallas_call x4 -> x9, Pallas kernels: 72.1 us -> 112 us  [per_expert(): pl.pallas_call(kernel, grid=(experts,), in_specs=in_specs, out_specs=[who...]
    pallas_call x0 -> x14, Pallas kernels: none -> 29.5 us  [kernel_call(): pl.pallas_call(kernel, in_specs=[pl.BlockSpec(memory_space=pltpu.SMEM)] *...]
    unnamed x363 -> x367, local copies, waits for them, and re-layouts: 69.1 us -> 42.4 us
    psum x1 -> x0, waiting for transfers between devices: 25.8 us -> none  [per_device(): tokenwise = lax.psum(tokenwise, 'tp')]
    ppermute x181 -> x201, starting transfers between devices: 147 us -> 171 us  [hop(): return lax.ppermute(values, ('dp', 'tp'), pairs)]
    dot_general x21 -> x0, matrix products: 24 us -> none  [the longest x4 6.11 us: dot_first(): lax.dot_general(a, b, (((0,), (0,)), ((), ())), preferred_element_type=f32)]
  transfers between devices with their start and end apart: 184 -> 201, of which waited for: 81 -> 63; matrix products, arithmetic and copies ran while one was open for 19% -> 7% of each run, Pallas kernels for 13% -> 25%
where the time goes in v2:
time: 742 us; the launch traced here: 732 us
  waiting for transfers between devices  275 us (37%)
  Pallas kernels  185 us (25%)
  starting transfers between devices  171 us (23%)
  local copies, waits for them, and re-layouts  65.3 us (9%)
  other arithmetic  31.3 us (4%)
    ppermute x201, waiting for transfers between devices, hop(): return lax.ppermute(values, ('dp', 'tp'), pairs)  275 us
    ppermute x201, starting transfers between devices, hop(): return lax.ppermute(values, ('dp', 'tp'), pairs)  171 us
    pallas_call x9, Pallas kernels, per_expert(): pl.pallas_call(kernel, grid=(experts,), in_specs=in_specs, out_specs=[who...  112 us
    unnamed x367, local copies, waits for them, and re-layouts  42.4 us
    pallas_call x14, Pallas kernels, kernel_call(): pl.pallas_call(kernel, in_specs=[pl.BlockSpec(memory_space=pltpu.SMEM)] *...  29.5 us
    pallas_call x4, Pallas kernels, tokens_of_slots(): pl.pallas_call(kernel, grid=(sequences,), in_specs=[pl.BlockSpec((1, expe...  23.2 us
    pallas_call x4, Pallas kernels, rows_of_slots(): pl.pallas_call(kernel, grid=(sequences,), in_specs=[pl.BlockSpec((1, expe...  19.8 us
  transfers between devices with their start and end apart: 201, of which 63 were waited for; matrix products, arithmetic and copies ran while one was open for 7% of the time, Pallas kernels for 25%

profile of v2, /device:TPU:0, one launch (start us, length us, event | category | flops | bytes accessed | tf_op | source)
XLA Modules:
  0.0 731.5 jit_solution(13704234704548461751)
XLA Ops:
  198.2 9.0 %grad_of_hidden.2.grad_ref = f32[8,192,256]{2,1,0:T(8,128)S(1)} custom-call(bf16[8,192,2048]{2,1,0:T(8,128)(2,1)} %rows_of_slots.4.cot_ref.c_ref, bf16[8,256,2048]{2,1,0:T(8,128)(2,1)} %down_ref.7), custom_call_target="tpu_custom_call" | custom-call | flops 1610612736 | bytes 16252928 | tf_op jit(solution)/shard_map/grad_of_hidden/pallas_call | solution.py:253
  216.2 8.9 %grad_of_hidden.3.grad_ref = f32[8,192,256]{2,1,0:T(8,128)S(1)} custom-call(bf16[8,192,2048]{2,1,0:T(8,128)(2,1)} %rows_of_slots.5.cot_ref.d_ref, bf16[8,256,2048]{2,1,0:T(8,128)(2,1)} %down_ref.7), custom_call_target="tpu_custom_call" | custom-call | flops 1610612736 | bytes 16252928 | tf_op jit(solution)/shard_map/grad_of_hidden/pallas_call | solution.py:253
  228.6 9.2 %collective-permute-done.81.refs_4_ = bf16[64,2176]{1,0:T(8,128)(2,1)S(1)} collective-permute-done((bf16[64,2176]{1,0:T(8,128)(2,1)S(1)}, bf16[64,2176]{1,0:T(8,128)(2,1)S(1)}, u32[]{:S(2)}, u32[]{:S(2)}) %collective-permute-start.81) | collective-permute-done | bytes 278560 | tf_op jit(solution)/shard_map/ppermute | solution.py:30
  239.9 7.9 %collective-permute-done.85.refs_8_ = bf16[64,2176]{1,0:T(8,128)(2,1)S(1)} collective-permute-done((bf16[64,2176]{1,0:T(8,128)(2,1)S(1)}, bf16[64,2176]{1,0:T(8,128)(2,1)S(1)}, u32[]{:S(2)}, u32[]{:S(2)}) %collective-permute-start.85) | collective-permute-done | bytes 278560 | tf_op jit(solution)/shard_map/ppermute | solution.py:30
  251.3 5.9 collective-permute-done.89.refs_12_
  279.9 5.2 rows_of_slots.7.x_ref.b_ref
  286.2 5.4 collective-permute-done.87.refs_10_
  291.6 5.6 collective-permute-done.91.refs_14_
  297.2 16.3 %expert_step.3 = (bf16[8,192,2176]{2,1,0:T(8,128)(2,1)}, bf16[8,192,256]{2,1,0:T(8,128)(2,1)S(1)}, bf16[8,192,256]{2,1,0:T(8,128)(2,1)S(1)}, bf16[8,192,256]{2,1,0:T(8,128)(2,1)S(1)}) custom-call(s32[1]{0:T(128)} %bitcast.22.base_ref, bf16[8,192,2176]{2,1,0:T(8,128)(2,1)} %rows_of_slots.7.x_ref.b_ref, bf16[8,2048,256]{2,1,0:T(8,128)(2,1)} %gate_ref.3, ...), custom_call_target="tpu_custom_call" | custom-call | flops 6442450944 | bytes 34078720 | tf_op jit(solution)/shard_map/expert_step/pallas_call | solution.py:253
  314.4 5.7 tokens_of_slots.4
  320.8 5.2 rows_of_slots.6.x_ref.a_ref
  326.0 16.3 %expert_step.2 = (bf16[8,192,2176]{2,1,0:T(8,128)(2,1)}, bf16[8,192,256]{2,1,0:T(8,128)(2,1)S(1)}, bf16[8,192,256]{2,1,0:T(8,128)(2,1)S(1)}, bf16[8,192,256]{2,1,0:T(8,128)(2,1)S(1)}) custom-call(s32[1]{0:T(128)} %bitcast.22.base_ref, bf16[8,192,2176]{2,1,0:T(8,128)(2,1)} %rows_of_slots.6.x_ref.a_ref, bf16[8,2048,256]{2,1,0:T(8,128)(2,1)} %gate_ref.3, ...), custom_call_target="tpu_custom_call" | custom-call | flops 6442450944 | bytes 34078720 | tf_op jit(solution)/shard_map/expert_step/pallas_call | solution.py:253
  344.1 6.2 tokens_of_slots.6
  355.7 9.4 %expert_out.2.rows_ref = bf16[8,192,2048]{2,1,0:T(8,128)(2,1)} custom-call(bf16[8,192,256]{2,1,0:T(8,128)(2,1)S(1)} %get-tuple-element.170.act_ref.a_ref, bf16[8,256,2048]{2,1,0:T(8,128)(2,1)} %down_ref.7), custom_call_target="tpu_custom_call" | custom-call | flops 1610612736 | bytes 15466496 | tf_op jit(solution)/shard_map/expert_out/pallas_call | solution.py:253
  365.1 14.7 %collective-permute-done.114 = bf16[256,2176]{1,0:T(8,128)(2,1)S(1)} collective-permute-done((bf16[256,2176]{1,0:T(8,128)(2,1)S(1)}, bf16[256,2176]{1,0:T(8,128)(2,1)S(1)}, u32[]{:S(2)}, u32[]{:S(2)}) %collective-permute-start.114) | collective-permute-done | bytes 1114144 | tf_op jit(solution)/shard_map/ppermute | solution.py:30
  384.3 9.5 %expert_out.3.rows_ref = bf16[8,192,2048]{2,1,0:T(8,128)(2,1)} custom-call(bf16[8,192,256]{2,1,0:T(8,128)(2,1)S(1)} %get-tuple-element.171.act_ref.b_ref, bf16[8,256,2048]{2,1,0:T(8,128)(2,1)} %down_ref.7), custom_call_target="tpu_custom_call" | custom-call | flops 1610612736 | bytes 15466496 | tf_op jit(solution)/shard_map/expert_out/pallas_call | solution.py:253
  393.8 9.1 %collective-permute-done.112 = bf16[256,2176]{1,0:T(8,128)(2,1)} collective-permute-done((bf16[256,2176]{1,0:T(8,128)(2,1)}, bf16[256,2176]{1,0:T(8,128)(2,1)}, u32[]{:S(2)}, u32[]{:S(2)}) %collective-permute-start.112) | collective-permute-done | bytes 1114144 | tf_op jit(solution)/shard_map/ppermute | solution.py:30
  418.6 5.2 tokens_of_slots.5
  425.8 5.8 collective-permute-done.149
  434.9 6.0 tokens_of_slots.7
  449.3 5.1 collective-permute-done.118.b_ref
  464.0 14.4 %grad_gate.1 = f32[8,2048,256]{2,1,0:T(8,128)} custom-call(bf16[8,192,2176]{2,1,0:T(8,128)(2,1)} %rows_of_slots.6.x_ref.a_ref, bf16[8,192,2176]{2,1,0:T(8,128)(2,1)} %rows_of_slots.7.x_ref.b_ref, bf16[8,192,256]{2,1,0:T(8,128)(2,1)S(1)} %copy-done.108, bf16[8,192,256]{2,1,0:T(8,128)(2,1)S(1)} %copy-done.106), custom_call_target="tpu_custom_call" | custom-call | flops 3221225472 | bytes 30932992 | tf_op jit(solution)/shard_map/grad_gate/pallas_call | solution.py:253
  478.5 5.6 attend_back.1
  506.0 20.5 %collective-permute-done.123 = f32[256,128]{1,0:T(8,128)S(1)} collective-permute-done((f32[256,128]{1,0:T(8,128)S(1)}, f32[256,128]{1,0:T(8,128)S(1)}, u32[]{:S(2)}, u32[]{:S(2)}) %collective-permute-start.123) | collective-permute-done | bytes 131104 | tf_op jit(solution)/shard_map/ppermute | solution.py:30
  542.6 7.0 collective-permute-done.139.c_ref
  556.4 29.2 %collective-permute-done.143 = f32[4,66,256]{2,1,0:T(8,128)S(1)} collective-permute-done((f32[4,66,256]{2,1,0:T(8,128)S(1)}, f32[4,66,256]{2,1,0:T(8,128)S(1)}, u32[]{:S(2)}, u32[]{:S(2)}) %collective-permute-start.143) | collective-permute-done | bytes 270368 | tf_op jit(solution)/shard_map/ppermute | solution.py:30
  600.9 7.2 collective-permute-done.191.refs_6_
  654.5 5.7 collective-permute-done.161.refs_6_
  664.9 6.5 collective-permute-done.175.refs_7_
  677.8 14.1 %grad_down.1 = f32[8,256,2048]{2,1,0:T(8,128)} custom-call(bf16[8,192,256]{2,1,0:T(8,128)(2,1)S(1)} %get-tuple-element.170.act_ref.a_ref, bf16[8,192,256]{2,1,0:T(8,128)(2,1)S(1)} %get-tuple-element.171.act_ref.b_ref, bf16[8,192,2048]{2,1,0:T(8,128)(2,1)} %rows_of_slots.4.cot_ref.c_ref, bf16[8,192,2048]{2,1,0:T(8,128)(2,1)} %rows_of_slots.5.cot_ref.d_ref), custom_call_target="tpu_custom_call" | custom-call | flops 3221225472 | bytes 30932992 | tf_op jit(solution)/shard_map/grad_down/pallas_call | solution.py:253
  694.1 14.2 %grad_up.1 = f32[8,2048,256]{2,1,0:T(8,128)} custom-call(bf16[8,192,2176]{2,1,0:T(8,128)(2,1)} %rows_of_slots.6.x_ref.a_ref, bf16[8,192,2176]{2,1,0:T(8,128)(2,1)} %rows_of_slots.7.x_ref.b_ref, bf16[8,192,256]{2,1,0:T(8,128)(2,1)S(1)} %copy-done.104, bf16[8,192,256]{2,1,0:T(8,128)(2,1)S(1)} %copy-done.102), custom_call_target="tpu_custom_call" | custom-call | flops 3221225472 | bytes 30932992 | tf_op jit(solution)/shard_map/grad_up/pallas_call | solution.py:253
  718.6 6.5 collective-permute-done.173.refs_11_
  (869 shorter events, 425.5 us)
Async XLA Ops:
  113.7 24.4 %collective-permute-start.60 = (bf16[64,2048]{1,0:T(8,128)(2,1)}, bf16[64,2048]{1,0:T(8,128)(2,1)}, u32[]{:S(2)}, u32[]{:S(2)}) collective-permute-start(bf16[64,2048]{1,0:T(8,128)(2,1)} %collective-permute-done.58.refs_12_), channel_id=1, source_target_pairs={{0,2},{1,3},{2,0},{3,1},{4,6},{5,7},{6,4},{7,5},{8,10},{9,11},{10,... | collective-permute-start | bytes 786440 | tf_op jit(solution)/shard_map/ppermute | solution.py:30
  115.2 24.0 %collective-permute-start.34 = (bf16[512,256]{1,0:T(8,128)(2,1)}, bf16[512,256]{1,0:T(8,128)(2,1)S(1)}, u32[]{:S(2)}, u32[]{:S(2)}) collective-permute-start(bf16[512,256]{1,0:T(8,128)(2,1)} %refs_4_), channel_id=1, source_target_pairs={{0,4},{1,5},{2,6},{3,7},{4,0},{5,1},{6,2},{7,3},{8,12},{9,13},{10,... | collective-permute-start | bytes 786440 | tf_op jit(solution)/shard_map/ppermute | solution.py:30
  152.3 37.2 %collective-permute-start.53 = (bf16[64,2048]{1,0:T(8,128)(2,1)}, bf16[64,2048]{1,0:T(8,128)(2,1)}, u32[]{:S(2)}, u32[]{:S(2)}) collective-permute-start(bf16[64,2048]{1,0:T(8,128)(2,1)} %collective-permute-done.52.refs_6_), channel_id=1, source_target_pairs={{0,1},{1,0},{2,3},{3,2},{4,5},{5,4},{6,7},{7,6},{8,9},{9,8},{10,11... | collective-permute-start | bytes 786440 | tf_op jit(solution)/shard_map/ppermute | solution.py:30
  157.9 33.0 %collective-permute-start.74 = (bf16[64,2048]{1,0:T(8,128)(2,1)}, bf16[64,2048]{1,0:T(8,128)(2,1)}, u32[]{:S(2)}, u32[]{:S(2)}) collective-permute-start(bf16[64,2048]{1,0:T(8,128)(2,1)} %collective-permute-done.58.refs_12_), channel_id=1, source_target_pairs={{0,4},{1,5},{2,6},{3,7},{4,0},{5,1},{6,2},{7,3},{8,12},{9,13},{10,... | collective-permute-start | bytes 786440 | tf_op jit(solution)/shard_map/ppermute | solution.py:30
  163.5 27.6 %collective-permute-start.59 = (bf16[64,2048]{1,0:T(8,128)(2,1)}, bf16[64,2048]{1,0:T(8,128)(2,1)}, u32[]{:S(2)}, u32[]{:S(2)}) collective-permute-start(bf16[64,2048]{1,0:T(8,128)(2,1)} %collective-permute-done.58.refs_12_), channel_id=1, source_target_pairs={{0,1},{1,0},{2,3},{3,2},{4,5},{5,4},{6,7},{7,6},{8,9},{9,8},{10,11... | collective-permute-start | bytes 786440 | tf_op jit(solution)/shard_map/ppermute | solution.py:30
  163.6 28.1 %collective-permute-start.57 = (bf16[64,2048]{1,0:T(8,128)(2,1)}, bf16[64,2048]{1,0:T(8,128)(2,1)}, u32[]{:S(2)}, u32[]{:S(2)}) collective-permute-start(bf16[64,2048]{1,0:T(8,128)(2,1)} %collective-permute-done.56.refs_10_), channel_id=1, source_target_pairs={{0,1},{1,0},{2,3},{3,2},{4,5},{5,4},{6,7},{7,6},{8,9},{9,8},{10,11... | collective-permute-start | bytes 786440 | tf_op jit(solution)/shard_map/ppermute | solution.py:30
  169.1 24.1 %collective-permute-start.61 = (bf16[64,2048]{1,0:T(8,128)(2,1)}, bf16[64,2048]{1,0:T(8,128)(2,1)}, u32[]{:S(2)}, u32[]{:S(2)}) collective-permute-start(bf16[64,2048]{1,0:T(8,128)(2,1)} %collective-permute-done.60.refs_14_), channel_id=1, source_target_pairs={{0,1},{1,0},{2,3},{3,2},{4,5},{5,4},{6,7},{7,6},{8,9},{9,8},{10,11... | collective-permute-start | bytes 786440 | tf_op jit(solution)/shard_map/ppermute | solution.py:30
  285.7 34.5 %collective-permute-start.86 = (bf16[64,2176]{1,0:T(8,128)(2,1)S(1)}, bf16[64,2176]{1,0:T(8,128)(2,1)S(1)}, u32[]{:S(2)}, u32[]{:S(2)}) collective-permute-start(bf16[64,2176]{1,0:T(8,128)(2,1)S(1)} %collective-permute-done.85.refs_8_), channel_id=1, source_target_pairs={{0,1},{1,0},{2,3},{3,2},{4,5},{5,4},{6,7},{7,6},{8,9},{9,8},{10,11... | collective-permute-start | bytes 835592 | tf_op jit(solution)/shard_map/ppermute | solution.py:30
  285.7 35.1 %collective-permute-start.84 = (bf16[64,2176]{1,0:T(8,128)(2,1)S(1)}, bf16[64,2176]{1,0:T(8,128)(2,1)S(1)}, u32[]{:S(2)}, u32[]{:S(2)}) collective-permute-start(bf16[64,2176]{1,0:T(8,128)(2,1)S(1)} %collective-permute-done.83.refs_6_), channel_id=1, source_target_pairs={{0,1},{1,0},{2,3},{3,2},{4,5},{5,4},{6,7},{7,6},{8,9},{9,8},{10,11... | collective-permute-start | bytes 835592 | tf_op jit(solution)/shard_map/ppermute | solution.py:30
  286.2 34.6 %collective-permute-start.90 = (bf16[64,2176]{1,0:T(8,128)(2,1)S(1)}, bf16[64,2176]{1,0:T(8,128)(2,1)S(1)}, u32[]{:S(2)}, u32[]{:S(2)}) collective-permute-start(bf16[64,2176]{1,0:T(8,128)(2,1)S(1)} %collective-permute-done.89.refs_12_), channel_id=1, source_target_pairs={{0,1},{1,0},{2,3},{3,2},{4,5},{5,4},{6,7},{7,6},{8,9},{9,8},{10,11... | collective-permute-start | bytes 835592 | tf_op jit(solution)/shard_map/ppermute | solution.py:30
  291.6 29.1 %collective-permute-start.88 = (bf16[64,2176]{1,0:T(8,128)(2,1)S(1)}, bf16[64,2176]{1,0:T(8,128)(2,1)S(1)}, u32[]{:S(2)}, u32[]{:S(2)}) collective-permute-start(bf16[64,2176]{1,0:T(8,128)(2,1)S(1)} %collective-permute-done.87.refs_10_), channel_id=1, source_target_pairs={{0,1},{1,0},{2,3},{3,2},{4,5},{5,4},{6,7},{7,6},{8,9},{9,8},{10,11... | collective-permute-start | bytes 835592 | tf_op jit(solution)/shard_map/ppermute | solution.py:30
  297.2 23.5 %collective-permute-start.92 = (bf16[64,2176]{1,0:T(8,128)(2,1)S(1)}, bf16[64,2176]{1,0:T(8,128)(2,1)S(1)}, u32[]{:S(2)}, u32[]{:S(2)}) collective-permute-start(bf16[64,2176]{1,0:T(8,128)(2,1)S(1)} %collective-permute-done.91.refs_14_), channel_id=1, source_target_pairs={{0,1},{1,0},{2,3},{3,2},{4,5},{5,4},{6,7},{7,6},{8,9},{9,8},{10,11... | collective-permute-start | bytes 835592 | tf_op jit(solution)/shard_map/ppermute | solution.py:30
  320.2 30.7 %collective-permute-start.109 = (bf16[256,2176]{1,0:T(8,128)(2,1)S(1)}, bf16[256,2176]{1,0:T(8,128)(2,1)}, u32[]{:S(2)}, u32[]{:S(2)}) collective-permute-start(bf16[256,2176]{1,0:T(8,128)(2,1)S(1)} %get-tuple-element.109), channel_id=1, source_target_pairs={{0,1},{1,0},{2,3},{3,2},{4,5},{5,4},{6,7},{7,6},{8,9},{9,8},{10,11... | collective-permute-start | bytes 3342344 | tf_op jit(solution)/shard_map/ppermute | solution.py:30
  352.3 27.5 %collective-permute-start.114 = (bf16[256,2176]{1,0:T(8,128)(2,1)S(1)}, bf16[256,2176]{1,0:T(8,128)(2,1)S(1)}, u32[]{:S(2)}, u32[]{:S(2)}) collective-permute-start(bf16[256,2176]{1,0:T(8,128)(2,1)S(1)} %add_convert_fusion.2), channel_id=1, source_target_pairs={{0,2},{1,3},{2,0},{3,1},{4,6},{5,7},{6,4},{7,5},{8,10},{9,11},{10,... | collective-permute-start | bytes 3342344 | tf_op jit(solution)/shard_map/ppermute | solution.py:30
  353.5 40.3 %collective-permute-start.110 = (bf16[256,2176]{1,0:T(8,128)(2,1)}, bf16[256,2176]{1,0:T(8,128)(2,1)}, u32[]{:S(2)}, u32[]{:S(2)}) collective-permute-start(bf16[256,2176]{1,0:T(8,128)(2,1)} %get-tuple-element.115), channel_id=1, source_target_pairs={{0,1},{1,0},{2,3},{3,2},{4,5},{5,4},{6,7},{7,6},{8,9},{9,8},{10,11... | collective-permute-start | bytes 3342344 | tf_op jit(solution)/shard_map/ppermute | solution.py:30
  354.8 48.1 %collective-permute-start.112 = (bf16[256,2176]{1,0:T(8,128)(2,1)}, bf16[256,2176]{1,0:T(8,128)(2,1)}, u32[]{:S(2)}, u32[]{:S(2)}) collective-permute-start(bf16[256,2176]{1,0:T(8,128)(2,1)} %add_convert_fusion.1), channel_id=1, source_target_pairs={{0,2},{1,3},{2,0},{3,1},{4,6},{5,7},{6,4},{7,5},{8,10},{9,11},{10,... | collective-permute-start | bytes 3342344 | tf_op jit(solution)/shard_map/ppermute | solution.py:30
  381.2 25.1 %collective-permute-start.115 = (bf16[256,2176]{1,0:T(8,128)(2,1)}, bf16[256,2176]{1,0:T(8,128)(2,1)}, u32[]{:S(2)}, u32[]{:S(2)}) collective-permute-start(bf16[256,2176]{1,0:T(8,128)(2,1)} %add_convert_fusion), channel_id=1, source_target_pairs={{0,4},{1,5},{2,6},{3,7},{4,0},{5,1},{6,2},{7,3},{8,12},{9,13},{10,... | collective-permute-start | bytes 3342344 | tf_op jit(solution)/shard_map/ppermute | solution.py:30
  413.2 79.9 %collective-permute-start.155 = (bf16[64,256]{1,0:T(8,128)(2,1)}, bf16[64,256]{1,0:T(8,128)(2,1)}, u32[]{:S(2)}, u32[]{:S(2)}) collective-permute-start(bf16[64,256]{1,0:T(8,128)(2,1)} %get-tuple-element.206), channel_id=1, source_target_pairs={{0,28},{1,29},{2,30},{3,31},{4,24},{5,25},{6,26},{7,27},{8,4},{9,5... | collective-permute-start | bytes 98312 | tf_op jit(solution)/shard_map/ppermute | solution.py:30
  413.4 75.0 %collective-permute-start.154 = (bf16[64,256]{1,0:T(8,128)(2,1)}, bf16[64,256]{1,0:T(8,128)(2,1)}, u32[]{:S(2)}, u32[]{:S(2)}) collective-permute-start(bf16[64,256]{1,0:T(8,128)(2,1)} %get-tuple-element.207), channel_id=1, source_target_pairs={{0,20},{1,21},{2,22},{3,23},{4,16},{5,17},{6,18},{7,19},{8,28},{9,... | collective-permute-start | bytes 98312 | tf_op jit(solution)/shard_map/ppermute | solution.py:30
  413.9 44.7 %collective-permute-start.153 = (bf16[64,256]{1,0:T(8,128)(2,1)S(1)}, bf16[64,256]{1,0:T(8,128)(2,1)S(1)}, u32[]{:S(2)}, u32[]{:S(2)}) collective-permute-start(bf16[64,256]{1,0:T(8,128)(2,1)S(1)} %get-tuple-element.208), channel_id=1, source_target_pairs={{0,12},{1,13},{2,14},{3,15},{4,8},{5,9},{6,10},{7,11},{8,20},{9,21... | collective-permute-start | bytes 98312 | tf_op jit(solution)/shard_map/ppermute | solution.py:30
  416.2 31.9 %collective-permute-start.151 = (bf16[64,256]{1,0:T(8,128)(2,1)S(1)}, bf16[64,256]{1,0:T(8,128)(2,1)S(1)}, u32[]{:S(2)}, u32[]{:S(2)}) collective-permute-start(bf16[64,256]{1,0:T(8,128)(2,1)S(1)} %get-tuple-element.210), channel_id=1, source_target_pairs={{0,24},{1,25},{2,26},{3,27},{4,28},{5,29},{6,30},{7,31},{8,0},{9,1... | collective-permute-start | bytes 98312 | tf_op jit(solution)/shard_map/ppermute | solution.py:30
  458.6 40.0 %collective-permute-start.128 = (bf16[256,2048]{1,0:T(8,128)(2,1)}, bf16[256,2048]{1,0:T(8,128)(2,1)}, u32[]{:S(2)}, u32[]{:S(2)}) collective-permute-start(bf16[256,2048]{1,0:T(8,128)(2,1)} %get-tuple-element.130), channel_id=1, source_target_pairs={{0,1},{1,0},{2,3},{3,2},{4,5},{5,4},{6,7},{7,6},{8,9},{9,8},{10,11... | collective-permute-start | bytes 3145736 | tf_op jit(solution)/shard_map/ppermute | solution.py:30
  500.6 50.7 %collective-permute-start.129 = (bf16[256,2048]{1,0:T(8,128)(2,1)S(1)}, bf16[256,2048]{1,0:T(8,128)(2,1)S(1)}, u32[]{:S(2)}, u32[]{:S(2)}) collective-permute-start(bf16[256,2048]{1,0:T(8,128)(2,1)S(1)} %add_convert_fusion.4), channel_id=1, source_target_pairs={{0,2},{1,3},{2,0},{3,1},{4,6},{5,7},{6,4},{7,5},{8,10},{9,11},{10,... | collective-permute-start | bytes 3145736 | tf_op jit(solution)/shard_map/ppermute | solution.py:30
  504.7 30.8 %collective-permute-start.159 = (bf16[256,512]{1,0:T(8,128)(2,1)S(1)}, bf16[256,512]{1,0:T(8,128)(2,1)S(1)}, u32[]{:S(2)}, u32[]{:S(2)}) collective-permute-start(bf16[256,512]{1,0:T(8,128)(2,1)S(1)} %copy-done.68), channel_id=1, source_target_pairs={{0,8},{1,9},{2,10},{3,11},{4,12},{5,13},{6,14},{7,15},{8,16},{9,17... | collective-permute-start | bytes 786440 | tf_op jit(solution)/shard_map/ppermute | solution.py:30
  541.4 44.2 %collective-permute-start.126 = (bf16[256,2048]{1,0:T(8,128)(2,1)S(1)}, bf16[256,2048]{1,0:T(8,128)(2,1)}, u32[]{:S(2)}, u32[]{:S(2)}) collective-permute-start(bf16[256,2048]{1,0:T(8,128)(2,1)S(1)} %add_convert_fusion.5), channel_id=1, source_target_pairs={{0,2},{1,3},{2,0},{3,1},{4,6},{5,7},{6,4},{7,5},{8,10},{9,11},{10,... | collective-permute-start | bytes 3145736 | tf_op jit(solution)/shard_map/ppermute | solution.py:30
  551.3 35.5 %collective-permute-start.124 = (bf16[256,2048]{1,0:T(8,128)(2,1)S(1)}, bf16[256,2048]{1,0:T(8,128)(2,1)S(1)}, u32[]{:S(2)}, u32[]{:S(2)}) collective-permute-start(bf16[256,2048]{1,0:T(8,128)(2,1)S(1)} %copy-done.157), channel_id=1, source_target_pairs={{0,1},{1,0},{2,3},{3,2},{4,5},{5,4},{6,7},{7,6},{8,9},{9,8},{10,11... | collective-permute-start | bytes 3145736 | tf_op jit(solution)/shard_map/ppermute | solution.py:30
  553.2 34.6 %collective-permute-start.130 = (bf16[256,2048]{1,0:T(8,128)(2,1)S(1)}, bf16[256,2048]{1,0:T(8,128)(2,1)S(1)}, u32[]{:S(2)}, u32[]{:S(2)}) collective-permute-start(bf16[256,2048]{1,0:T(8,128)(2,1)S(1)} %add_convert_fusion.3), channel_id=1, source_target_pairs={{0,4},{1,5},{2,6},{3,7},{4,0},{5,1},{6,2},{7,3},{8,12},{9,13},{10,... | collective-permute-start | bytes 3145736 | tf_op jit(solution)/shard_map/ppermute | solution.py:30
  554.2 31.3 %collective-permute-start.143 = (f32[4,66,256]{2,1,0:T(8,128)S(1)}, f32[4,66,256]{2,1,0:T(8,128)S(1)}, u32[]{:S(2)}, u32[]{:S(2)}) collective-permute-start(f32[4,66,256]{2,1,0:T(8,128)S(1)} %pad_maximum_fusion.3), channel_id=1, source_target_pairs={{0,4},{1,5},{2,6},{3,7},{4,0},{5,1},{6,2},{7,3},{8,12},{9,13},{10,... | collective-permute-start | bytes 811016 | tf_op jit(solution)/shard_map/ppermute | solution.py:30
  555.5 37.2 %collective-permute-start.193 = (bf16[256,512]{1,0:T(8,128)(2,1)S(1)}, bf16[256,512]{1,0:T(8,128)(2,1)S(1)}, u32[]{:S(2)}, u32[]{:S(2)}) collective-permute-start(bf16[256,512]{1,0:T(8,128)(2,1)S(1)} %copy-done.144), channel_id=1, source_target_pairs={{0,4},{1,5},{2,6},{3,7},{4,0},{5,1},{6,2},{7,3},{8,12},{9,13},{10,... | collective-permute-start | bytes 786440 | tf_op jit(solution)/shard_map/ppermute | solution.py:30
  671.4 42.3 %collective-permute-start.140 = (f32[64,2048]{1,0:T(8,128)S(1)}, f32[64,2048]{1,0:T(8,128)S(1)}, u32[]{:S(2)}, u32[]{:S(2)}) collective-permute-start(f32[64,2048]{1,0:T(8,128)S(1)} %get-tuple-element.155), channel_id=1, source_target_pairs={{0,2},{1,3},{2,0},{3,1},{4,6},{5,7},{6,4},{7,5},{8,10},{9,11},{10,... | collective-permute-start | bytes 1572872 | tf_op jit(solution)/shard_map/ppermute | solution.py:30
  676.7 37.5 %collective-permute-start.134 = (f32[64,2048]{1,0:T(8,128)S(1)}, f32[64,2048]{1,0:T(8,128)S(1)}, u32[]{:S(2)}, u32[]{:S(2)}) collective-permute-start(f32[64,2048]{1,0:T(8,128)S(1)} %fusion.5), channel_id=1, source_target_pairs={{0,2},{1,3},{2,0},{3,1},{4,6},{5,7},{6,4},{7,5},{8,10},{9,11},{10,... | collective-permute-start | bytes 1572872 | tf_op jit(solution)/shard_map/ppermute | solution.py:30
  692.6 24.3 %collective-permute-start.169 = (bf16[256,512]{1,0:T(8,128)(2,1)S(1)}, bf16[256,512]{1,0:T(8,128)(2,1)S(1)}, u32[]{:S(2)}, u32[]{:S(2)}) collective-permute-start(bf16[256,512]{1,0:T(8,128)(2,1)S(1)} %collective-permute-done.168.refs_6_), channel_id=1, source_target_pairs={{0,8},{1,9},{2,10},{3,11},{4,12},{5,13},{6,14},{7,15},{8,16},{9,17... | collective-permute-start | bytes 786440 | tf_op jit(solution)/shard_map/ppermute | solution.py:30
  (340 other events, 4182.9 us)

commit v3 on v2

v3 whole, which is shorter than its diff:
```python
import math

import jax
import jax.numpy as jnp
from jax import lax
from jax.experimental import pallas as pl
from jax.experimental.pallas import tpu as pltpu
from jax.sharding import PartitionSpec as P

D = 2048
HD = 128
E = 64
TOPK = 8
CAP = 48
EXTRA = 2 * E

bf16 = jnp.bfloat16
f32 = jnp.float32

epsilon = 1e-05


def cost(flops, bytes_accessed, transcendentals):
    return pl.CostEstimate(
        flops=flops // 1000000, bytes_accessed=bytes_accessed // 1000000, transcendentals=0
    )


def swap(values, dp_bits, tp_bits):
    dp, tp = lax.axis_size("dp"), lax.axis_size("tp")
    pairs = [
        (a * tp + b, (a ^ dp_bits) * tp + (b ^ tp_bits)) for a in range(dp) for b in range(tp)
    ]
    return lax.ppermute(values, ("dp", "tp"), pairs)


def over_z(values, bits):
    return swap(values, 2 * bits, 0)


def over_y(values):
    return swap(values, 1, 0)


def over_x(values):
    return swap(values, 0, 2)


def over_core(values):
    return swap(values, 0, 1)


def z_bits():
    half = lax.axis_size("dp") // 2
    return [1 << i for i in range(half.bit_length() - 1)]


def masks_of(bits):
    masks = [0]
    for bit in bits:
        masks = masks + [mask ^ bit for mask in masks]
    return masks


def weight_masks():
    return masks_of([2 * bit for bit in z_bits()] + [1])


def token_masks():
    return masks_of([2 * bit for bit in z_bits()[:-1]] + [1, 2 * z_bits()[-1]])


def owners(masks):
    return lax.axis_index("dp") ^ jnp.array(masks, jnp.int32)


def gather_line(pieces, bits):
    for bit in bits:
        pieces = pieces + [over_z(v, bit) for v in pieces]
    return pieces


def gather_dp(values):
    line = gather_line([values], z_bits())
    return line + [over_y(v) for v in line]


def gather_all(values):
    line = gather_line([values], z_bits())
    pairs = {}
    for mask, near in zip(masks_of([2 * bit for bit in z_bits()]), line, strict=True):
        if mask & 2 * z_bits()[-1]:
            aside = over_x(near)
            pairs[mask], pairs[mask + 1] = (near, aside), (over_y(near), over_y(aside))
        else:
            across = over_y(near)
            pairs[mask], pairs[mask + 1] = (near, over_x(near)), (across, over_x(across))
    return [
        (pairs[m][0], over_core(pairs[m][0]), pairs[m][1], over_core(pairs[m][1]))
        for m in token_masks()
    ]


def gather_tp(values):
    other = over_x(values)
    return [values, over_core(values), other, over_core(other)]


def sorted_by_bits(pieces, me):
    bit = 1
    while bit < len(pieces):
        odd = me & bit != 0
        pieces = [jnp.where(odd, pieces[i ^ bit], pieces[i]) for i in range(len(pieces))]
        bit *= 2
    return pieces


def absolute_dp(pieces):
    dp = len(pieces)
    by_mask = [pieces[i // 2 + i % 2 * (dp // 2)] for i in range(dp)]
    return jnp.stack(sorted_by_bits(by_mask, lax.axis_index("dp")))


def absolute_tp(pieces, axis=0):
    return jnp.concatenate(sorted_by_bits(list(pieces), lax.axis_index("tp")), axis=axis)


def added(*terms):
    total = terms[0].astype(f32)
    for term in terms[1:]:
        total = total + term.astype(f32)
    return total


def combined(terms, cut, waits=(), sent=bf16):
    shape = terms[0].shape
    outs = [shape_of((shape[0] - cut,) + shape[1:], sent)]
    if cut:
        outs.insert(0, shape_of((cut,) + shape[1:], f32))

    def kernel(*refs):
        for out, part in zip(refs[len(terms) :], (slice(0, cut), slice(cut, None))[-len(outs) :]):
            out[...] = added(*[ref[part] for ref in refs[: len(terms)]]).astype(out.dtype)

    result = kernel_call(kernel, "combined", [], list(terms), outs, 0, waits=waits)
    return result if cut else result[0]


def held(arrays, dtype, waits):
    def kernel(*refs):
        at = 0
        for ref in refs[:-1]:
            refs[-1][at : at + ref.shape[0], :] = ref[...].astype(dtype)
            at += ref.shape[0]

    rows = sum(array.shape[0] for array in arrays)
    out = shape_of((rows, arrays[0].shape[1]), dtype)
    return kernel_call(kernel, "held", [], list(arrays), [out], 0, waits=waits)[0]


def scatter_tp(parts):
    mine, far = over_core(parts[1]), over_core(parts[3])
    crossing = combined([parts[2], far], 0)
    return (parts[0], mine, over_x(crossing)), crossing


class TokenSums:
    def __init__(self, first, second):
        self.mid = first[0].shape[0] // 2
        self.first, self.second = first, second
        self.first_core = [over_core(first[1]), over_core(first[3])]
        self.second_core = [over_core(second[1]), over_core(second[3])]

    def start(self, *others):
        first, second = self.first, self.second
        self.b0, b0_far = combined([second[0], self.second_core[0]], self.mid, others)
        self.b1, b1_far = combined([second[2], self.second_core[1]], self.mid, others)
        a1 = combined([first[2], self.first_core[1]], 0, others)
        self.sent = [b0_far, b1_far, a1]
        self.came = [over_y(b0_far), over_y(b1_far), over_x(a1)]
        return self

    def turn(self, *others):
        b = combined([self.b1, self.came[1]], 0, others)
        self.a, a = combined([self.first[0], self.first_core[0], self.came[2]], self.mid, others)
        self.sent = [b, a]
        self.turned = [over_x(b), over_y(a)]
        return self

    def top(self, *others):
        self.sent = [combined([self.b0, self.came[0], self.turned[0]], 0, others)]
        self.from_top = over_z(self.sent[0], z_bits()[-1])
        return self

    def last(self, *others):
        terms = [self.a, self.turned[1], self.from_top]
        for bit in reversed(z_bits()[:-1]):
            near, sent = combined(terms, terms[0].shape[0] // 2, others if bit == 1 else ())
            terms = [near, over_z(sent, bit)]
        self.sent = [sent]
        return terms


def reduce_all(near, far):
    terms = [near, over_y(far)]
    for bit in reversed(z_bits()):
        near, sent = combined(terms, bit, sent=f32)
        terms = [near, over_z(sent, bit)]
    return reduce_tp(added(*terms)[0])


def reduce_tp(values):
    values = values + over_core(values)
    return values + over_x(values)


def reduce_heads(values):
    return reduce_tp(values + over_z(values, 1))


class WeightSums:
    def __init__(self, near, far):
        self.near, self.sent = near, far
        self.came = over_y(far)

    def along_z(self, *others):
        for bit in reversed(z_bits()[1:]):
            self.near, self.sent = combined([self.near, self.came], bit, others)
            self.came = over_z(self.sent, bit)
        return self

    def to_mate(self, *others):
        self.near, self.sent = combined([self.near, self.came], 1, others)
        self.came = over_z(self.sent, 1)
        return self

    def in_order(self, here, count, *others):
        _, rows, columns = self.near.shape
        size = columns // count if count else rows
        shape = (rows, 2 * size) if count else (2 * rows, columns)

        def kernel(here_ref, mine_ref, other_ref, *outs):
            for ref, which in ((mine_ref, here_ref[1]), (other_ref, 1 - here_ref[1])):
                part = pl.ds(pl.multiple_of(which * size, size), size)
                for j, out in enumerate(outs):
                    if count:
                        out[:, part] = ref[0, :, j * size : (j + 1) * size].astype(f32)
                    else:
                        out[part, :] = ref[0].astype(f32)

        return kernel_call(
            kernel,
            "in_order",
            [here],
            [self.near, self.came],
            [shape_of(shape, f32)] * max(count, 1),
            0,
            waits=others,
        )


def chosen_slots(table):
    experts, tokens = table.shape
    place = lax.broadcasted_iota(jnp.int32, (experts, CAP, tokens), 1)
    hit = place == table[:, None, :]
    return jnp.where(hit, 1.0, 0.0).astype(bf16).reshape(experts * CAP, tokens)


def rows_of_slots(pieces, table, waits, order=None):
    sequences, experts, tokens = table.shape
    if order is None:
        flat = [piece for group in pieces for piece in group]
        share, width = flat[0].shape
    else:
        flat = pieces
        share, width = tokens // 4, pieces[0].shape[1]
    count = sequences * 4

    def kernel(*refs):
        table_ref, *sources = refs[:-3]
        out_ref, buffer, arrived = refs[-3:]
        step = pl.program_id(0)

        def piece(i):
            if order is None:
                return sources[i]
            return sources[i % 4].at[pl.ds(order[i // 4] * share, share), :]

        @pl.when(step == 0)
        def _():
            for i in range(count):
                pltpu.make_async_copy(
                    piece(i), buffer.at[i // 4, pl.ds(i % 4 * share, share)], arrived.at[i]
                ).start()

        for i in range(4):
            pltpu.make_async_copy(
                piece(i), buffer.at[step, pl.ds(i * share, share)], arrived.at[step * 4 + i]
            ).wait()
        picked = jnp.dot(chosen_slots(table_ref[0]), buffer[step], preferred_element_type=f32)
        out_ref[...] = picked.astype(bf16).reshape(experts, CAP, width)

    return pl.pallas_call(
        without(kernel, 1 + len(flat), len(waits)),
        grid=(sequences,),
        in_specs=[pl.BlockSpec((1, experts, tokens), lambda s: (s, 0, 0))]
        + [pl.BlockSpec(memory_space=pl.ANY)] * (len(flat) + len(waits)),
        out_specs=pl.BlockSpec((experts, CAP, width), lambda s: (0, s, 0)),
        out_shape=jax.ShapeDtypeStruct((experts, sequences * CAP, width), bf16),
        scratch_shapes=[
            pltpu.VMEM((sequences, tokens, width), bf16),
            pltpu.SemaphoreType.DMA((count,)),
        ],
        compiler_params=pltpu.CompilerParams(vmem_limit_bytes=48 << 20),
        cost_estimate=cost(
            flops=2 * experts * CAP * sequences * tokens * width,
            bytes_accessed=2 * sequences * (tokens + experts * CAP) * width,
            transcendentals=0,
        ),
        name="rows_of_slots",
    )(table, *flat, *waits)


def tokens_of_slots(rows, table, first, waits):
    sequences, experts, tokens = table.shape
    width = rows.shape[-1]
    share = tokens // 4

    def kernel(table_ref, rows_ref, *outs):
        picked = chosen_slots(table_ref[0])
        total = lax.dot_general(
            picked,
            rows_ref[...].reshape(experts * CAP, width),
            (((0,), (0,)), ((), ())),
            preferred_element_type=f32,
        ).astype(bf16)
        for q, out in enumerate(outs):
            out[...] = total[q * share : (q + 1) * share]

    return pl.pallas_call(
        without(kernel, 2, len(waits)),
        grid=(sequences,),
        in_specs=[
            pl.BlockSpec((1, experts, tokens), lambda s: (s, 0, 0)),
            pl.BlockSpec((experts, CAP, width), lambda s: (0, s + first, 0)),
        ]
        + [pl.BlockSpec(memory_space=pl.ANY)] * len(waits),
        out_specs=[pl.BlockSpec((share, width), lambda s: (s, 0))] * 4,
        out_shape=[jax.ShapeDtypeStruct((sequences * share, width), bf16)] * 4,
        compiler_params=pltpu.CompilerParams(vmem_limit_bytes=48 << 20),
        cost_estimate=cost(
            flops=2 * experts * CAP * sequences * tokens * width,
            bytes_accessed=2 * sequences * (tokens + experts * CAP) * width,
            transcendentals=0,
        ),
        name="tokens_of_slots",
    )(table, rows, *waits)


def dot_last(a, b):
    return lax.dot_general(a, b, (((1,), (1,)), ((), ())), preferred_element_type=f32)


def dot_first(a, b):
    return lax.dot_general(a, b, (((0,), (0,)), ((), ())), preferred_element_type=f32)


def per_expert(kernel, experts, ins, outs, flops, name, scalars=(), waits=()):
    whole = lambda shape: pl.BlockSpec((1,) + tuple(shape[1:]), lambda e: (e, 0, 0))
    in_specs = [pl.BlockSpec(memory_space=pltpu.SMEM)] * len(scalars)
    moved = 0
    for array, block in ins:
        in_specs.append(pl.BlockSpec((1,) + block, lambda e: (e, 0, 0)))
        moved += experts * math.prod(block) * array.dtype.itemsize
    moved += sum(math.prod(o.shape) * o.dtype.itemsize for o in outs)
    return pl.pallas_call(
        without(kernel, len(in_specs), len(waits)),
        grid=(experts,),
        in_specs=in_specs + [pl.BlockSpec(memory_space=pl.ANY)] * len(waits),
        out_specs=[whole(o.shape) for o in outs],
        out_shape=list(outs),
        compiler_params=pltpu.CompilerParams(vmem_limit_bytes=48 << 20),
        cost_estimate=cost(flops=flops, bytes_accessed=moved, transcendentals=0),
        name=name,
    )(*scalars, *[array for array, _ in ins], *waits)


def grad_of_hidden(cot_rows, down_weight):
    experts, rows, width = cot_rows.shape
    hidden = down_weight.shape[1]

    def kernel(cot_ref, down_ref, out_ref):
        out_ref[0] = dot_last(cot_ref[0], down_ref[0])

    return per_expert(
        kernel,
        experts,
        [(cot_rows, (rows, width)), (down_weight, (hidden, width))],
        [jax.ShapeDtypeStruct((experts, rows, hidden), f32)],
        2 * experts * rows * width * hidden,
        "grad_of_hidden",
    )[0]


def expert_step(x_halves, gate_weight, up_weight, hidden_grad, first_expert):
    experts, half_rows, wide = x_halves[0].shape
    rows = half_rows * 2
    width, hidden = gate_weight.shape[1:]

    def kernel(base_ref, a_ref, b_ref, gate_ref, up_ref, grad_ref, back_ref, act_ref, gate_grad_ref, up_grad_ref):
        mine = base_ref[0] + pl.program_id(0)
        x = jnp.concatenate([a_ref[0, :, :width], b_ref[0, :, :width]])
        lane = lax.broadcasted_iota(jnp.int32, (rows, EXTRA), 1)
        probs = jnp.concatenate([a_ref[0, :, width:], b_ref[0, :, width:]]).astype(f32)
        mix = jnp.sum(
            jnp.where((lane == mine) | (lane == mine + E), probs, 0.0), axis=1, keepdims=True
        )
        gate_act = jnp.dot(x, gate_ref[0], preferred_element_type=f32)
        up_act = jnp.dot(x, up_ref[0], preferred_element_type=f32)
        raw = grad_ref[0]
        sig = jax.nn.sigmoid(gate_act)
        silu = gate_act * sig
        act = silu * up_act
        grad_mix = jnp.sum(act * raw, axis=1, keepdims=True)
        act_ref[0] = (mix * act).astype(bf16)
        weighted = mix * raw
        gate_grad = (weighted * up_act * sig * (1.0 + gate_act * (1.0 - sig))).astype(bf16)
        up_grad = (weighted * silu).astype(bf16)
        gate_grad_ref[0] = gate_grad
        up_grad_ref[0] = up_grad
        back_ref[0, :, :width] = (
            dot_last(gate_grad, gate_ref[0]) + dot_last(up_grad, up_ref[0])
        ).astype(bf16)
        coarse = grad_mix.astype(bf16).astype(f32)
        fine = grad_mix - coarse
        back_ref[0, :, width:] = jnp.where(
            lane == mine, coarse, jnp.where(lane == mine + E, fine, 0.0)
        ).astype(bf16)

    small = jax.ShapeDtypeStruct((experts, rows, hidden), bf16)
    return per_expert(
        kernel,
        experts,
        [
            (x_halves[0], (half_rows, wide)),
            (x_halves[1], (half_rows, wide)),
            (gate_weight, (width, hidden)),
            (up_weight, (width, hidden)),
            (hidden_grad, (rows, hidden)),
        ],
        [jax.ShapeDtypeStruct((experts, rows, wide), bf16), small, small, small],
        8 * experts * rows * width * hidden,
        "expert_step",
        (first_expert,),
    )


def expert_out(act, down_weight, waits):
    experts, rows, hidden = act.shape
    width = down_weight.shape[2]

    def kernel(act_ref, down_ref, out_ref):
        out_ref[0] = jnp.dot(act_ref[0], down_ref[0], preferred_element_type=f32).astype(bf16)

    return per_expert(
        kernel,
        experts,
        [(act, (rows, hidden)), (down_weight, (hidden, width))],
        [jax.ShapeDtypeStruct((experts, rows, width), bf16)],
        2 * experts * rows * width * hidden,
        "expert_out",
        waits=waits,
    )[0]


def expert_weight_grads(x_halves, cot_rows, act, gate_grad, up_grad, first, count, into, waits):
    experts, rows, hidden = act.shape
    width = cot_rows.shape[2]

    def kernel(a_ref, b_ref, cot_ref, act_ref, gate_ref, up_ref, *refs):
        gate_out, up_out, down_out, mark = refs[-4:]
        mark[...] = jnp.zeros_like(mark)
        x = jnp.concatenate([a_ref[0], b_ref[0]])
        gate_out[0] = dot_first(x, gate_ref[0])
        up_out[0] = dot_first(x, up_ref[0])
        down_out[0] = dot_first(act_ref[0], cot_ref[0])

    block = lambda *shape: pl.BlockSpec((1,) + shape, lambda e: (e + first, 0, 0))
    ins = [*x_halves, cot_rows, act, gate_grad, up_grad]
    return pl.pallas_call(
        kernel,
        grid=(count,),
        in_specs=[block(rows // 2, width)] * 2
        + [block(rows, width)]
        + [block(rows, hidden)] * 3
        + [pl.BlockSpec(memory_space=pl.ANY)] * (len(into) + len(waits)),
        out_specs=[block(width, hidden), block(width, hidden), block(hidden, width)]
        + [pl.BlockSpec((8, 128), lambda e: (0, 0))],
        out_shape=[
            jax.ShapeDtypeStruct((experts, width, hidden), f32),
            jax.ShapeDtypeStruct((experts, width, hidden), f32),
            jax.ShapeDtypeStruct((experts, hidden, width), f32),
            jax.ShapeDtypeStruct((8, 128), f32),
        ],
        input_output_aliases={len(ins) + i: i for i in range(len(into))},
        compiler_params=pltpu.CompilerParams(vmem_limit_bytes=48 << 20),
        cost_estimate=cost(
            flops=6 * count * rows * width * hidden,
            bytes_accessed=count * (4 * rows * (width + hidden) + 12 * width * hidden),
            transcendentals=0,
        ),
        name="expert_weight_grads",
    )(*ins, *into, *waits)


def without(kernel, start, count):
    return lambda *refs: kernel(*refs[:start], *refs[start + count :])


def kernel_call(kernel, name, scalars, ins, outs, flops, scratch=(), waits=()):
    moved = sum(a.size * a.dtype.itemsize for a in ins)
    moved += sum(math.prod(o.shape) * o.dtype.itemsize for o in outs)
    large = [i for i, a in enumerate(ins) if a.size * a.dtype.itemsize >= 1 << 16]
    first, last = len(scalars), len(scalars) + len(ins)
    made = last + len(waits)

    def body(*refs):
        given = list(refs[first:last])
        kept = made + len(outs) + len(scratch)
        copies = []
        for k, i in enumerate(large):
            copies.append(pltpu.make_async_copy(given[i], refs[kept + k], refs[-1].at[k]))
            copies[-1].start()
            given[i] = refs[kept + k]
        for copy in copies:
            copy.wait()
        kernel(*refs[:first], *given, *refs[made:kept])

    places = [pl.ANY if i in large else pltpu.VMEM for i in range(len(ins))]
    return pl.pallas_call(
        body,
        in_specs=[pl.BlockSpec(memory_space=pltpu.SMEM)] * len(scalars)
        + [pl.BlockSpec(memory_space=place) for place in places]
        + [pl.BlockSpec(memory_space=pl.ANY)] * len(waits),
        out_specs=[pl.BlockSpec(memory_space=pltpu.VMEM)] * len(outs),
        out_shape=list(outs),
        scratch_shapes=list(scratch)
        + [pltpu.VMEM(ins[i].shape, ins[i].dtype) for i in large]
        + [pltpu.SemaphoreType.DMA((max(len(large), 1),))],
        compiler_params=pltpu.CompilerParams(vmem_limit_bytes=40 << 20),
        cost_estimate=cost(flops=flops, bytes_accessed=moved, transcendentals=0),
        name=name,
    )(*scalars, *ins, *waits)


def shape_of(shape, dtype):
    return jax.ShapeDtypeStruct(shape, dtype)


def row_of(place_ref, dp, tokens, share, q, mate):
    which = (1 - place_ref[dp + 1]) if mate else place_ref[dp + 1]
    return pl.multiple_of(which * tokens + (place_ref[dp] ^ q) * share, share)


def split_heads(weights, here):
    rows, columns = weights[0].shape
    half = columns // 2

    def kernel(here_ref, *refs):
        keep_ref, give_ref, scratch = refs[len(weights) :]
        for j, ref in enumerate(refs[: len(weights)]):
            for i in range(2):
                scratch[i, :, j * half : (j + 1) * half] = ref[:, i * half : (i + 1) * half]
        keep_ref[...] = scratch[here_ref[1]]
        give_ref[...] = scratch[1 - here_ref[1]]

    shape = (rows, half * len(weights))
    return kernel_call(
        kernel,
        "split_heads",
        [here],
        list(weights),
        [shape_of(shape, bf16)] * 2,
        0,
        [pltpu.VMEM((2,) + shape, bf16)],
    )


def paired(own, mates, places, dp):
    share, width = mates[0].shape
    if len(mates) == 1:
        share = share // 4
    tokens = 4 * share
    slab = width // dp

    def kernel(place_ref, *refs):
        out_ref = refs[-1]
        if len(own) == 1:
            start = pl.multiple_of(place_ref[dp + 1] * tokens, tokens)
            for i in range(dp):
                out_ref[i, pl.ds(start, tokens), :] = refs[0][:, i * slab : (i + 1) * slab]
        for q in range(4):
            sources = []
            if len(own) == 4:
                sources.append((refs[q][...], False))
            if len(mates) == 4:
                sources.append((refs[len(own) + q][...], True))
            else:
                sources.append((refs[len(own)][q * share : (q + 1) * share, :], True))
            for rows, mate in sources:
                start = row_of(place_ref, dp, tokens, share, q, mate)
                for i in range(dp):
                    out_ref[i, pl.ds(start, share), :] = rows[:, i * slab : (i + 1) * slab]

    return kernel_call(
        kernel, "paired", [places], [*own, *mates], [shape_of((dp, 2 * tokens, slab), bf16)], 0
    )[0]


def as_rows(first, second):
    lane = lax.broadcasted_iota(jnp.int32, (first.shape[0], 128), 1)
    return jnp.where(lane < 4, first, second).T[:8]


def as_columns(pair):
    wide = jnp.concatenate([pair] * 16).T
    return wide[:, 0:1], wide[:, 4:5]


def project(x_slabs, pieces, places):
    dp, tokens, _ = x_slabs.shape
    columns = pieces[0].shape[1] // 3

    def kernel(place_ref, x_ref, *refs):
        totals = []
        for j in range(3):
            total = None
            for i in range(dp):
                part = jnp.dot(
                    x_ref[place_ref[i]],
                    refs[i][:, j * columns : (j + 1) * columns],
                    preferred_element_type=f32,
                )
                total = part if total is None else total + part
            totals.append(total)
        queries, keys, values = totals
        qk_out, v_out, squares_out = refs[dp:]
        qk_out[0] = queries
        qk_out[1] = keys
        v_out[...] = values.astype(bf16)
        squares_out[...] = as_rows(
            jnp.sum(queries * queries, axis=1, keepdims=True),
            jnp.sum(keys * keys, axis=1, keepdims=True),
        )

    return kernel_call(
        kernel,
        "project",
        [places],
        [x_slabs, *pieces],
        [
            shape_of((2, tokens, columns), f32),
            shape_of((tokens, columns), bf16),
            shape_of((8, tokens), f32),
        ],
        6 * x_slabs.size * columns,
    )


def turned(values):
    return pltpu.roll(values, HD // 2, 1)


def attend(projected, squares, values, gains, tables, bias, places, dp, waits=()):
    _, rows, columns = projected.shape
    tokens = rows // 2
    heads = columns // HD
    lanes = 128 // heads

    def kernel(place_ref, qk_ref, sq_ref, v_ref, gain_ref, table_ref, bias_ref, *refs):
        turned_out, log_out, att_out, keep_out, give_out = refs
        turned_out[2] = v_ref[...]
        cosine, sine = table_ref[0], table_ref[1]
        lane = lax.broadcasted_iota(jnp.int32, (tokens, 128), 1)
        q_squares, k_squares = as_columns(sq_ref[...])
        for which in range(2):
            row = slice(which * tokens, (which + 1) * tokens)
            q_scale = lax.rsqrt(q_squares[row] / D + epsilon)
            k_scale = lax.rsqrt(k_squares[row] / D + epsilon)
            logs = jnp.zeros((tokens, 128), f32)
            for h in range(heads):
                cut = slice(h * HD, (h + 1) * HD)
                q = qk_ref[0, row, cut] * q_scale * gain_ref[0:1, cut]
                k = qk_ref[1, row, cut] * k_scale * gain_ref[1:2, cut]
                q = (q * cosine + turned(q) * sine).astype(bf16)
                k = (k * cosine + turned(k) * sine).astype(bf16)
                turned_out[0, row, cut] = q
                turned_out[1, row, cut] = k
                scores = dot_last(q, k) * (1.0 / math.sqrt(HD)) + bias_ref[which]
                largest = jnp.max(scores, axis=1, keepdims=True)
                raised = jnp.exp(scores - largest)
                total = jnp.sum(raised, axis=1, keepdims=True)
                logs = jnp.where(lane // lanes == h, largest + jnp.log(total), logs)
                probs = (raised / total).astype(bf16)
                att_out[row, cut] = jnp.dot(
                    probs, v_ref[row, cut], preferred_element_type=f32
                ).astype(bf16)
            log_out[row, :] = logs
        upper = place_ref[dp + 1]
        keep_out[...] = att_out[pl.ds(pl.multiple_of(upper * tokens, tokens), tokens), :]
        give_out[...] = att_out[pl.ds(pl.multiple_of((1 - upper) * tokens, tokens), tokens), :]

    part = shape_of((tokens, columns), bf16)
    return kernel_call(
        kernel,
        "attend",
        [places],
        [projected, squares, values, gains, tables, bias],
        [
            shape_of((3, rows, columns), bf16),
            shape_of((rows, 128), f32),
            shape_of((rows, columns), bf16),
            part,
            part,
        ],
        4 * tokens * rows * columns,
        waits=waits,
    )


def output_project(keep, got, pieces, places, waits=()):
    tokens, columns = keep.shape
    dp = len(pieces)
    slab = pieces[0].shape[1]
    share = tokens // 4

    def kernel(place_ref, keep_ref, got_ref, *refs):
        weights, parts, scratch = refs[:dp], refs[dp:-1], refs[-1]
        upper = place_ref[dp + 1]
        mine = pl.ds(pl.multiple_of(upper * columns, columns), columns)
        other = pl.ds(pl.multiple_of((1 - upper) * columns, columns), columns)
        for i in range(dp):
            scratch[place_ref[i]] = (
                jnp.dot(keep_ref[...], weights[i][mine, :], preferred_element_type=f32)
                + jnp.dot(got_ref[...], weights[i][other, :], preferred_element_type=f32)
            ).astype(bf16)
        for q, part in enumerate(parts):
            start = pl.multiple_of((place_ref[dp] ^ q) * share, share)
            for i in range(dp):
                part[:, i * slab : (i + 1) * slab] = scratch[i, pl.ds(start, share), :]

    return kernel_call(
        kernel,
        "output_project",
        [places],
        [keep, got, *pieces],
        [shape_of((share, slab * dp), bf16)] * 4,
        4 * tokens * columns * slab * dp,
        [pltpu.VMEM((dp, tokens, slab), bf16)],
        waits=waits,
    )


def route(terms, hidden, gain, router, waits=()):
    share, width = hidden.shape

    def kernel(a_ref, b_ref, c_ref, hidden_ref, gain_ref, router_ref, middle_ref, x_ref, probs_ref):
        middle = hidden_ref[...] + added(a_ref[...], b_ref[...], c_ref[...])
        middle_ref[...] = middle
        scale = lax.rsqrt(jnp.mean(middle * middle, axis=1, keepdims=True) + epsilon)
        normed = (middle * scale * gain_ref[...]).astype(bf16)
        x_ref[:, :width] = normed
        logits = dot_last(normed, router_ref[...])
        raised = jnp.exp(logits - jnp.max(logits, axis=1, keepdims=True))
        probs = raised / (0.5 * jnp.sum(raised, axis=1, keepdims=True))
        probs_ref[...] = probs
        coarse = probs.astype(bf16).astype(f32)
        lane = lax.broadcasted_iota(jnp.int32, probs.shape, 1)
        x_ref[:, width:] = jnp.where(lane < E, coarse, probs - coarse).astype(bf16)

    return kernel_call(
        kernel,
        "route",
        [],
        [*terms, hidden, gain, router],
        [
            shape_of((share, width), f32),
            shape_of((share, width + EXTRA), bf16),
            shape_of((share, EXTRA), f32),
        ],
        2 * share * width * EXTRA,
        waits=waits,
    )


def route_back(terms, middle, x_piece, probs, cotangent, gain, router, waits=()):
    share, width = middle.shape

    def kernel(a_ref, b_ref, middle_ref, x_ref, probs_ref, cot_ref, gain_ref, router_ref, *outs):
        grad_ref, low_ref, router_out, gain_out = outs
        pair = added(a_ref[:, width:], b_ref[:, width:])
        grad_probs = pair + pltpu.roll(pair, E, 1)
        probs = probs_ref[...]
        inner = 0.5 * jnp.sum(probs * grad_probs, axis=1, keepdims=True)
        grad_logits = probs * (grad_probs - inner)
        middle = middle_ref[...]
        scale = lax.rsqrt(jnp.mean(middle * middle, axis=1, keepdims=True) + epsilon)
        lane = lax.broadcasted_iota(jnp.int32, probs.shape, 1)
        once = jnp.where(lane < E, grad_logits, 0.0)
        normed_grad = added(a_ref[:, :width], b_ref[:, :width]) + lax.dot_general(
            once,
            router_ref[...].astype(f32),
            (((1,), (0,)), ((), ())),
            precision=lax.Precision.HIGHEST,
            preferred_element_type=f32,
        )
        router_out[...] = lax.dot_general(
            once,
            x_ref[:, :width].astype(f32),
            (((0,), (0,)), ((), ())),
            precision=lax.Precision.HIGHEST,
            preferred_element_type=f32,
        )
        gain_out[...] = jnp.sum(normed_grad * middle * scale, axis=0, keepdims=True)
        scaled = normed_grad * gain_ref[...]
        grad = (
            cot_ref[...]
            + scale * scaled
            - middle * (scale * scale * scale) * jnp.mean(scaled * middle, axis=1, keepdims=True)
        )
        grad_ref[...] = grad
        low_ref[...] = grad.astype(bf16)

    return kernel_call(
        kernel,
        "route_back",
        [],
        [*terms, middle, x_piece, probs, cotangent, gain, router],
        [
            shape_of((share, width), f32),
            shape_of((share, width), bf16),
            shape_of((EXTRA, width), f32),
            shape_of((1, width), f32),
        ],
        24 * share * width * EXTRA,
        waits=waits,
    )


def output_back(low_pieces, pieces, places, waits):
    dp = len(pieces)
    columns, slab = pieces[0].shape
    share = low_pieces[0].shape[0]
    tokens = 4 * share
    half = columns // 2

    def kernel(place_ref, *refs):
        lows, weights, (keep_ref, give_ref, scratch, both) = refs[:4], refs[4 : 4 + dp], refs[4 + dp :]
        for q, low in enumerate(lows):
            start = pl.multiple_of((place_ref[dp] ^ q) * share, share)
            for i in range(dp):
                scratch[i, pl.ds(start, share), :] = low[:, i * slab : (i + 1) * slab]
        total = None
        for i in range(dp):
            part = dot_last(scratch[place_ref[i]], weights[i][...])
            total = part if total is None else total + part
        both[0] = total[:, :half].astype(bf16)
        both[1] = total[:, half:].astype(bf16)
        upper = place_ref[dp + 1]
        keep_ref[...] = both[upper]
        give_ref[...] = both[1 - upper]

    return kernel_call(
        kernel,
        "output_back",
        [places],
        [*low_pieces, *pieces],
        [shape_of((tokens, half), bf16)] * 2,
        2 * tokens * columns * slab * dp,
        [pltpu.VMEM((dp, tokens, slab), bf16), pltpu.VMEM((2, tokens, half), bf16)],
        waits=waits,
    )


def attend_back(keep, got, places, dp, turned_rows, logs, projected, squares, gains, tables, bias, waits):
    _, rows, columns = projected.shape
    tokens = rows // 2
    heads = columns // HD
    lanes = 128 // heads

    def kernel(place_ref, keep_ref, got_ref, *refs):
        turned_ref, log_ref, qk_ref, sq_ref, gain_ref, table_ref, bias_ref = refs[:7]
        gv_ref, gqk_ref, inner_ref, gains_ref, scratch = refs[7:]
        upper = place_ref[dp + 1]
        scratch[upper] = keep_ref[...]
        scratch[1 - upper] = got_ref[...]
        cosine, sine = table_ref[0], table_ref[1]
        q_squares, k_squares = as_columns(sq_ref[...])
        for which in range(2):
            row = slice(which * tokens, (which + 1) * tokens)
            q_scale = lax.rsqrt(q_squares[row] / D + epsilon)
            k_scale = lax.rsqrt(k_squares[row] / D + epsilon)
            inner = [jnp.zeros((tokens, 1), f32), jnp.zeros((tokens, 1), f32)]
            for h in range(heads):
                cut = slice(h * HD, (h + 1) * HD)
                qr, kr, v = (turned_ref[i, row, cut] for i in range(3))
                grad = scratch[which, :, cut]
                scores = dot_last(qr, kr) * (1.0 / math.sqrt(HD)) + bias_ref[which]
                probs = jnp.exp(scores - log_ref[row, h * lanes : h * lanes + 1])
                gv_ref[row, cut] = dot_first(probs.astype(bf16), grad).astype(bf16)
                grad_probs = dot_last(grad, v)
                dots = jnp.sum(probs * grad_probs, axis=1, keepdims=True)
                grad_scores = (probs * (grad_probs - dots) * (1.0 / math.sqrt(HD))).astype(bf16)
                gq = jnp.dot(grad_scores, kr, preferred_element_type=f32)
                gk = dot_first(grad_scores, qr)
                gq = gq * cosine - turned(gq) * sine
                gk = gk * cosine - turned(gk) * sine
                q, k = qk_ref[0, row, cut], qk_ref[1, row, cut]
                for i, (grad_sum, value, scale) in enumerate(((gq, q, q_scale), (gk, k, k_scale))):
                    total = jnp.sum(grad_sum * value * scale, axis=0, keepdims=True)
                    if which:
                        total = total + gains_ref[i : i + 1, cut]
                    gains_ref[i : i + 1, cut] = total
                gq = gq * gain_ref[0:1, cut]
                gk = gk * gain_ref[1:2, cut]
                gqk_ref[0, row, cut] = gq
                gqk_ref[1, row, cut] = gk
                inner[0] = inner[0] + jnp.sum(gq * q, axis=1, keepdims=True)
                inner[1] = inner[1] + jnp.sum(gk * k, axis=1, keepdims=True)
            inner_ref[:, row] = as_rows(*inner)

    return kernel_call(
        kernel,
        "attend_back",
        [places],
        [keep, got, turned_rows, logs, projected, squares, gains, tables, bias],
        [
            shape_of((rows, columns), bf16),
            shape_of((2, rows, columns), f32),
            shape_of((8, rows), f32),
            shape_of((2, columns), f32),
        ],
        10 * tokens * rows * columns,
        [pltpu.VMEM((2, tokens, columns), bf16)],
        waits=waits,
    )


def norm_back(grads, projected, squares, inner, waits=()):
    _, tokens, columns = projected.shape

    def kernel(grad_ref, value_ref, sq_ref, inner_ref, *outs):
        squares, inners = as_columns(sq_ref[...]), as_columns(inner_ref[...])
        for i, out in enumerate(outs):
            scale = lax.rsqrt(squares[i] / D + epsilon)
            mean = inners[i] / D
            out[...] = (
                scale * grad_ref[i] - value_ref[i] * (scale * scale * scale) * mean
            ).astype(bf16)

    low = shape_of((tokens, columns), bf16)
    return kernel_call(
        kernel,
        "norm_back",
        [],
        [grads, projected, squares, inner],
        [low, low],
        0,
        waits=waits,
    )


def project_back(grads, weights, places, waits=()):
    rows, columns = grads[0].shape
    tokens = rows // 2
    dp = len(weights)
    slab = weights[0].shape[0]
    share = tokens // 4

    def kernel(place_ref, *refs):
        values = [ref[...] for ref in refs[: len(grads)]]
        pieces = refs[len(grads) : len(grads) + dp]
        parts, scratch = refs[len(grads) + dp : -1], refs[-1]
        for i in range(dp):
            total = None
            for j, value in enumerate(values):
                part = dot_last(value, pieces[i][:, j * columns : (j + 1) * columns])
                total = part if total is None else total + part
            scratch[place_ref[i]] = total.astype(bf16)
        for q, part in enumerate(parts):
            for mate in range(2):
                start = row_of(place_ref, dp, tokens, share, q, mate)
                for i in range(dp):
                    part[mate * share : (mate + 1) * share, i * slab : (i + 1) * slab] = scratch[
                        i, pl.ds(start, share), :
                    ]

    return kernel_call(
        kernel,
        "project_back",
        [places],
        [*grads, *weights],
        [shape_of((2 * share, slab * dp), bf16)] * 4,
        2 * len(grads) * rows * columns * slab * dp,
        [pltpu.VMEM((dp, rows, slab), bf16)],
        waits=waits,
    )


def weight_parts(slabs, wholes, places, slab_first, waits=()):
    dp, rows, slab = slabs.shape
    columns = wholes[0].shape[1]
    half = dp // 2
    shape = (slab, columns * len(wholes)) if slab_first else (columns, slab)

    def kernel(place_ref, slab_ref, *refs):
        outs = refs[len(wholes) :]
        for i in range(dp):
            left = slab_ref[place_ref[i]]
            for j, whole in enumerate(refs[: len(wholes)]):
                pair = (left, whole[...]) if slab_first else (whole[...], left)
                cut = slice(j * columns, (j + 1) * columns) if slab_first else slice(None)
                outs[i // half][i % half, :, cut] = dot_first(*pair).astype(bf16)

    return kernel_call(
        kernel,
        "weight_parts",
        [places],
        [slabs, *wholes],
        [shape_of((half,) + shape, bf16)] * 2,
        2 * slabs.size * columns * len(wholes),
        waits=waits,
    )


def hidden_back(terms, from_mate, hidden, grad_middle, gain, waits=()):
    share, width = hidden.shape

    def kernel(a_ref, b_ref, c_ref, d_ref, hidden_ref, grad_ref, gain_ref, out_ref, gain_out):
        normed_grad = added(a_ref[:share, :], b_ref[:share, :], c_ref[:share, :], d_ref[...])
        hidden = hidden_ref[...]
        scale = lax.rsqrt(jnp.mean(hidden * hidden, axis=1, keepdims=True) + epsilon)
        gain_out[...] = jnp.sum(normed_grad * hidden * scale, axis=0, keepdims=True)
        scaled = normed_grad * gain_ref[...]
        out_ref[...] = (
            grad_ref[...]
            + scale * scaled
            - hidden * (scale * scale * scale) * jnp.mean(scaled * hidden, axis=1, keepdims=True)
        )

    return kernel_call(
        kernel,
        "hidden_back",
        [],
        [*terms, from_mate, hidden, grad_middle, gain],
        [shape_of((share, width), f32), shape_of((1, width), f32)],
        0,
        waits=waits,
    )


def rope_tables(length, head_size):
    half_size = head_size // 2
    inverse = 10000.0 ** (-2.0 * jnp.arange(half_size, dtype=jnp.float32) / head_size)
    angles = jnp.arange(length, dtype=jnp.float32)[:, None] * inverse[None, :]
    cosine, sine = jnp.cos(angles), jnp.sin(angles)
    return jnp.stack(
        [jnp.concatenate([cosine, cosine], axis=1), jnp.concatenate([-sine, sine], axis=1)]
    )


def unpack(pieces, places, rows, experts, heads, half_heads, token_order, waits=()):
    dp = len(pieces)
    tokens = pieces[0].shape[1]
    at = [0]
    for n in rows:
        at.append(at[-1] + n)
    slab = D // dp
    head_slab = HD // dp
    share = tokens // 4

    def kernel(place_ref, *refs):
        parts = refs[:dp]
        router_ref, one_ref, two_ref, gain_ref, table_ref, bias_ref, wide, heads_at = refs[dp:]
        tp, upper = place_ref[dp], place_ref[dp + 1]
        for i in range(dp):
            wide[place_ref[i]] = parts[i][...].astype(f32)
        for j in range(dp):
            cut = slice(j * slab, (j + 1) * slab)
            weight = wide[j, : at[1], :slab].astype(bf16)
            router_ref[: at[1], cut] = weight
            router_ref[at[1] :, cut] = weight
            one_ref[:, cut] = wide[j, at[1] : at[2], :slab]
            two_ref[:, cut] = wide[j, at[2] : at[3], :slab]
            for i in range(2):
                heads_at[i, :heads, j * head_slab : (j + 1) * head_slab] = wide[
                    j, at[3 + i] : at[4 + i], :head_slab
                ]
        for i in range(2):
            for h in range(half_heads):
                gain_ref[i : i + 1, h * HD : (h + 1) * HD] = heads_at[
                    i, pl.ds(upper * half_heads + h, 1), :
                ]
        row = lax.broadcasted_iota(jnp.int32, (tokens, tokens), 0)
        column = lax.broadcasted_iota(jnp.int32, (tokens, tokens), 1)
        before = jnp.where(row < column, 1.0, 0.0).astype(bf16)
        lane = lax.broadcasted_iota(jnp.int32, (at[6] - at[5], tokens), 1)
        first = place_ref[0] * experts
        for at_tokens, i in enumerate(token_order):
            ids = parts[i][at[5] : at[6], :].astype(f32)
            for bit, step in ((1, share), (2, 2 * share)):
                turned_ids = jnp.where(
                    lane // step % 2 == 0,
                    pltpu.roll(ids, tokens - step, 1),
                    pltpu.roll(ids, step, 1),
                )
                ids = jnp.where((tp & bit) != 0, turned_ids, ids)
            named = jnp.concatenate(
                [
                    jnp.sum(
                        jnp.where(ids == (first + e).astype(f32), 1.0, 0.0), axis=0, keepdims=True
                    )
                    for e in range(experts)
                ]
            )
            slot = jnp.dot(named.astype(bf16), before, preferred_element_type=f32)
            table_ref[at_tokens] = jnp.where(named > 0.5, slot, -1.0).astype(jnp.int32)
        for i in range(2):
            line = parts[i][at[6] : at[7], :].astype(f32)
            segments = jnp.broadcast_to(line, (tokens, tokens))
            allowed = (column <= row) & (segments.T == segments)
            bias_ref[upper ^ i] = jnp.where(allowed, 0.0, -1e30)

    return kernel_call(
        kernel,
        "unpack",
        [places],
        pieces,
        [
            shape_of((2 * at[1], D), bf16),
            shape_of((1, D), f32),
            shape_of((1, D), f32),
            shape_of((2, half_heads * HD), f32),
            shape_of((dp, experts, tokens), jnp.int32),
            shape_of((2, tokens, tokens), f32),
        ],
        0,
        [
            pltpu.VMEM((dp,) + pieces[0].shape, f32),
            pltpu.VMEM((2, 8, HD), f32),
        ],
        waits=waits,
    )


def packed_sums(groups, heads, places, dp, waits=()):
    slab = D // dp
    head_slab = HD // dp
    here = 0 if heads is None else heads.shape[1] // HD
    count = 4 * 2 * here
    rows = sum(-(-group.shape[0] // 8) * 8 for group in groups)

    def kernel(place_ref, *refs):
        scratch, by_head = refs[-2:]
        outs = refs[-4:-2]
        scratch[...] = jnp.zeros_like(scratch)
        if here:
            first = place_ref[dp] * 2 * here + place_ref[dp + 1] * here
            by_head[...] = jnp.zeros_like(by_head)
            for i in range(2):
                for h in range(here):
                    by_head[pl.ds(i * count + first + h, 1), :] = refs[len(groups)][
                        i : i + 1, h * HD : (h + 1) * HD
                    ]
        for j in range(dp):
            at = 0
            for ref in refs[: len(groups)]:
                scratch[j, at : at + ref.shape[0], :] = ref[:, j * slab : (j + 1) * slab]
                at += -(-ref.shape[0] // 8) * 8
            if here:
                scratch[j, at:, :head_slab] = by_head[:, j * head_slab : (j + 1) * head_slab]
        for i in range(dp):
            outs[i // (dp // 2)][i % (dp // 2)] = scratch[place_ref[i]]

    shape = (dp, rows + 2 * count, slab)
    return kernel_call(
        kernel,
        "packed_sums",
        [places],
        [*groups] + ([heads] if here else []),
        [shape_of((dp // 2,) + shape[1:], f32)] * 2,
        0,
        [pltpu.VMEM(shape, f32), pltpu.VMEM((max(2 * count, 8), HD), f32)],
        waits=waits,
    )


def per_device(
    hidden_in,
    cotangent,
    segment_ids,
    expert_ids,
    first_gain,
    query_weight,
    key_weight,
    value_weight,
    output_weight,
    query_gain,
    key_gain,
    second_gain,
    router_weight,
    gate_weight,
    up_weight,
    down_weight,
):
    data_size = lax.axis_size("dp")
    tensor_size = lax.axis_size("tp")
    half = data_size // 2
    seq_len, width = hidden_in.shape
    share = seq_len // tensor_size
    slab = width // data_size
    me_dp, me_tp = lax.axis_index("dp"), lax.axis_index("tp")
    upper = me_dp // 2 % 2
    own = lambda values: lax.dynamic_slice_in_dim(values, me_tp * share, share, 0)
    local_experts = E // data_size
    first_expert = (me_dp * local_experts).astype(jnp.int32).reshape(1)
    here = jnp.stack([me_tp, upper]).astype(jnp.int32)
    places = jnp.concatenate([owners(weight_masks()), here])
    token_order = [weight_masks().index(mask) for mask in token_masks()]

    hidden_own, cot_own = own(hidden_in), own(cotangent)
    heads_local, head_slab = query_gain.shape
    small = [
        router_weight.T,
        first_gain[None],
        second_gain[None],
        query_gain,
        key_gain,
        expert_ids.T.astype(bf16),
        segment_ids.astype(bf16),
    ]
    small_rows = [array.shape[0] for array in small]
    wide = [jnp.pad(array, ((0, 0), (0, seq_len - array.shape[1]))) for array in small]
    small = gather_dp(jnp.concatenate(wide))
    column_half = heads_local * HD // 2
    kept, given = split_heads([query_weight, key_weight, value_weight], here)
    head_line = gather_line([kept, over_z(given, 1)], z_bits()[1:])
    head_pieces = head_line + [over_y(v) for v in head_line]
    cot_line = gather_dp(cot_own.astype(bf16))
    output_pieces = gather_dp(held([output_weight], bf16, [head_line[-1]]))
    router, gain_one, gain_two, gains, table, bias = unpack(
        small,
        places,
        small_rows,
        local_experts,
        heads_local,
        heads_local // 2,
        token_order,
        waits=[head_line[1]],
    )
    tables = rope_tables(seq_len, HD)
    first_scale = lax.rsqrt(jnp.mean(hidden_in * hidden_in, axis=-1, keepdims=True) + epsilon)
    normed_one = (hidden_in * first_scale * gain_one).astype(bf16)
    mates = gather_tp(over_z(own(normed_one), 1))
    x_slabs = paired([normed_one], mates, places, data_size)
    cot_all = gather_tp(held(cot_line, bf16, [mates[2]]))
    cot_rows = rows_of_slots(cot_all, table, [], token_order)
    hidden_grad = grad_of_hidden(cot_rows, down_weight)
    projected, values, squares = project(
        x_slabs, head_pieces, places
    )
    squares = reduce_heads(squares)
    turned_rows, logs, attended, keep, give = attend(
        projected, squares, values, gains, tables, bias, places, data_size, waits=output_pieces[:half]
    )
    parts = output_project(keep, over_z(give, 1), output_pieces, places)
    middle, x_piece, probs = route(scatter_tp(parts)[0], hidden_own, gain_two, router)

    picks = (slice(0, half), slice(half, None))
    x_pieces = gather_all(x_piece)
    x_first = rows_of_slots(x_pieces[picks[0]], table[picks[0]], [hidden_grad])
    x_halves = [x_first, rows_of_slots(x_pieces[picks[1]], table[picks[1]], [x_first])]
    back_rows, act, gate_grad, up_grad = expert_step(
        x_halves, gate_weight, up_weight, hidden_grad, first_expert
    )
    second = tokens_of_slots(back_rows, table[picks[1]], half, [])
    first = tokens_of_slots(back_rows, table[picks[0]], 0, [second[0]])
    back = TokenSums(first, second).start()
    out_rows = expert_out(act, down_weight, back.sent)
    out_second = tokens_of_slots(out_rows, table[picks[1]], half, [])
    back.turn(out_second[0])
    out_first = tokens_of_slots(out_rows, table[picks[0]], 0, back.sent)
    chunk = max(local_experts // 4, 1)
    grads = []

    def some_grads(i, *waits):
        *grads[:], mark = expert_weight_grads(
            x_halves, cot_rows, act, gate_grad, up_grad, i * chunk, chunk, list(grads), waits
        )
        return mark

    mark = some_grads(0, out_first[0])
    back.top(mark)
    moe = TokenSums(out_first, out_second).start(*back.sent)
    mark = some_grads(1, mark, *moe.sent)
    back = back.last(mark)

    grad_middle, grad_low, router_sum, gain_sum = route_back(
        back, middle, x_piece, probs, cot_own, gain_two, router, waits=moe.came
    )
    low_pieces = gather_tp(grad_low)
    keep, give = output_back(low_pieces, output_pieces, places, [])
    moe.turn(keep)
    grad_values, gqk, inner, gain_sums = attend_back(
        keep, over_z(give, 1), places, data_size, turned_rows, logs, projected, squares, gains, tables, bias,
        [],
    )
    moe.top(gain_sums)
    inner = reduce_heads(inner)
    grad_queries, grad_keys = norm_back(gqk, projected, squares, inner, waits=moe.turned)
    head_grads = [grad_queries, grad_keys, grad_values]
    head_sums_at = WeightSums(*weight_parts(x_slabs, head_grads, places, True))
    parts = project_back(head_grads, head_pieces, places, waits=[head_sums_at.sent])
    terms, crossing = scatter_tp(parts)
    for_mate = combined([term[share:] for term in terms], 0)
    from_mate = over_z(for_mate, 1)
    head_sums_at.along_z(moe.from_top)
    mates_low = over_z(held(low_pieces, bf16, [for_mate]), 1)
    mark = some_grads(2, mark, head_sums_at.sent)
    moe = moe.last(head_sums_at.sent)
    low_slabs = paired(low_pieces, [mates_low], places, data_size)
    output_parts = weight_parts(
        low_slabs, [attended], places, False, waits=[head_sums_at.sent]
    )
    output_sums = WeightSums(*output_parts)
    grad_hidden, first_sum = hidden_back(terms, from_mate, hidden_own, grad_middle, gain_one)
    late = packed_sums(
        [router_sum[:E], gain_sum, first_sum],
        gain_sums,
        places,
        data_size,
        [head_sums_at.sent],
    )
    grad_hidden = gather_tp(grad_hidden)
    output_sums.along_z(mark)
    mark = some_grads(3, mark, output_sums.sent)
    head_sums_at.to_mate(output_sums.sent)
    output_sums.to_mate(head_sums_at.sent)
    total = reduce_all(*late)
    grad_hidden = absolute_tp(grad_hidden)
    hidden_out = absolute_tp(gather_tp(combined([middle, *moe], 0, sent=f32)))
    late = total[E + 8 :]
    head_sums = late[8:, :head_slab].reshape(2, heads_local * tensor_size, head_slab)
    head_sums = lax.dynamic_slice_in_dim(head_sums, me_tp * heads_local, heads_local, 1)
    grad_query, grad_key, grad_value = head_sums_at.in_order(here, 3, output_sums.sent)
    (grad_output,) = output_sums.in_order(here, 0)
    return (
        hidden_out,
        grad_hidden,
        late[0],
        grad_query,
        grad_key,
        grad_value,
        grad_output,
        head_sums[0],
        head_sums[1],
        total[E],
        total[:E].T,
        *grads,
    )


def solution(mesh):
    return jax.shard_map(
        per_device,
        mesh=mesh,
        in_specs=(
            P("dp", None),
            P("dp", None),
            P("dp", None),
            P("dp", None),
            P("dp"),
            P("dp", "tp"),
            P("dp", "tp"),
            P("dp", "tp"),
            P("tp", "dp"),
            P("tp", "dp"),
            P("tp", "dp"),
            P("dp"),
            P("dp", None),
            P("dp", None, "tp"),
            P("dp", None, "tp"),
            P("dp", "tp", None),
        ),
        out_specs=(
            P("dp", None),
            P("dp", None),
            P("dp"),
            P("dp", "tp"),
            P("dp", "tp"),
            P("dp", "tp"),
            P("tp", "dp"),
            P("tp", "dp"),
            P("tp", "dp"),
            P("dp"),
            P("dp", None),
            P("dp", None, "tp"),
            P("dp", None, "tp"),
            P("dp", "tp", None),
        ),
        check_vma=False,
    )
```

time: 742 us -> 621 us (0.84)
  starting transfers between devices: 171 us -> 95.1 us
  local copies, waits for them, and re-layouts: 65.3 us -> 43.6 us
  other arithmetic: 31.3 us -> 15.4 us
  Pallas kernels: 185 us -> 177 us
    ppermute x201 -> x124, starting transfers between devices: 171 us -> 95.1 us  [swap(): return lax.ppermute(values, ('dp', 'tp'), pairs)]
    another operation x16 -> x0, local copies, waits for them, and re-layouts: 10.4 us -> none  [the longest x5 4.42 us: absolute_dp(): near = jnp.stack([pieces[dz] for dz in backwards])]
    pallas_call x31 -> x60, Pallas kernels: 185 us -> 177 us  [the longest x46 55.9 us: kernel_call(): pl.pallas_call(body, in_specs=[pl.BlockSpec(memory_space=pltpu.SMEM)] * l...]
    unnamed x367 -> x268, local copies, waits for them, and re-layouts: 42.4 us -> 37 us
    ppermute x201 -> x124, waiting for transfers between devices: 275 us -> 278 us  [swap(): return lax.ppermute(values, ('dp', 'tp'), pairs)]
  transfers between devices with their start and end apart: 201 -> 124, of which waited for: 63 -> 50; matrix products, arithmetic and copies ran while one was open for 7% -> 3% of each run, Pallas kernels for 25% -> 20%
where the time goes in v3:
time: 621 us; the launch traced here: 612 us
  waiting for transfers between devices  278 us (45%)
  Pallas kernels  177 us (29%)
  starting transfers between devices  95.1 us (15%)
  local copies, waits for them, and re-layouts  43.6 us (7%)
  other arithmetic  15.4 us (2%)
    ppermute x124, waiting for transfers between devices, swap(): return lax.ppermute(values, ('dp', 'tp'), pairs)  278 us
    ppermute x124, starting transfers between devices, swap(): return lax.ppermute(values, ('dp', 'tp'), pairs)  95.1 us
    pallas_call x46, Pallas kernels, kernel_call(): pl.pallas_call(body, in_specs=[pl.BlockSpec(memory_space=pltpu.SMEM)] * l...  55.9 us
    pallas_call x3, Pallas kernels, per_expert(): pl.pallas_call(without(kernel, len(in_specs), len(waits)), grid=(experts,...  44.2 us
    unnamed x268, local copies, waits for them, and re-layouts  37 us
    pallas_call x4, Pallas kernels, expert_weight_grads(): pl.pallas_call(kernel, grid=(count,), in_specs=[block(rows // 2, width)]...  31.6 us
    pallas_call x4, Pallas kernels, tokens_of_slots(): pl.pallas_call(without(kernel, 2, len(waits)), grid=(sequences,), in_spec...  25.7 us
    pallas_call x3, Pallas kernels, rows_of_slots(): pl.pallas_call(without(kernel, 1 + len(flat), len(waits)), grid=(sequence...  19.3 us
  transfers between devices with their start and end apart: 124, of which 50 were waited for; matrix products, arithmetic and copies ran while one was open for 3% of the time, Pallas kernels for 20%

profile of v3, /device:TPU:0, one launch (start us, length us, event | category | flops | bytes accessed | tf_op | source)
XLA Modules:
  0.0 612.2 jit_solution(1053064567562739421)
XLA Ops:
  25.9 10.9 %collective-permute-done.2.refs_4_ = bf16[83,256]{1,0:T(8,128)(2,1)S(1)} collective-permute-done((bf16[83,256]{1,0:T(8,128)(2,1)S(1)}, bf16[83,256]{1,0:T(8,128)(2,1)S(1)}, u32[]{:S(2)}, u32[]{:S(2)}) %collective-permute-start.2) | collective-permute-done | bytes 42528 | tf_op jit(solution)/shard_map/ppermute | solution.py:34
  72.0 9.8 %collective-permute-done.12.refs_4_.refs_6_ = bf16[256,768]{1,0:T(8,128)(2,1)S(1)} collective-permute-done((bf16[256,768]{1,0:T(8,128)(2,1)S(1)}, bf16[256,768]{1,0:T(8,128)(2,1)S(1)}, u32[]{:S(2)}, u32[]{:S(2)}) %collective-permute-start.12) | collective-permute-done | bytes 393248 | tf_op jit(solution)/shard_map/ppermute | solution.py:34
  94.0 8.4 %collective-permute-done.16.refs_8_.refs_10_ = bf16[256,768]{1,0:T(8,128)(2,1)S(1)} collective-permute-done((bf16[256,768]{1,0:T(8,128)(2,1)S(1)}, bf16[256,768]{1,0:T(8,128)(2,1)S(1)}, u32[]{:S(2)}, u32[]{:S(2)}) %collective-permute-start.16) | collective-permute-done | bytes 393248 | tf_op jit(solution)/shard_map/ppermute | solution.py:34
  102.4 5.5 collective-permute-done.17.refs_9_.refs_11_
  118.5 12.7 %collective-permute-done.22.refs_9_.refs_5_.refs_7_ = bf16[512,256]{1,0:T(8,128)(2,1)S(1)} collective-permute-done((bf16[512,256]{1,0:T(8,128)(2,1)S(1)}, bf16[512,256]{1,0:T(8,128)(2,1)S(1)}, u32[]{:S(2)}, u32[]{:S(2)}) %collective-permute-start.22) | collective-permute-done | bytes 262176 | tf_op jit(solution)/shard_map/ppermute | solution.py:34
  154.5 5.7 collective-permute-done.31.refs_2_
  164.9 5.2 collective-permute-done.35.refs_5_
  174.7 9.3 %collective-permute-done.57.refs_1_ = bf16[64,2176]{1,0:T(8,128)(2,1)S(1)} collective-permute-done((bf16[64,2176]{1,0:T(8,128)(2,1)S(1)}, bf16[64,2176]{1,0:T(8,128)(2,1)S(1)}, u32[]{:S(2)}, u32[]{:S(2)}) %collective-permute-start.57) | collective-permute-done | bytes 278560 | tf_op jit(solution)/shard_map/ppermute | solution.py:34
  186.7 5.8 collective-permute-done.41.refs_11_
  197.3 10.8 %collective-permute-done.61.refs_5_ = bf16[64,2176]{1,0:T(8,128)(2,1)S(1)} collective-permute-done((bf16[64,2176]{1,0:T(8,128)(2,1)S(1)}, bf16[64,2176]{1,0:T(8,128)(2,1)S(1)}, u32[]{:S(2)}, u32[]{:S(2)}) %collective-permute-start.61) | collective-permute-done | bytes 278560 | tf_op jit(solution)/shard_map/ppermute | solution.py:34
  250.7 9.1 %rows_of_slots.3.refs_0_.cot_ref = bf16[8,384,2048]{2,1,0:T(8,128)(2,1)} custom-call(s32[8,8,256]{2,1,0:T(8,128)S(1)} %get-tuple-element.144.refs_0_, bf16[512,2048]{1,0:T(8,128)(2,1)S(1)} %held.4.refs_1_, bf16[512,2048]{1,0:T(8,128)(2,1)S(1)} %copy-done.32, bf16[512,2048]{1,0:T(8,128)(2,1)} %copy-done.131, bf16[512,2048]{1,0:T(8,128)(2,1)} %copy-done.132), custom_call_target="tpu_custom_call" | custom-call | flops 3221 | bytes 20 | tf_op jit(solution)/shard_map/rows_of_slots/pallas_call | solution.py:303
  260.0 10.8 %grad_of_hidden.1.refs_17_.refs_5_ = f32[8,384,256]{2,1,0:T(8,128)S(1)} custom-call(bf16[8,384,2048]{2,1,0:T(8,128)(2,1)} %rows_of_slots.3.refs_0_.cot_ref, bf16[8,256,2048]{2,1,0:T(8,128)(2,1)} %refs_1_.5), custom_call_target="tpu_custom_call" | custom-call | flops 3221 | bytes 24 | tf_op jit(solution)/shard_map/grad_of_hidden/pallas_call | solution.py:376
  278.5 5.1 rows_of_slots.5.refs_2_.b_ref
  283.7 21.9 %expert_step.1 = (bf16[8,384,2176]{2,1,0:T(8,128)(2,1)}, bf16[8,384,256]{2,1,0:T(8,128)(2,1)S(1)}, bf16[8,384,256]{2,1,0:T(8,128)(2,1)S(1)}, bf16[8,384,256]{2,1,0:T(8,128)(2,1)S(1)}) custom-call(s32[1]{0:T(128)} %bitcast.7.refs_0_, bf16[8,192,2176]{2,1,0:T(8,128)(2,1)} %rows_of_slots.4.refs_17_.refs_1_.a_ref, ...), custom_call_target="tpu_custom_call" | custom-call | flops 12884 | bytes 51 | tf_op jit(solution)/shard_map/expert_step/pallas_call | solution.py:376
  305.6 7.0 %tokens_of_slots.4 = (bf16[256,2176]{1,0:T(8,128)(2,1)S(1)}, bf16[256,2176]{1,0:T(8,128)(2,1)}, bf16[256,2176]{1,0:T(8,128)(2,1)S(1)}, bf16[256,2176]{1,0:T(8,128)(2,1)}) custom-call(s32[4,8,256]{2,1,0:T(8,128)S(1)} %get-tuple-element.252.refs_0_, bf16[8,384,2176]{2,1,0:T(8,128)(2,1)} %get-tuple-element.147.refs_1_), custom_call_target="tpu_custom_call" | custom-call | flops 1711 | bytes 11 | tf_op jit(solution)/shard_map/tokens_of_slots/pallas_call | solution.py:340
  313.6 6.2 %tokens_of_slots.5 = (bf16[256,2176]{1,0:T(8,128)(2,1)S(1)}, bf16[256,2176]{1,0:T(8,128)(2,1)}, bf16[256,2176]{1,0:T(8,128)(2,1)S(1)}, bf16[256,2176]{1,0:T(8,128)(2,1)S(1)}) custom-call(s32[4,8,256]{2,1,0:T(8,128)S(1)} %get-tuple-element.253.refs_0_, bf16[8,384,2176]{2,1,0:T(8,128)(2,1)} %get-tuple-element.147.refs_1_, ...), custom_call_target="tpu_custom_call" | custom-call | flops 1711 | bytes 11 | tf_op jit(solution)/shard_map/tokens_of_slots/pallas_call | solution.py:340
  328.9 11.5 %expert_out.1.refs_1_ = bf16[8,384,2048]{2,1,0:T(8,128)(2,1)} custom-call(bf16[8,384,256]{2,1,0:T(8,128)(2,1)S(1)} %get-tuple-element.146.refs_0_.act_ref, bf16[8,256,2048]{2,1,0:T(8,128)(2,1)} %refs_1_.5, bf16[128,2176]{1,0:T(8,128)(2,1)S(1)} %get-tuple-element.150.refs_2_, bf16[128,2176]{1,0:T(8,128)(2,1)S(1)} %get-tuple-element.153.refs_3_, ...), custom_call_target="tpu_custom_call" | custom-call | flops 3221 | bytes 22 | tf_op jit(solution)/shard_map/expert_out/pallas_call | solution.py:376
  340.4 6.3 %tokens_of_slots.6 = (bf16[256,2048]{1,0:T(8,128)(2,1)S(1)}, bf16[256,2048]{1,0:T(8,128)(2,1)}, bf16[256,2048]{1,0:T(8,128)(2,1)S(1)}, bf16[256,2048]{1,0:T(8,128)(2,1)}) custom-call(s32[4,8,256]{2,1,0:T(8,128)S(1)} %get-tuple-element.252.refs_0_, bf16[8,384,2048]{2,1,0:T(8,128)(2,1)} %expert_out.1.refs_1_), custom_call_target="tpu_custom_call" | custom-call | flops 1610 | bytes 10 | tf_op jit(solution)/shard_map/tokens_of_slots/pallas_call | solution.py:340
  355.2 6.1 %tokens_of_slots.7 = (bf16[256,2048]{1,0:T(8,128)(2,1)S(1)}, bf16[256,2048]{1,0:T(8,128)(2,1)}, bf16[256,2048]{1,0:T(8,128)(2,1)S(1)}, bf16[256,2048]{1,0:T(8,128)(2,1)}) custom-call(s32[4,8,256]{2,1,0:T(8,128)S(1)} %get-tuple-element.253.refs_0_, bf16[8,384,2048]{2,1,0:T(8,128)(2,1)} %expert_out.1.refs_1_, bf16[128,2176]{1,0:T(8,128)(2,1)S(1)} %combined.28.refs_2_, ...), custom_call_target="tpu_custom_call" | custom-call | flops 1610 | bytes 10 | tf_op jit(solution)/shard_map/tokens_of_slots/pallas_call | solution.py:340
  363.7 7.9 %expert_weight_grads.4 = (f32[8,2048,256]{2,1,0:T(8,128)}, f32[8,2048,256]{2,1,0:T(8,128)}, f32[8,256,2048]{2,1,0:T(8,128)}, f32[8,128]{1,0:T(8,128)S(1)}) custom-call(bf16[8,192,2176]{2,1,0:T(8,128)(2,1)} %rows_of_slots.4.refs_17_.refs_1_.a_ref, bf16[8,192,2176]{2,1,0:T(8,128)(2,1)} %rows_of_slots.5.refs_2_.b_ref, ...), custom_call_target="tpu_custom_call" | custom-call | flops 2415 | bytes 19 | tf_op jit(solution)/shard_map/expert_weight_grads/pallas_call | solution.py:490
  387.4 16.8 %collective-permute-done.85.refs_2_ = bf16[128,2176]{1,0:T(8,128)(2,1)S(1)} collective-permute-done((bf16[128,2176]{1,0:T(8,128)(2,1)S(1)}, bf16[128,2176]{1,0:T(8,128)(2,1)S(1)}, u32[]{:S(2)}, u32[]{:S(2)}) %collective-permute-start.85) | collective-permute-done | bytes 557088 | tf_op jit(solution)/shard_map/ppermute | solution.py:34
  404.2 7.8 %expert_weight_grads.5 = (f32[8,2048,256]{2,1,0:T(8,128)}, f32[8,2048,256]{2,1,0:T(8,128)}, f32[8,256,2048]{2,1,0:T(8,128)}, f32[8,128]{1,0:T(8,128)S(1)}) custom-call(bf16[8,192,2176]{2,1,0:T(8,128)(2,1)} %rows_of_slots.4.refs_17_.refs_1_.a_ref, ...), custom_call_target="tpu_custom_call", output_to_operand_aliasing={{0}: (6, {}), {1}: (7, {}), {2}: (8, {})} | custom-call | flops 2415 | bytes 19 | tf_op jit(solution)/shard_map/expert_weight_grads/pallas_call | solution.py:490
  415.3 7.3 %collective-permute-done.88.refs_1_ = bf16[64,2176]{1,0:T(8,128)(2,1)S(1)} collective-permute-done((bf16[64,2176]{1,0:T(8,128)(2,1)S(1)}, bf16[64,2176]{1,0:T(8,128)(2,1)S(1)}, u32[]{:S(2)}, u32[]{:S(2)}) %collective-permute-start.88) | collective-permute-done | bytes 278560 | tf_op jit(solution)/shard_map/ppermute | solution.py:34
  425.3 7.4 %collective-permute-done.92.refs_3_.refs_2_ = bf16[64,2048]{1,0:T(8,128)(2,1)S(1)} collective-permute-done((bf16[64,2048]{1,0:T(8,128)(2,1)S(1)}, bf16[64,2048]{1,0:T(8,128)(2,1)S(1)}, u32[]{:S(2)}, u32[]{:S(2)}) %collective-permute-start.92) | collective-permute-done | bytes 262176 | tf_op jit(solution)/shard_map/ppermute | solution.py:34
  471.6 11.1 %collective-permute-done.108.refs_2_ = bf16[128,2048]{1,0:T(8,128)(2,1)S(1)} collective-permute-done((bf16[128,2048]{1,0:T(8,128)(2,1)S(1)}, bf16[128,2048]{1,0:T(8,128)(2,1)S(1)}, u32[]{:S(2)}, u32[]{:S(2)}) %collective-permute-start.108) | collective-permute-done | bytes 524320 | tf_op jit(solution)/shard_map/ppermute | solution.py:34
  486.3 15.9 %collective-permute-done.109.refs_3_ = bf16[64,2048]{1,0:T(8,128)(2,1)S(1)} collective-permute-done((bf16[64,2048]{1,0:T(8,128)(2,1)S(1)}, bf16[64,2048]{1,0:T(8,128)(2,1)S(1)}, u32[]{:S(2)}, u32[]{:S(2)}) %collective-permute-start.109) | collective-permute-done | bytes 262176 | tf_op jit(solution)/shard_map/ppermute | solution.py:34
  507.1 10.7 %collective-permute-done.113.refs_1_ = f32[4,112,256]{2,1,0:T(8,128)S(1)} collective-permute-done((f32[4,112,256]{2,1,0:T(8,128)S(1)}, f32[4,112,256]{2,1,0:T(8,128)S(1)}, u32[]{:S(2)}, u32[]{:S(2)}) %collective-permute-start.113) | collective-permute-done | bytes 458784 | tf_op jit(solution)/shard_map/ppermute | solution.py:34
  518.6 16.0 %collective-permute-done.102.refs_2_ = bf16[64,2048]{1,0:T(8,128)(2,1)S(1)} collective-permute-done((bf16[64,2048]{1,0:T(8,128)(2,1)S(1)}, bf16[64,2048]{1,0:T(8,128)(2,1)S(1)}, u32[]{:S(2)}, u32[]{:S(2)}) %collective-permute-start.102) | collective-permute-done | bytes 262176 | tf_op jit(solution)/shard_map/ppermute | solution.py:34
  539.8 8.1 %expert_weight_grads.6 = (f32[8,2048,256]{2,1,0:T(8,128)}, f32[8,2048,256]{2,1,0:T(8,128)}, f32[8,256,2048]{2,1,0:T(8,128)}, f32[8,128]{1,0:T(8,128)S(1)}) custom-call(bf16[8,192,2176]{2,1,0:T(8,128)(2,1)} %rows_of_slots.4.refs_17_.refs_1_.a_ref, ...), custom_call_target="tpu_custom_call", output_to_operand_aliasing={{0}: (6, {}), {1}: (7, {}), {2}: (8, {})} | custom-call | flops 2415 | bytes 19 | tf_op jit(solution)/shard_map/expert_weight_grads/pallas_call | solution.py:490
  564.0 5.4 collective-permute-done.120.refs_1_
  571.4 20.3 %collective-permute-done.118.refs_1_ = bf16[2,256,768]{2,1,0:T(8,128)(2,1)S(1)} collective-permute-done((bf16[2,256,768]{2,1,0:T(8,128)(2,1)S(1)}, bf16[2,256,768]{2,1,0:T(8,128)(2,1)S(1)}, u32[]{:S(2)}, u32[]{:S(2)}) %collective-permute-start.118) | collective-permute-done | bytes 786464 | tf_op jit(solution)/shard_map/ppermute | solution.py:34
  592.1 7.8 %expert_weight_grads.7 = (f32[8,2048,256]{2,1,0:T(8,128)}, f32[8,2048,256]{2,1,0:T(8,128)}, f32[8,256,2048]{2,1,0:T(8,128)}, f32[8,128]{1,0:T(8,128)}) custom-call(bf16[8,192,2176]{2,1,0:T(8,128)(2,1)} %rows_of_slots.4.refs_17_.refs_1_.a_ref, ...), custom_call_target="tpu_custom_call", output_to_operand_aliasing={{0}: (6, {}), {1}: (7, {}), {2}: (8, {})} | custom-call | flops 2415 | bytes 19 | tf_op jit(solution)/shard_map/expert_weight_grads/pallas_call | solution.py:490
  (586 shorter events, 298.4 us)
Async XLA Ops:
  16.6 30.7 %collective-permute-start.7 = (bf16[256,768]{1,0:T(8,128)(2,1)S(1)}, bf16[256,768]{1,0:T(8,128)(2,1)S(1)}, u32[]{:S(2)}, u32[]{:S(2)}) collective-permute-start(bf16[256,768]{1,0:T(8,128)(2,1)S(1)} %get-tuple-element.127), channel_id=1, source_target_pairs={{0,8},{1,9},{2,10},{3,11},{4,12},{5,13},{6,14},{7,15},{8,0},{9,1},... | collective-permute-start | bytes 1179656 | tf_op jit(solution)/shard_map/ppermute | solution.py:34
  54.9 26.8 %collective-permute-start.12 = (bf16[256,768]{1,0:T(8,128)(2,1)S(1)}, bf16[256,768]{1,0:T(8,128)(2,1)S(1)}, u32[]{:S(2)}, u32[]{:S(2)}) collective-permute-start(bf16[256,768]{1,0:T(8,128)(2,1)S(1)} %get-tuple-element.129.refs_2_.refs_4_), channel_id=1, source_target_pairs={{0,16},{1,17},{2,18},{3,19},{4,20},{5,21},{6,22},{7,23},{8,24},{9,... | collective-permute-start | bytes 1179656 | tf_op jit(solution)/shard_map/ppermute | solution.py:34
  56.8 26.4 %collective-permute-start.14 = (bf16[256,768]{1,0:T(8,128)(2,1)S(1)}, bf16[256,768]{1,0:T(8,128)(2,1)S(1)}, u32[]{:S(2)}, u32[]{:S(2)}) collective-permute-start(bf16[256,768]{1,0:T(8,128)(2,1)S(1)} %get-tuple-element.129.refs_2_.refs_4_), channel_id=1, source_target_pairs={{0,4},{1,5},{2,6},{3,7},{4,0},{5,1},{6,2},{7,3},{8,12},{9,13},{10,... | collective-permute-start | bytes 1179656 | tf_op jit(solution)/shard_map/ppermute | solution.py:34
  61.5 26.2 %collective-permute-start.13 = (bf16[256,768]{1,0:T(8,128)(2,1)S(1)}, bf16[256,768]{1,0:T(8,128)(2,1)S(1)}, u32[]{:S(2)}, u32[]{:S(2)}) collective-permute-start(bf16[256,768]{1,0:T(8,128)(2,1)S(1)} %collective-permute-done.7.refs_9_.refs_3_.refs_5_), channel_id=1, source_target_pairs={{0,16},{1,17},{2,18},{3,19},{4,20},{5,21},{6,22},{7,23},{8,24},{9,... | collective-permute-start | bytes 1179656 | tf_op jit(solution)/shard_map/ppermute | solution.py:34
  81.7 88.9 %collective-permute-start.55 = (bf16[512,2048]{1,0:T(8,128)(2,1)S(1)}, bf16[512,2048]{1,0:T(8,128)(2,1)S(1)}, u32[]{:S(2)}, u32[]{:S(2)}) collective-permute-start(bf16[512,2048]{1,0:T(8,128)(2,1)S(1)} %held.4.refs_1_), channel_id=1, source_target_pairs={{0,2},{1,3},{2,0},{3,1},{4,6},{5,7},{6,4},{7,5},{8,10},{9,11},{10,... | collective-permute-start | bytes 6291464 | tf_op jit(solution)/shard_map/ppermute | solution.py:34
  89.8 24.5 %collective-permute-start.21 = (bf16[512,256]{1,0:T(8,128)(2,1)S(1)}, bf16[512,256]{1,0:T(8,128)(2,1)S(1)}, u32[]{:S(2)}, u32[]{:S(2)}) collective-permute-start(bf16[512,256]{1,0:T(8,128)(2,1)S(1)} %held.3.refs_7_.refs_3_.refs_5_), channel_id=1, source_target_pairs={{0,8},{1,9},{2,10},{3,11},{4,12},{5,13},{6,14},{7,15},{8,0},{9,1},... | collective-permute-start | bytes 786440 | tf_op jit(solution)/shard_map/ppermute | solution.py:34
  116.0 25.0 %collective-permute-start.25 = (bf16[512,256]{1,0:T(8,128)(2,1)S(1)}, bf16[512,256]{1,0:T(8,128)(2,1)S(1)}, u32[]{:S(2)}, u32[]{:S(2)}) collective-permute-start(bf16[512,256]{1,0:T(8,128)(2,1)S(1)} %held.3.refs_7_.refs_3_.refs_5_), channel_id=1, source_target_pairs={{0,4},{1,5},{2,6},{3,7},{4,0},{5,1},{6,2},{7,3},{8,12},{9,13},{10,... | collective-permute-start | bytes 786440 | tf_op jit(solution)/shard_map/ppermute | solution.py:34
  170.6 69.6 %collective-permute-start.54 = (bf16[512,2048]{1,0:T(8,128)(2,1)S(1)}, bf16[512,2048]{1,0:T(8,128)(2,1)S(1)}, u32[]{:S(2)}, u32[]{:S(2)}) collective-permute-start(bf16[512,2048]{1,0:T(8,128)(2,1)S(1)} %held.4.refs_1_), channel_id=1, source_target_pairs={{0,1},{1,0},{2,3},{3,2},{4,5},{5,4},{6,7},{7,6},{8,9},{9,8},{10,11... | collective-permute-start | bytes 6291464 | tf_op jit(solution)/shard_map/ppermute | solution.py:34
  170.6 76.7 %collective-permute-start.56 = (bf16[512,2048]{1,0:T(8,128)(2,1)S(1)}, bf16[512,2048]{1,0:T(8,128)(2,1)S(1)}, u32[]{:S(2)}, u32[]{:S(2)}) collective-permute-start(bf16[512,2048]{1,0:T(8,128)(2,1)S(1)} %collective-permute-done.55.refs_3_), channel_id=1, source_target_pairs={{0,1},{1,0},{2,3},{3,2},{4,5},{5,4},{6,7},{7,6},{8,9},{9,8},{10,11... | collective-permute-start | bytes 6291464 | tf_op jit(solution)/shard_map/ppermute | solution.py:34
  240.0 38.5 %collective-permute-start.66 = (bf16[64,2176]{1,0:T(8,128)(2,1)}, bf16[64,2176]{1,0:T(8,128)(2,1)}, u32[]{:S(2)}, u32[]{:S(2)}) collective-permute-start(bf16[64,2176]{1,0:T(8,128)(2,1)} %collective-permute-done.65.refs_9_), channel_id=1, source_target_pairs={{0,1},{1,0},{2,3},{3,2},{4,5},{5,4},{6,7},{7,6},{8,9},{9,8},{10,11... | collective-permute-start | bytes 835592 | tf_op jit(solution)/shard_map/ppermute | solution.py:34
  241.5 36.9 %collective-permute-start.64 = (bf16[64,2176]{1,0:T(8,128)(2,1)}, bf16[64,2176]{1,0:T(8,128)(2,1)}, u32[]{:S(2)}, u32[]{:S(2)}) collective-permute-start(bf16[64,2176]{1,0:T(8,128)(2,1)} %collective-permute-done.63.refs_7_), channel_id=1, source_target_pairs={{0,1},{1,0},{2,3},{3,2},{4,5},{5,4},{6,7},{7,6},{8,9},{9,8},{10,11... | collective-permute-start | bytes 835592 | tf_op jit(solution)/shard_map/ppermute | solution.py:34
  242.6 35.9 %collective-permute-start.68 = (bf16[64,2176]{1,0:T(8,128)(2,1)}, bf16[64,2176]{1,0:T(8,128)(2,1)}, u32[]{:S(2)}, u32[]{:S(2)}) collective-permute-start(bf16[64,2176]{1,0:T(8,128)(2,1)} %collective-permute-done.67.refs_11_), channel_id=1, source_target_pairs={{0,1},{1,0},{2,3},{3,2},{4,5},{5,4},{6,7},{7,6},{8,9},{9,8},{10,11... | collective-permute-start | bytes 835592 | tf_op jit(solution)/shard_map/ppermute | solution.py:34
  247.3 31.2 %collective-permute-start.70 = (bf16[64,2176]{1,0:T(8,128)(2,1)}, bf16[64,2176]{1,0:T(8,128)(2,1)}, u32[]{:S(2)}, u32[]{:S(2)}) collective-permute-start(bf16[64,2176]{1,0:T(8,128)(2,1)} %collective-permute-done.69.refs_13_), channel_id=1, source_target_pairs={{0,1},{1,0},{2,3},{3,2},{4,5},{5,4},{6,7},{7,6},{8,9},{9,8},{10,11... | collective-permute-start | bytes 835592 | tf_op jit(solution)/shard_map/ppermute | solution.py:34
  248.6 29.8 %collective-permute-start.72 = (bf16[64,2176]{1,0:T(8,128)(2,1)}, bf16[64,2176]{1,0:T(8,128)(2,1)}, u32[]{:S(2)}, u32[]{:S(2)}) collective-permute-start(bf16[64,2176]{1,0:T(8,128)(2,1)} %collective-permute-done.71.refs_15_), channel_id=1, source_target_pairs={{0,1},{1,0},{2,3},{3,2},{4,5},{5,4},{6,7},{7,6},{8,9},{9,8},{10,11... | collective-permute-start | bytes 835592 | tf_op jit(solution)/shard_map/ppermute | solution.py:34
  320.4 29.9 %collective-permute-start.77 = (bf16[256,2176]{1,0:T(8,128)(2,1)}, bf16[256,2176]{1,0:T(8,128)(2,1)S(1)}, u32[]{:S(2)}, u32[]{:S(2)}) collective-permute-start(bf16[256,2176]{1,0:T(8,128)(2,1)} %get-tuple-element.159), channel_id=1, source_target_pairs={{0,1},{1,0},{2,3},{3,2},{4,5},{5,4},{6,7},{7,6},{8,9},{9,8},{10,11... | collective-permute-start | bytes 3342344 | tf_op jit(solution)/shard_map/ppermute | solution.py:34
  324.7 26.7 %collective-permute-start.78 = (bf16[256,2176]{1,0:T(8,128)(2,1)S(1)}, bf16[256,2176]{1,0:T(8,128)(2,1)S(1)}, u32[]{:S(2)}, u32[]{:S(2)}) collective-permute-start(bf16[256,2176]{1,0:T(8,128)(2,1)S(1)} %combined.27.refs_4_), channel_id=1, source_target_pairs={{0,2},{1,3},{2,0},{3,1},{4,6},{5,7},{6,4},{7,5},{8,10},{9,11},{10,... | collective-permute-start | bytes 3342344 | tf_op jit(solution)/shard_map/ppermute | solution.py:34
  377.9 26.2 %collective-permute-start.85 = (bf16[128,2176]{1,0:T(8,128)(2,1)S(1)}, bf16[128,2176]{1,0:T(8,128)(2,1)S(1)}, u32[]{:S(2)}, u32[]{:S(2)}) collective-permute-start(bf16[128,2176]{1,0:T(8,128)(2,1)S(1)} %combined.30.refs_2_), channel_id=1, source_target_pairs={{0,16},{1,17},{2,18},{3,19},{4,20},{5,21},{6,22},{7,23},{8,24},{9,... | collective-permute-start | bytes 1671176 | tf_op jit(solution)/shard_map/ppermute | solution.py:34
  378.4 44.2 %collective-permute-start.83 = (bf16[256,2048]{1,0:T(8,128)(2,1)S(1)}, bf16[256,2048]{1,0:T(8,128)(2,1)S(1)}, u32[]{:S(2)}, u32[]{:S(2)}) collective-permute-start(bf16[256,2048]{1,0:T(8,128)(2,1)S(1)} %combined.31.refs_6_), channel_id=1, source_target_pairs={{0,2},{1,3},{2,0},{3,1},{4,6},{5,7},{6,4},{7,5},{8,10},{9,11},{10,... | collective-permute-start | bytes 3145736 | tf_op jit(solution)/shard_map/ppermute | solution.py:34
  379.0 33.0 %collective-permute-start.84 = (bf16[128,2176]{1,0:T(8,128)(2,1)}, bf16[128,2176]{1,0:T(8,128)(2,1)}, u32[]{:S(2)}, u32[]{:S(2)}) collective-permute-start(bf16[128,2176]{1,0:T(8,128)(2,1)} %get-tuple-element.160.refs_3_), channel_id=1, source_target_pairs={{0,4},{1,5},{2,6},{3,7},{4,0},{5,1},{6,2},{7,3},{8,12},{9,13},{10,... | collective-permute-start | bytes 1671176 | tf_op jit(solution)/shard_map/ppermute | solution.py:34
  383.0 30.6 %collective-permute-start.90 = (bf16[128,2048]{1,0:T(8,128)(2,1)}, bf16[128,2048]{1,0:T(8,128)(2,1)S(1)}, u32[]{:S(2)}, u32[]{:S(2)}) collective-permute-start(bf16[128,2048]{1,0:T(8,128)(2,1)} %get-tuple-element.177.refs_5_), channel_id=1, source_target_pairs={{0,4},{1,5},{2,6},{3,7},{4,0},{5,1},{6,2},{7,3},{8,12},{9,13},{10,... | collective-permute-start | bytes 1572872 | tf_op jit(solution)/shard_map/ppermute | solution.py:34
  386.7 28.6 %collective-permute-start.89 = (bf16[128,2048]{1,0:T(8,128)(2,1)}, bf16[128,2048]{1,0:T(8,128)(2,1)S(1)}, u32[]{:S(2)}, u32[]{:S(2)}) collective-permute-start(bf16[128,2048]{1,0:T(8,128)(2,1)} %get-tuple-element.174.refs_4_), channel_id=1, source_target_pairs={{0,4},{1,5},{2,6},{3,7},{4,0},{5,1},{6,2},{7,3},{8,12},{9,13},{10,... | collective-permute-start | bytes 1572872 | tf_op jit(solution)/shard_map/ppermute | solution.py:34
  404.2 32.7 %collective-permute-start.79 = (bf16[256,2048]{1,0:T(8,128)(2,1)}, bf16[256,2048]{1,0:T(8,128)(2,1)S(1)}, u32[]{:S(2)}, u32[]{:S(2)}) collective-permute-start(bf16[256,2048]{1,0:T(8,128)(2,1)} %get-tuple-element.162), channel_id=1, source_target_pairs={{0,1},{1,0},{2,3},{3,2},{4,5},{5,4},{6,7},{7,6},{8,9},{9,8},{10,11... | collective-permute-start | bytes 3145736 | tf_op jit(solution)/shard_map/ppermute | solution.py:34
  460.9 43.4 %collective-permute-start.101 = (bf16[4,256,768]{2,1,0:T(8,128)(2,1)S(1)}, bf16[4,256,768]{2,1,0:T(8,128)(2,1)S(1)}, u32[]{:S(2)}, u32[]{:S(2)}) collective-permute-start(bf16[4,256,768]{2,1,0:T(8,128)(2,1)S(1)} %get-tuple-element.198.refs_12_), channel_id=1, source_target_pairs={{0,4},{1,5},{2,6},{3,7},{4,0},{5,1},{6,2},{7,3},{8,12},{9,13},{10,... | collective-permute-start | bytes 4718600 | tf_op jit(solution)/shard_map/ppermute | solution.py:34
  470.6 33.7 %collective-permute-start.97 = (bf16[128,2048]{1,0:T(8,128)(2,1)S(1)}, bf16[128,2048]{1,0:T(8,128)(2,1)S(1)}, u32[]{:S(2)}, u32[]{:S(2)}) collective-permute-start(bf16[128,2048]{1,0:T(8,128)(2,1)S(1)} %combined.37), channel_id=1, source_target_pairs={{0,16},{1,17},{2,18},{3,19},{4,20},{5,21},{6,22},{7,23},{8,24},{9,... | collective-permute-start | bytes 1572872 | tf_op jit(solution)/shard_map/ppermute | solution.py:34
  484.7 63.3 %collective-permute-start.119 = (bf16[256,2048]{1,0:T(8,128)(2,1)}, bf16[256,2048]{1,0:T(8,128)(2,1)}, u32[]{:S(2)}, u32[]{:S(2)}) collective-permute-start(bf16[256,2048]{1,0:T(8,128)(2,1)} %held.5), channel_id=1, source_target_pairs={{0,8},{1,9},{2,10},{3,11},{4,12},{5,13},{6,14},{7,15},{8,0},{9,1},... | collective-permute-start | bytes 3145736 | tf_op jit(solution)/shard_map/ppermute | solution.py:34
  503.7 32.8 %collective-permute-start.110 = (f32[64,2048]{1,0:T(8,128)}, f32[64,2048]{1,0:T(8,128)}, u32[]{:S(2)}, u32[]{:S(2)}) collective-permute-start(f32[64,2048]{1,0:T(8,128)} %get-tuple-element.207), channel_id=1, source_target_pairs={{0,2},{1,3},{2,0},{3,1},{4,6},{5,7},{6,4},{7,5},{8,10},{9,11},{10,... | collective-permute-start | bytes 1572872 | tf_op jit(solution)/shard_map/ppermute | solution.py:34
  507.0 27.6 %collective-permute-start.102 = (bf16[64,2048]{1,0:T(8,128)(2,1)S(1)}, bf16[64,2048]{1,0:T(8,128)(2,1)S(1)}, u32[]{:S(2)}, u32[]{:S(2)}) collective-permute-start(bf16[64,2048]{1,0:T(8,128)(2,1)S(1)} %get-tuple-element.201), channel_id=1, source_target_pairs={{0,8},{1,9},{2,10},{3,11},{4,12},{5,13},{6,14},{7,15},{8,0},{9,1},... | collective-permute-start | bytes 786440 | tf_op jit(solution)/shard_map/ppermute | solution.py:34
  518.5 36.4 %collective-permute-start.112 = (f32[64,2048]{1,0:T(8,128)}, f32[64,2048]{1,0:T(8,128)}, u32[]{:S(2)}, u32[]{:S(2)}) collective-permute-start(f32[64,2048]{1,0:T(8,128)} %get-tuple-element.207), channel_id=1, source_target_pairs={{0,1},{1,0},{2,3},{3,2},{4,5},{5,4},{6,7},{7,6},{8,9},{9,8},{10,11... | collective-permute-start | bytes 1572872 | tf_op jit(solution)/shard_map/ppermute | solution.py:34
  547.9 43.8 %collective-permute-start.118 = (bf16[2,256,768]{2,1,0:T(8,128)(2,1)S(1)}, bf16[2,256,768]{2,1,0:T(8,128)(2,1)S(1)}, u32[]{:S(2)}, u32[]{:S(2)}) collective-permute-start(bf16[2,256,768]{2,1,0:T(8,128)(2,1)S(1)} %copy-done.6), channel_id=1, source_target_pairs={{0,16},{1,17},{2,18},{3,19},{4,20},{5,21},{6,22},{7,23},{8,24},{9,... | collective-permute-start | bytes 2359304 | tf_op jit(solution)/shard_map/ppermute | solution.py:34
  553.9 48.2 %collective-permute-start.105 = (f32[64,2048]{1,0:T(8,128)}, f32[64,2048]{1,0:T(8,128)S(1)}, u32[]{:S(2)}, u32[]{:S(2)}) collective-permute-start(f32[64,2048]{1,0:T(8,128)} %combined.40), channel_id=1, source_target_pairs={{0,1},{1,0},{2,3},{3,2},{4,5},{5,4},{6,7},{7,6},{8,9},{9,8},{10,11... | collective-permute-start | bytes 1572872 | tf_op jit(solution)/shard_map/ppermute | solution.py:34
  555.6 46.5 %collective-permute-start.104 = (f32[64,2048]{1,0:T(8,128)}, f32[64,2048]{1,0:T(8,128)S(1)}, u32[]{:S(2)}, u32[]{:S(2)}) collective-permute-start(f32[64,2048]{1,0:T(8,128)} %collective-permute-done.103), channel_id=1, source_target_pairs={{0,1},{1,0},{2,3},{3,2},{4,5},{5,4},{6,7},{7,6},{8,9},{9,8},{10,11... | collective-permute-start | bytes 1572872 | tf_op jit(solution)/shard_map/ppermute | solution.py:34
  569.5 30.4 %collective-permute-start.122 = (bf16[2,256,256]{2,1,0:T(8,128)(2,1)S(1)}, bf16[2,256,256]{2,1,0:T(8,128)(2,1)S(1)}, u32[]{:S(2)}, u32[]{:S(2)}) collective-permute-start(bf16[2,256,256]{2,1,0:T(8,128)(2,1)S(1)} %get-tuple-element.225.refs_2_.refs_4_), channel_id=1, source_target_pairs={{0,16},{1,17},{2,18},{3,19},{4,20},{5,21},{6,22},{7,23},{8,24},{9,... | collective-permute-start | bytes 786440 | tf_op jit(solution)/shard_map/ppermute | solution.py:34
  (226 other events, 2741.8 us)

commit v4 on v3

--- a/solution.py
+++ b/solution.py
@@ -85,11 +85,15 @@
     return line + [over_y(v) for v in line]
 
 
-def gather_all(values):
-    line = gather_line([values], z_bits())
+def gather_all(values, first_wait, second_wait):
+    *bits, high = z_bits()
+    line = gather_line([values], bits)
+    going = [values] + [held([v], v.dtype, first_wait) for v in line[1:]]
+    over = [over_z(v, high) for v in going]
+    line = line + over[:-1] + [held(over[-1:], values.dtype, second_wait)]
     pairs = {}
     for mask, near in zip(masks_of([2 * bit for bit in z_bits()]), line, strict=True):
-        if mask & 2 * z_bits()[-1]:
+        if mask & 2 * high:
             aside = over_x(near)
             pairs[mask], pairs[mask + 1] = (near, aside), (over_y(near), over_y(aside))
         else:
@@ -304,7 +308,8 @@
         without(kernel, 1 + len(flat), len(waits)),
         grid=(sequences,),
         in_specs=[pl.BlockSpec((1, experts, tokens), lambda s: (s, 0, 0))]
-        + [pl.BlockSpec(memory_space=pl.ANY)] * (len(flat) + len(waits)),
+        + [pl.BlockSpec(memory_space=pltpu.HBM)] * len(flat)
+        + [pl.BlockSpec(memory_space=pl.ANY)] * len(waits),
         out_specs=pl.BlockSpec((experts, CAP, width), lambda s: (0, s, 0)),
         out_shape=jax.ShapeDtypeStruct((experts, sequences * CAP, width), bf16),
         scratch_shapes=[
@@ -1263,9 +1268,8 @@
     normed_one = (hidden_in * first_scale * gain_one).astype(bf16)
     mates = gather_tp(over_z(own(normed_one), 1))
     x_slabs = paired([normed_one], mates, places, data_size)
-    cot_all = gather_tp(held(cot_line, bf16, [mates[2]]))
-    cot_rows = rows_of_slots(cot_all, table, [], token_order)
-    hidden_grad = grad_of_hidden(cot_rows, down_weight)
+    cot_near = held(cot_line, bf16, [mates[2]])
+    cot_far = over_x(cot_near)
     projected, values, squares = project(
         x_slabs, head_pieces, places
     )
@@ -1277,7 +1281,11 @@
     middle, x_piece, probs = route(scatter_tp(parts)[0], hidden_own, gain_two, router)
 
     picks = (slice(0, half), slice(half, None))
-    x_pieces = gather_all(x_piece)
+    cot_far = held([cot_far], bf16, [x_piece])
+    cot_all = [cot_near, over_core(cot_near), cot_far, over_core(cot_far)]
+    cot_rows = rows_of_slots(cot_all, table, [], token_order)
+    hidden_grad = grad_of_hidden(cot_rows, down_weight)
+    x_pieces = gather_all(x_piece, [cot_rows], [hidden_grad])
     x_first = rows_of_slots(x_pieces[picks[0]], table[picks[0]], [hidden_grad])
     x_halves = [x_first, rows_of_slots(x_pieces[picks[1]], table[picks[1]], [x_first])]
     back_rows, act, gate_grad, up_grad = expert_step(

time: 621 us -> 613 us (0.987)
  waiting for transfers between devices: 278 us -> 262 us
  local copies, waits for them, and re-layouts: 43.6 us -> 52.4 us
    ppermute x124, waiting for transfers between devices: 278 us -> 262 us  [swap(): return lax.ppermute(values, ('dp', 'tp'), pairs)]
    unnamed x268 -> x280, local copies, waits for them, and re-layouts: 37 us -> 45.7 us
    pallas_call x46 -> x49, Pallas kernels: 55.9 us -> 57.1 us  [kernel_call(): pl.pallas_call(body, in_specs=[pl.BlockSpec(memory_space=pltpu.SMEM)] * l...]
  transfers between devices with their start and end apart: 124 -> 124, of which waited for: 50 -> 47; matrix products, arithmetic and copies ran while one was open for 3% -> 3% of each run, Pallas kernels for 20% -> 21%
where the time goes in v4:
time: 613 us; the launch traced here: 603 us
  waiting for transfers between devices  262 us (43%)
  Pallas kernels  178 us (29%)
  starting transfers between devices  92.9 us (15%)
  local copies, waits for them, and re-layouts  52.4 us (9%)
  other arithmetic  14.3 us (2%)
    ppermute x124, waiting for transfers between devices, swap(): return lax.ppermute(values, ('dp', 'tp'), pairs)  262 us
    ppermute x124, starting transfers between devices, swap(): return lax.ppermute(values, ('dp', 'tp'), pairs)  92.9 us
    pallas_call x49, Pallas kernels, kernel_call(): pl.pallas_call(body, in_specs=[pl.BlockSpec(memory_space=pltpu.SMEM)] * l...  57.1 us
    unnamed x280, local copies, waits for them, and re-layouts  45.7 us
    pallas_call x3, Pallas kernels, per_expert(): pl.pallas_call(without(kernel, len(in_specs), len(waits)), grid=(experts,...  44 us
    pallas_call x4, Pallas kernels, expert_weight_grads(): pl.pallas_call(kernel, grid=(count,), in_specs=[block(rows // 2, width)]...  31.6 us
    pallas_call x4, Pallas kernels, tokens_of_slots(): pl.pallas_call(without(kernel, 2, len(waits)), grid=(sequences,), in_spec...  25.6 us
    pallas_call x3, Pallas kernels, rows_of_slots(): pl.pallas_call(without(kernel, 1 + len(flat), len(waits)), grid=(sequence...  20.1 us
  transfers between devices with their start and end apart: 124, of which 47 were waited for; matrix products, arithmetic and copies ran while one was open for 3% of the time, Pallas kernels for 21%

profile of v4, /device:TPU:0, one launch (start us, length us, event | category | flops | bytes accessed | tf_op | source)
XLA Modules:
  0.0 603.0 jit_solution(16819376429213321394)
XLA Ops:
  24.9 6.3 %collective-permute-done.2.refs_4_ = bf16[83,256]{1,0:T(8,128)(2,1)S(1)} collective-permute-done((bf16[83,256]{1,0:T(8,128)(2,1)S(1)}, bf16[83,256]{1,0:T(8,128)(2,1)S(1)}, u32[]{:S(2)}, u32[]{:S(2)}) %collective-permute-start.2) | collective-permute-done | bytes 42528 | tf_op jit(solution)/shard_map/ppermute | solution.py:34
  43.0 8.6 %collective-permute-done.48.refs_2_ = bf16[64,2048]{1,0:T(8,128)(2,1)S(1)} collective-permute-done((bf16[64,2048]{1,0:T(8,128)(2,1)S(1)}, bf16[64,2048]{1,0:T(8,128)(2,1)S(1)}, u32[]{:S(2)}, u32[]{:S(2)}) %collective-permute-start.48) | collective-permute-done | bytes 262176 | tf_op jit(solution)/shard_map/ppermute | solution.py:34
  67.1 16.7 %collective-permute-done.12.refs_4_.refs_6_ = bf16[256,768]{1,0:T(8,128)(2,1)S(1)} collective-permute-done((bf16[256,768]{1,0:T(8,128)(2,1)S(1)}, bf16[256,768]{1,0:T(8,128)(2,1)S(1)}, u32[]{:S(2)}, u32[]{:S(2)}) %collective-permute-start.12) | collective-permute-done | bytes 393248 | tf_op jit(solution)/shard_map/ppermute | solution.py:34
  85.4 6.8 %collective-permute-done.13.refs_5_.refs_1_.refs_7_ = bf16[256,768]{1,0:T(8,128)(2,1)S(1)} collective-permute-done((bf16[256,768]{1,0:T(8,128)(2,1)S(1)}, bf16[256,768]{1,0:T(8,128)(2,1)S(1)}, u32[]{:S(2)}, u32[]{:S(2)}) %collective-permute-start.13) | collective-permute-done | bytes 393248 | tf_op jit(solution)/shard_map/ppermute | solution.py:34
  95.8 8.4 %collective-permute-done.16.refs_8_.refs_10_ = bf16[256,768]{1,0:T(8,128)(2,1)S(1)} collective-permute-done((bf16[256,768]{1,0:T(8,128)(2,1)S(1)}, bf16[256,768]{1,0:T(8,128)(2,1)S(1)}, u32[]{:S(2)}, u32[]{:S(2)}) %collective-permute-start.16) | collective-permute-done | bytes 393248 | tf_op jit(solution)/shard_map/ppermute | solution.py:34
  104.2 8.0 %collective-permute-done.17.refs_9_.refs_11_ = bf16[256,768]{1,0:T(8,128)(2,1)S(1)} collective-permute-done((bf16[256,768]{1,0:T(8,128)(2,1)S(1)}, bf16[256,768]{1,0:T(8,128)(2,1)S(1)}, u32[]{:S(2)}, u32[]{:S(2)}) %collective-permute-start.17) | collective-permute-done | bytes 393248 | tf_op jit(solution)/shard_map/ppermute | solution.py:34
  123.9 14.1 %collective-permute-done.22.refs_9_.refs_5_.refs_7_ = bf16[512,256]{1,0:T(8,128)(2,1)S(1)} collective-permute-done((bf16[512,256]{1,0:T(8,128)(2,1)S(1)}, bf16[512,256]{1,0:T(8,128)(2,1)S(1)}, u32[]{:S(2)}, u32[]{:S(2)}) %collective-permute-start.22) | collective-permute-done | bytes 262176 | tf_op jit(solution)/shard_map/ppermute | solution.py:34
  147.2 5.6 collective-permute-done.27.refs_9_.refs_11_
  162.8 6.6 %collective-permute-done.31.refs_2_ = bf16[64,2048]{1,0:T(8,128)(2,1)S(1)} collective-permute-done((bf16[64,2048]{1,0:T(8,128)(2,1)S(1)}, bf16[64,2048]{1,0:T(8,128)(2,1)S(1)}, u32[]{:S(2)}, u32[]{:S(2)}) %collective-permute-start.31) | collective-permute-done | bytes 262176 | tf_op jit(solution)/shard_map/ppermute | solution.py:34
  172.4 8.1 %collective-permute-done.35.refs_5_.refs_0_ = bf16[64,2176]{1,0:T(8,128)(2,1)S(1)} collective-permute-done((bf16[64,2176]{1,0:T(8,128)(2,1)S(1)}, bf16[64,2176]{1,0:T(8,128)(2,1)S(1)}, u32[]{:S(2)}, u32[]{:S(2)}) %collective-permute-start.35) | collective-permute-done | bytes 278560 | tf_op jit(solution)/shard_map/ppermute | solution.py:34
  182.2 9.6 %rows_of_slots.3.refs_0_.refs_1_.cot_ref = bf16[8,384,2048]{2,1,0:T(8,128)(2,1)} custom-call(s32[8,8,256]{2,1,0:T(8,128)S(1)} %get-tuple-element.144.refs_0_, bf16[512,2048]{1,0:T(8,128)(2,1)S(1)} %held.7.refs_1_, bf16[512,2048]{1,0:T(8,128)(2,1)S(1)} %collective-permute-done.54.refs_2_, bf16[512,2048]{1,0:T(8,128)(2,1)} %copy-done.10, ...), custom_call_target="tpu_custom_call" | custom-call | flops 3221 | bytes 20 | tf_op jit(solution)/shard_map/rows_of_slots/pallas_call | solution.py:307
  215.2 10.6 %grad_of_hidden.1.refs_17_.refs_1_.refs_5_ = f32[8,384,256]{2,1,0:T(8,128)S(1)} custom-call(bf16[8,384,2048]{2,1,0:T(8,128)(2,1)} %rows_of_slots.3.refs_0_.refs_1_.cot_ref, bf16[8,256,2048]{2,1,0:T(8,128)(2,1)} %refs_1_.5), custom_call_target="tpu_custom_call" | custom-call | flops 3221 | bytes 24 | tf_op jit(solution)/shard_map/grad_of_hidden/pallas_call | solution.py:381
  268.0 5.2 rows_of_slots.4.refs_17_.refs_1_.a_ref
  273.4 5.2 rows_of_slots.5.refs_2_.b_ref
  278.6 21.9 %expert_step.1 = (bf16[8,384,2176]{2,1,0:T(8,128)(2,1)}, bf16[8,384,256]{2,1,0:T(8,128)(2,1)S(1)}, bf16[8,384,256]{2,1,0:T(8,128)(2,1)S(1)}, bf16[8,384,256]{2,1,0:T(8,128)(2,1)S(1)}) custom-call(s32[1]{0:T(128)} %bitcast.7.refs_0_, bf16[8,192,2176]{2,1,0:T(8,128)(2,1)} %rows_of_slots.4.refs_17_.refs_1_.a_ref, ...), custom_call_target="tpu_custom_call" | custom-call | flops 12884 | bytes 51 | tf_op jit(solution)/shard_map/expert_step/pallas_call | solution.py:381
  300.5 7.0 %tokens_of_slots.4 = (bf16[256,2176]{1,0:T(8,128)(2,1)S(1)}, bf16[256,2176]{1,0:T(8,128)(2,1)}, bf16[256,2176]{1,0:T(8,128)(2,1)S(1)}, bf16[256,2176]{1,0:T(8,128)(2,1)}) custom-call(s32[4,8,256]{2,1,0:T(8,128)S(1)} %get-tuple-element.252.refs_0_, bf16[8,384,2176]{2,1,0:T(8,128)(2,1)} %get-tuple-element.147.refs_1_), custom_call_target="tpu_custom_call" | custom-call | flops 1711 | bytes 11 | tf_op jit(solution)/shard_map/tokens_of_slots/pallas_call | solution.py:345
  308.5 6.2 %tokens_of_slots.5 = (bf16[256,2176]{1,0:T(8,128)(2,1)S(1)}, bf16[256,2176]{1,0:T(8,128)(2,1)}, bf16[256,2176]{1,0:T(8,128)(2,1)S(1)}, bf16[256,2176]{1,0:T(8,128)(2,1)S(1)}) custom-call(s32[4,8,256]{2,1,0:T(8,128)S(1)} %get-tuple-element.253.refs_0_, bf16[8,384,2176]{2,1,0:T(8,128)(2,1)} %get-tuple-element.147.refs_1_, ...), custom_call_target="tpu_custom_call" | custom-call | flops 1711 | bytes 11 | tf_op jit(solution)/shard_map/tokens_of_slots/pallas_call | solution.py:345
  324.2 11.5 %expert_out.1.refs_1_ = bf16[8,384,2048]{2,1,0:T(8,128)(2,1)} custom-call(bf16[8,384,256]{2,1,0:T(8,128)(2,1)S(1)} %get-tuple-element.146.refs_0_.act_ref, bf16[8,256,2048]{2,1,0:T(8,128)(2,1)} %refs_1_.5, bf16[128,2176]{1,0:T(8,128)(2,1)S(1)} %get-tuple-element.150.refs_2_, bf16[128,2176]{1,0:T(8,128)(2,1)S(1)} %get-tuple-element.153.refs_3_, ...), custom_call_target="tpu_custom_call" | custom-call | flops 3221 | bytes 22 | tf_op jit(solution)/shard_map/expert_out/pallas_call | solution.py:381
  335.6 6.1 %tokens_of_slots.6 = (bf16[256,2048]{1,0:T(8,128)(2,1)S(1)}, bf16[256,2048]{1,0:T(8,128)(2,1)}, bf16[256,2048]{1,0:T(8,128)(2,1)S(1)}, bf16[256,2048]{1,0:T(8,128)(2,1)}) custom-call(s32[4,8,256]{2,1,0:T(8,128)S(1)} %get-tuple-element.252.refs_0_, bf16[8,384,2048]{2,1,0:T(8,128)(2,1)} %expert_out.1.refs_1_), custom_call_target="tpu_custom_call" | custom-call | flops 1610 | bytes 10 | tf_op jit(solution)/shard_map/tokens_of_slots/pallas_call | solution.py:345
  350.4 6.3 %tokens_of_slots.7 = (bf16[256,2048]{1,0:T(8,128)(2,1)S(1)}, bf16[256,2048]{1,0:T(8,128)(2,1)}, bf16[256,2048]{1,0:T(8,128)(2,1)S(1)}, bf16[256,2048]{1,0:T(8,128)(2,1)}) custom-call(s32[4,8,256]{2,1,0:T(8,128)S(1)} %get-tuple-element.253.refs_0_, bf16[8,384,2048]{2,1,0:T(8,128)(2,1)} %expert_out.1.refs_1_, bf16[128,2176]{1,0:T(8,128)(2,1)S(1)} %combined.28.refs_2_, ...), custom_call_target="tpu_custom_call" | custom-call | flops 1610 | bytes 10 | tf_op jit(solution)/shard_map/tokens_of_slots/pallas_call | solution.py:345
  359.3 7.9 %expert_weight_grads.4 = (f32[8,2048,256]{2,1,0:T(8,128)}, f32[8,2048,256]{2,1,0:T(8,128)}, f32[8,256,2048]{2,1,0:T(8,128)}, f32[8,128]{1,0:T(8,128)S(1)}) custom-call(bf16[8,192,2176]{2,1,0:T(8,128)(2,1)} %rows_of_slots.4.refs_17_.refs_1_.a_ref, bf16[8,192,2176]{2,1,0:T(8,128)(2,1)} %rows_of_slots.5.refs_2_.b_ref, ...), custom_call_target="tpu_custom_call" | custom-call | flops 2415 | bytes 19 | tf_op jit(solution)/shard_map/expert_weight_grads/pallas_call | solution.py:495
  383.9 15.6 %collective-permute-done.85.refs_2_ = bf16[128,2176]{1,0:T(8,128)(2,1)S(1)} collective-permute-done((bf16[128,2176]{1,0:T(8,128)(2,1)S(1)}, bf16[128,2176]{1,0:T(8,128)(2,1)S(1)}, u32[]{:S(2)}, u32[]{:S(2)}) %collective-permute-start.85) | collective-permute-done | bytes 557088 | tf_op jit(solution)/shard_map/ppermute | solution.py:34
  399.6 7.8 %expert_weight_grads.5 = (f32[8,2048,256]{2,1,0:T(8,128)}, f32[8,2048,256]{2,1,0:T(8,128)}, f32[8,256,2048]{2,1,0:T(8,128)}, f32[8,128]{1,0:T(8,128)S(1)}) custom-call(bf16[8,192,2176]{2,1,0:T(8,128)(2,1)} %rows_of_slots.4.refs_17_.refs_1_.a_ref, ...), custom_call_target="tpu_custom_call", output_to_operand_aliasing={{0}: (6, {}), {1}: (7, {}), {2}: (8, {})} | custom-call | flops 2415 | bytes 19 | tf_op jit(solution)/shard_map/expert_weight_grads/pallas_call | solution.py:495
  411.7 6.3 %collective-permute-done.88.refs_1_ = bf16[64,2176]{1,0:T(8,128)(2,1)S(1)} collective-permute-done((bf16[64,2176]{1,0:T(8,128)(2,1)S(1)}, bf16[64,2176]{1,0:T(8,128)(2,1)S(1)}, u32[]{:S(2)}, u32[]{:S(2)}) %collective-permute-start.88) | collective-permute-done | bytes 278560 | tf_op jit(solution)/shard_map/ppermute | solution.py:34
  422.3 6.7 %collective-permute-done.92.refs_3_.refs_2_ = bf16[64,2048]{1,0:T(8,128)(2,1)S(1)} collective-permute-done((bf16[64,2048]{1,0:T(8,128)(2,1)S(1)}, bf16[64,2048]{1,0:T(8,128)(2,1)S(1)}, u32[]{:S(2)}, u32[]{:S(2)}) %collective-permute-start.92) | collective-permute-done | bytes 262176 | tf_op jit(solution)/shard_map/ppermute | solution.py:34
  468.3 11.3 %collective-permute-done.108.refs_2_ = bf16[128,2048]{1,0:T(8,128)(2,1)S(1)} collective-permute-done((bf16[128,2048]{1,0:T(8,128)(2,1)S(1)}, bf16[128,2048]{1,0:T(8,128)(2,1)S(1)}, u32[]{:S(2)}, u32[]{:S(2)}) %collective-permute-start.108) | collective-permute-done | bytes 524320 | tf_op jit(solution)/shard_map/ppermute | solution.py:34
  483.2 15.1 %collective-permute-done.109.refs_3_ = bf16[64,2048]{1,0:T(8,128)(2,1)S(1)} collective-permute-done((bf16[64,2048]{1,0:T(8,128)(2,1)S(1)}, bf16[64,2048]{1,0:T(8,128)(2,1)S(1)}, u32[]{:S(2)}, u32[]{:S(2)}) %collective-permute-start.109) | collective-permute-done | bytes 262176 | tf_op jit(solution)/shard_map/ppermute | solution.py:34
  504.1 10.6 %collective-permute-done.113.refs_1_ = f32[4,112,256]{2,1,0:T(8,128)S(1)} collective-permute-done((f32[4,112,256]{2,1,0:T(8,128)S(1)}, f32[4,112,256]{2,1,0:T(8,128)S(1)}, u32[]{:S(2)}, u32[]{:S(2)}) %collective-permute-start.113) | collective-permute-done | bytes 458784 | tf_op jit(solution)/shard_map/ppermute | solution.py:34
  520.4 6.8 %collective-permute-done.114.refs_1_ = f32[2,112,256]{2,1,0:T(8,128)S(1)} collective-permute-done((f32[2,112,256]{2,1,0:T(8,128)S(1)}, f32[2,112,256]{2,1,0:T(8,128)S(1)}, u32[]{:S(2)}, u32[]{:S(2)}) %collective-permute-start.114) | collective-permute-done | bytes 229408 | tf_op jit(solution)/shard_map/ppermute | solution.py:34
  531.1 8.2 %expert_weight_grads.6 = (f32[8,2048,256]{2,1,0:T(8,128)}, f32[8,2048,256]{2,1,0:T(8,128)}, f32[8,256,2048]{2,1,0:T(8,128)}, f32[8,128]{1,0:T(8,128)S(1)}) custom-call(bf16[8,192,2176]{2,1,0:T(8,128)(2,1)} %rows_of_slots.4.refs_17_.refs_1_.a_ref, ...), custom_call_target="tpu_custom_call", output_to_operand_aliasing={{0}: (6, {}), {1}: (7, {}), {2}: (8, {})} | custom-call | flops 2415 | bytes 19 | tf_op jit(solution)/shard_map/expert_weight_grads/pallas_call | solution.py:495
  564.0 19.1 %collective-permute-done.118.refs_1_ = bf16[2,256,768]{2,1,0:T(8,128)(2,1)S(1)} collective-permute-done((bf16[2,256,768]{2,1,0:T(8,128)(2,1)S(1)}, bf16[2,256,768]{2,1,0:T(8,128)(2,1)S(1)}, u32[]{:S(2)}, u32[]{:S(2)}) %collective-permute-start.118) | collective-permute-done | bytes 786464 | tf_op jit(solution)/shard_map/ppermute | solution.py:34
  583.5 7.8 %expert_weight_grads.7 = (f32[8,2048,256]{2,1,0:T(8,128)}, f32[8,2048,256]{2,1,0:T(8,128)}, f32[8,256,2048]{2,1,0:T(8,128)}, f32[8,128]{1,0:T(8,128)}) custom-call(bf16[8,192,2176]{2,1,0:T(8,128)(2,1)} %rows_of_slots.4.refs_17_.refs_1_.a_ref, ...), custom_call_target="tpu_custom_call", output_to_operand_aliasing={{0}: (6, {}), {1}: (7, {}), {2}: (8, {})} | custom-call | flops 2415 | bytes 19 | tf_op jit(solution)/shard_map/expert_weight_grads/pallas_call | solution.py:495
  (601 shorter events, 297.9 us)
Async XLA Ops:
  59.0 24.8 %collective-permute-start.12 = (bf16[256,768]{1,0:T(8,128)(2,1)S(1)}, bf16[256,768]{1,0:T(8,128)(2,1)S(1)}, u32[]{:S(2)}, u32[]{:S(2)}) collective-permute-start(bf16[256,768]{1,0:T(8,128)(2,1)S(1)} %get-tuple-element.129.refs_2_.refs_4_), channel_id=1, source_target_pairs={{0,16},{1,17},{2,18},{3,19},{4,20},{5,21},{6,22},{7,23},{8,24},{9,... | collective-permute-start | bytes 1179656 | tf_op jit(solution)/shard_map/ppermute | solution.py:34
  64.7 106.3 %collective-permute-start.55 = (bf16[512,2048]{1,0:T(8,128)(2,1)S(1)}, bf16[512,2048]{1,0:T(8,128)(2,1)S(1)}, u32[]{:S(2)}, u32[]{:S(2)}) collective-permute-start(bf16[512,2048]{1,0:T(8,128)(2,1)S(1)} %held.7.refs_1_), channel_id=1, source_target_pairs={{0,2},{1,3},{2,0},{3,1},{4,6},{5,7},{6,4},{7,5},{8,10},{9,11},{10,... | collective-permute-start | bytes 6291464 | tf_op jit(solution)/shard_map/ppermute | solution.py:34
  67.0 25.1 %collective-permute-start.13 = (bf16[256,768]{1,0:T(8,128)(2,1)S(1)}, bf16[256,768]{1,0:T(8,128)(2,1)S(1)}, u32[]{:S(2)}, u32[]{:S(2)}) collective-permute-start(bf16[256,768]{1,0:T(8,128)(2,1)S(1)} %collective-permute-done.7.refs_9_.refs_3_.refs_5_), channel_id=1, source_target_pairs={{0,16},{1,17},{2,18},{3,19},{4,20},{5,21},{6,22},{7,23},{8,24},{9,... | collective-permute-start | bytes 1179656 | tf_op jit(solution)/shard_map/ppermute | solution.py:34
  67.1 26.5 %collective-permute-start.9 = (bf16[64,2048]{1,0:T(8,128)(2,1)S(1)}, bf16[64,2048]{1,0:T(8,128)(2,1)S(1)}, u32[]{:S(2)}, u32[]{:S(2)}) collective-permute-start(bf16[64,2048]{1,0:T(8,128)(2,1)S(1)} %collective-permute-done.8.refs_2_), channel_id=1, source_target_pairs={{0,1},{1,0},{2,3},{3,2},{4,5},{5,4},{6,7},{7,6},{8,9},{9,8},{10,11... | collective-permute-start | bytes 786440 | tf_op jit(solution)/shard_map/ppermute | solution.py:34
  94.2 26.6 %collective-permute-start.21 = (bf16[512,256]{1,0:T(8,128)(2,1)S(1)}, bf16[512,256]{1,0:T(8,128)(2,1)S(1)}, u32[]{:S(2)}, u32[]{:S(2)}) collective-permute-start(bf16[512,256]{1,0:T(8,128)(2,1)S(1)} %held.6.refs_7_.refs_3_.refs_5_), channel_id=1, source_target_pairs={{0,8},{1,9},{2,10},{3,11},{4,12},{5,13},{6,14},{7,15},{8,0},{9,1},... | collective-permute-start | bytes 786440 | tf_op jit(solution)/shard_map/ppermute | solution.py:34
  120.9 22.6 %collective-permute-start.23 = (bf16[512,256]{1,0:T(8,128)(2,1)S(1)}, bf16[512,256]{1,0:T(8,128)(2,1)S(1)}, u32[]{:S(2)}, u32[]{:S(2)}) collective-permute-start(bf16[512,256]{1,0:T(8,128)(2,1)S(1)} %collective-permute-done.21.refs_8_.refs_4_.refs_6_), channel_id=1, source_target_pairs={{0,16},{1,17},{2,18},{3,19},{4,20},{5,21},{6,22},{7,23},{8,24},{9,... | collective-permute-start | bytes 786440 | tf_op jit(solution)/shard_map/ppermute | solution.py:34
  121.0 25.7 %collective-permute-start.25 = (bf16[512,256]{1,0:T(8,128)(2,1)S(1)}, bf16[512,256]{1,0:T(8,128)(2,1)S(1)}, u32[]{:S(2)}, u32[]{:S(2)}) collective-permute-start(bf16[512,256]{1,0:T(8,128)(2,1)S(1)} %held.6.refs_7_.refs_3_.refs_5_), channel_id=1, source_target_pairs={{0,4},{1,5},{2,6},{3,7},{4,0},{5,1},{6,2},{7,3},{8,12},{9,13},{10,... | collective-permute-start | bytes 786440 | tf_op jit(solution)/shard_map/ppermute | solution.py:34
  171.5 25.0 %collective-permute-start.39 = (bf16[64,2176]{1,0:T(8,128)(2,1)S(1)}, bf16[64,2176]{1,0:T(8,128)(2,1)S(1)}, u32[]{:S(2)}, u32[]{:S(2)}) collective-permute-start(bf16[64,2176]{1,0:T(8,128)(2,1)S(1)} %get-tuple-element.145.refs_1_.refs_3_), channel_id=1, source_target_pairs={{0,4},{1,5},{2,6},{3,7},{4,0},{5,1},{6,2},{7,3},{8,12},{9,13},{10,... | collective-permute-start | bytes 835592 | tf_op jit(solution)/shard_map/ppermute | solution.py:34
  171.8 25.2 %collective-permute-start.33 = (bf16[64,2176]{1,0:T(8,128)(2,1)S(1)}, bf16[64,2176]{1,0:T(8,128)(2,1)S(1)}, u32[]{:S(2)}, u32[]{:S(2)}) collective-permute-start(bf16[64,2176]{1,0:T(8,128)(2,1)S(1)} %get-tuple-element.145.refs_1_.refs_3_), channel_id=1, source_target_pairs={{0,2},{1,3},{2,0},{3,1},{4,6},{5,7},{6,4},{7,5},{8,10},{9,11},{10,... | collective-permute-start | bytes 835592 | tf_op jit(solution)/shard_map/ppermute | solution.py:34
  240.9 32.3 %collective-permute-start.68 = (bf16[64,2176]{1,0:T(8,128)(2,1)}, bf16[64,2176]{1,0:T(8,128)(2,1)}, u32[]{:S(2)}, u32[]{:S(2)}) collective-permute-start(bf16[64,2176]{1,0:T(8,128)(2,1)} %collective-permute-done.67.refs_11_), channel_id=1, source_target_pairs={{0,1},{1,0},{2,3},{3,2},{4,5},{5,4},{6,7},{7,6},{8,9},{9,8},{10,11... | collective-permute-start | bytes 835592 | tf_op jit(solution)/shard_map/ppermute | solution.py:34
  241.6 31.6 %collective-permute-start.62 = (bf16[64,2176]{1,0:T(8,128)(2,1)}, bf16[64,2176]{1,0:T(8,128)(2,1)}, u32[]{:S(2)}, u32[]{:S(2)}) collective-permute-start(bf16[64,2176]{1,0:T(8,128)(2,1)} %held.10.refs_5_), channel_id=1, source_target_pairs={{0,1},{1,0},{2,3},{3,2},{4,5},{5,4},{6,7},{7,6},{8,9},{9,8},{10,11... | collective-permute-start | bytes 835592 | tf_op jit(solution)/shard_map/ppermute | solution.py:34
  242.9 30.4 %collective-permute-start.64 = (bf16[64,2176]{1,0:T(8,128)(2,1)}, bf16[64,2176]{1,0:T(8,128)(2,1)}, u32[]{:S(2)}, u32[]{:S(2)}) collective-permute-start(bf16[64,2176]{1,0:T(8,128)(2,1)} %collective-permute-done.63.refs_7_), channel_id=1, source_target_pairs={{0,1},{1,0},{2,3},{3,2},{4,5},{5,4},{6,7},{7,6},{8,9},{9,8},{10,11... | collective-permute-start | bytes 835592 | tf_op jit(solution)/shard_map/ppermute | solution.py:34
  248.1 25.2 %collective-permute-start.70 = (bf16[64,2176]{1,0:T(8,128)(2,1)}, bf16[64,2176]{1,0:T(8,128)(2,1)}, u32[]{:S(2)}, u32[]{:S(2)}) collective-permute-start(bf16[64,2176]{1,0:T(8,128)(2,1)} %collective-permute-done.69.refs_13_), channel_id=1, source_target_pairs={{0,1},{1,0},{2,3},{3,2},{4,5},{5,4},{6,7},{7,6},{8,9},{9,8},{10,11... | collective-permute-start | bytes 835592 | tf_op jit(solution)/shard_map/ppermute | solution.py:34
  315.8 29.5 %collective-permute-start.77 = (bf16[256,2176]{1,0:T(8,128)(2,1)}, bf16[256,2176]{1,0:T(8,128)(2,1)S(1)}, u32[]{:S(2)}, u32[]{:S(2)}) collective-permute-start(bf16[256,2176]{1,0:T(8,128)(2,1)} %get-tuple-element.159), channel_id=1, source_target_pairs={{0,1},{1,0},{2,3},{3,2},{4,5},{5,4},{6,7},{7,6},{8,9},{9,8},{10,11... | collective-permute-start | bytes 3342344 | tf_op jit(solution)/shard_map/ppermute | solution.py:34
  319.7 26.9 %collective-permute-start.78 = (bf16[256,2176]{1,0:T(8,128)(2,1)S(1)}, bf16[256,2176]{1,0:T(8,128)(2,1)S(1)}, u32[]{:S(2)}, u32[]{:S(2)}) collective-permute-start(bf16[256,2176]{1,0:T(8,128)(2,1)S(1)} %combined.27.refs_4_), channel_id=1, source_target_pairs={{0,2},{1,3},{2,0},{3,1},{4,6},{5,7},{6,4},{7,5},{8,10},{9,11},{10,... | collective-permute-start | bytes 3342344 | tf_op jit(solution)/shard_map/ppermute | solution.py:34
  358.8 22.3 %collective-permute-start.86 = (bf16[256,2048]{1,0:T(8,128)(2,1)}, bf16[256,2048]{1,0:T(8,128)(2,1)}, u32[]{:S(2)}, u32[]{:S(2)}) collective-permute-start(bf16[256,2048]{1,0:T(8,128)(2,1)} %get-tuple-element.173), channel_id=1, source_target_pairs={{0,1},{1,0},{2,3},{3,2},{4,5},{5,4},{6,7},{7,6},{8,9},{9,8},{10,11... | collective-permute-start | bytes 3145736 | tf_op jit(solution)/shard_map/ppermute | solution.py:34
  372.7 26.8 %collective-permute-start.85 = (bf16[128,2176]{1,0:T(8,128)(2,1)S(1)}, bf16[128,2176]{1,0:T(8,128)(2,1)S(1)}, u32[]{:S(2)}, u32[]{:S(2)}) collective-permute-start(bf16[128,2176]{1,0:T(8,128)(2,1)S(1)} %combined.30.refs_2_), channel_id=1, source_target_pairs={{0,16},{1,17},{2,18},{3,19},{4,20},{5,21},{6,22},{7,23},{8,24},{9,... | collective-permute-start | bytes 1671176 | tf_op jit(solution)/shard_map/ppermute | solution.py:34
  375.1 42.9 %collective-permute-start.83 = (bf16[256,2048]{1,0:T(8,128)(2,1)S(1)}, bf16[256,2048]{1,0:T(8,128)(2,1)S(1)}, u32[]{:S(2)}, u32[]{:S(2)}) collective-permute-start(bf16[256,2048]{1,0:T(8,128)(2,1)S(1)} %combined.31.refs_6_), channel_id=1, source_target_pairs={{0,2},{1,3},{2,0},{3,1},{4,6},{5,7},{6,4},{7,5},{8,10},{9,11},{10,... | collective-permute-start | bytes 3145736 | tf_op jit(solution)/shard_map/ppermute | solution.py:34
  375.7 31.7 %collective-permute-start.84 = (bf16[128,2176]{1,0:T(8,128)(2,1)}, bf16[128,2176]{1,0:T(8,128)(2,1)}, u32[]{:S(2)}, u32[]{:S(2)}) collective-permute-start(bf16[128,2176]{1,0:T(8,128)(2,1)} %get-tuple-element.160.refs_3_), channel_id=1, source_target_pairs={{0,4},{1,5},{2,6},{3,7},{4,0},{5,1},{6,2},{7,3},{8,12},{9,13},{10,... | collective-permute-start | bytes 1671176 | tf_op jit(solution)/shard_map/ppermute | solution.py:34
  379.5 29.4 %collective-permute-start.90 = (bf16[128,2048]{1,0:T(8,128)(2,1)}, bf16[128,2048]{1,0:T(8,128)(2,1)S(1)}, u32[]{:S(2)}, u32[]{:S(2)}) collective-permute-start(bf16[128,2048]{1,0:T(8,128)(2,1)} %get-tuple-element.177.refs_5_), channel_id=1, source_target_pairs={{0,4},{1,5},{2,6},{3,7},{4,0},{5,1},{6,2},{7,3},{8,12},{9,13},{10,... | collective-permute-start | bytes 1572872 | tf_op jit(solution)/shard_map/ppermute | solution.py:34
  383.4 28.4 %collective-permute-start.89 = (bf16[128,2048]{1,0:T(8,128)(2,1)}, bf16[128,2048]{1,0:T(8,128)(2,1)S(1)}, u32[]{:S(2)}, u32[]{:S(2)}) collective-permute-start(bf16[128,2048]{1,0:T(8,128)(2,1)} %get-tuple-element.174.refs_4_), channel_id=1, source_target_pairs={{0,4},{1,5},{2,6},{3,7},{4,0},{5,1},{6,2},{7,3},{8,12},{9,13},{10,... | collective-permute-start | bytes 1572872 | tf_op jit(solution)/shard_map/ppermute | solution.py:34
  399.6 34.3 %collective-permute-start.79 = (bf16[256,2048]{1,0:T(8,128)(2,1)}, bf16[256,2048]{1,0:T(8,128)(2,1)S(1)}, u32[]{:S(2)}, u32[]{:S(2)}) collective-permute-start(bf16[256,2048]{1,0:T(8,128)(2,1)} %get-tuple-element.162), channel_id=1, source_target_pairs={{0,1},{1,0},{2,3},{3,2},{4,5},{5,4},{6,7},{7,6},{8,9},{9,8},{10,11... | collective-permute-start | bytes 3145736 | tf_op jit(solution)/shard_map/ppermute | solution.py:34
  432.6 22.1 %collective-permute-start.95 = (bf16[128,2048]{1,0:T(8,128)(2,1)S(1)}, bf16[128,2048]{1,0:T(8,128)(2,1)S(1)}, u32[]{:S(2)}, u32[]{:S(2)}) collective-permute-start(bf16[128,2048]{1,0:T(8,128)(2,1)S(1)} %combined.36), channel_id=1, source_target_pairs={{0,2},{1,3},{2,0},{3,1},{4,6},{5,7},{6,4},{7,5},{8,10},{9,11},{10,... | collective-permute-start | bytes 1572872 | tf_op jit(solution)/shard_map/ppermute | solution.py:34
  458.3 43.0 %collective-permute-start.101 = (bf16[4,256,768]{2,1,0:T(8,128)(2,1)S(1)}, bf16[4,256,768]{2,1,0:T(8,128)(2,1)S(1)}, u32[]{:S(2)}, u32[]{:S(2)}) collective-permute-start(bf16[4,256,768]{2,1,0:T(8,128)(2,1)S(1)} %get-tuple-element.198.refs_12_), channel_id=1, source_target_pairs={{0,4},{1,5},{2,6},{3,7},{4,0},{5,1},{6,2},{7,3},{8,12},{9,13},{10,... | collective-permute-start | bytes 4718600 | tf_op jit(solution)/shard_map/ppermute | solution.py:34
  466.8 34.4 %collective-permute-start.97 = (bf16[128,2048]{1,0:T(8,128)(2,1)S(1)}, bf16[128,2048]{1,0:T(8,128)(2,1)S(1)}, u32[]{:S(2)}, u32[]{:S(2)}) collective-permute-start(bf16[128,2048]{1,0:T(8,128)(2,1)S(1)} %combined.37), channel_id=1, source_target_pairs={{0,16},{1,17},{2,18},{3,19},{4,20},{5,21},{6,22},{7,23},{8,24},{9,... | collective-permute-start | bytes 1572872 | tf_op jit(solution)/shard_map/ppermute | solution.py:34
  481.6 60.1 %collective-permute-start.119 = (bf16[256,2048]{1,0:T(8,128)(2,1)}, bf16[256,2048]{1,0:T(8,128)(2,1)}, u32[]{:S(2)}, u32[]{:S(2)}) collective-permute-start(bf16[256,2048]{1,0:T(8,128)(2,1)} %held.11), channel_id=1, source_target_pairs={{0,8},{1,9},{2,10},{3,11},{4,12},{5,13},{6,14},{7,15},{8,0},{9,1},... | collective-permute-start | bytes 3145736 | tf_op jit(solution)/shard_map/ppermute | solution.py:34
  515.7 31.7 %collective-permute-start.112 = (f32[64,2048]{1,0:T(8,128)}, f32[64,2048]{1,0:T(8,128)}, u32[]{:S(2)}, u32[]{:S(2)}) collective-permute-start(f32[64,2048]{1,0:T(8,128)} %get-tuple-element.207), channel_id=1, source_target_pairs={{0,1},{1,0},{2,3},{3,2},{4,5},{5,4},{6,7},{7,6},{8,9},{9,8},{10,11... | collective-permute-start | bytes 1572872 | tf_op jit(solution)/shard_map/ppermute | solution.py:34
  515.7 32.5 %collective-permute-start.111 = (f32[64,2048]{1,0:T(8,128)}, f32[64,2048]{1,0:T(8,128)}, u32[]{:S(2)}, u32[]{:S(2)}) collective-permute-start(f32[64,2048]{1,0:T(8,128)} %collective-permute-done.110), channel_id=1, source_target_pairs={{0,1},{1,0},{2,3},{3,2},{4,5},{5,4},{6,7},{7,6},{8,9},{9,8},{10,11... | collective-permute-start | bytes 1572872 | tf_op jit(solution)/shard_map/ppermute | solution.py:34
  539.3 43.8 %collective-permute-start.118 = (bf16[2,256,768]{2,1,0:T(8,128)(2,1)S(1)}, bf16[2,256,768]{2,1,0:T(8,128)(2,1)S(1)}, u32[]{:S(2)}, u32[]{:S(2)}) collective-permute-start(bf16[2,256,768]{2,1,0:T(8,128)(2,1)S(1)} %copy-done.7), channel_id=1, source_target_pairs={{0,16},{1,17},{2,18},{3,19},{4,20},{5,21},{6,22},{7,23},{8,24},{9,... | collective-permute-start | bytes 2359304 | tf_op jit(solution)/shard_map/ppermute | solution.py:34
  546.4 47.1 %collective-permute-start.105 = (f32[64,2048]{1,0:T(8,128)S(1)}, f32[64,2048]{1,0:T(8,128)S(1)}, u32[]{:S(2)}, u32[]{:S(2)}) collective-permute-start(f32[64,2048]{1,0:T(8,128)S(1)} %combined.40), channel_id=1, source_target_pairs={{0,1},{1,0},{2,3},{3,2},{4,5},{5,4},{6,7},{7,6},{8,9},{9,8},{10,11... | collective-permute-start | bytes 1572872 | tf_op jit(solution)/shard_map/ppermute | solution.py:34
  556.2 37.3 %collective-permute-start.104 = (f32[64,2048]{1,0:T(8,128)S(1)}, f32[64,2048]{1,0:T(8,128)S(1)}, u32[]{:S(2)}, u32[]{:S(2)}) collective-permute-start(f32[64,2048]{1,0:T(8,128)S(1)} %collective-permute-done.103), channel_id=1, source_target_pairs={{0,1},{1,0},{2,3},{3,2},{4,5},{5,4},{6,7},{7,6},{8,9},{9,8},{10,11... | collective-permute-start | bytes 1572872 | tf_op jit(solution)/shard_map/ppermute | solution.py:34
  562.0 29.3 %collective-permute-start.122 = (bf16[2,256,256]{2,1,0:T(8,128)(2,1)S(1)}, bf16[2,256,256]{2,1,0:T(8,128)(2,1)S(1)}, u32[]{:S(2)}, u32[]{:S(2)}) collective-permute-start(bf16[2,256,256]{2,1,0:T(8,128)(2,1)S(1)} %get-tuple-element.225.refs_2_.refs_4_), channel_id=1, source_target_pairs={{0,16},{1,17},{2,18},{3,19},{4,20},{5,21},{6,22},{7,23},{8,24},{9,... | collective-permute-start | bytes 786440 | tf_op jit(solution)/shard_map/ppermute | solution.py:34
  (232 other events, 2952.9 us)

commit v5 on v4

--- a/solution.py
+++ b/solution.py
@@ -205,10 +205,10 @@
         return terms
 
 
-def reduce_all(near, far):
+def reduce_all(near, far, waits):
     terms = [near, over_y(far)]
     for bit in reversed(z_bits()):
-        near, sent = combined(terms, bit, sent=f32)
+        near, sent = combined(terms, bit, waits, sent=f32)
         terms = [near, over_z(sent, bit)]
     return reduce_tp(added(*terms)[0])
 
@@ -1307,14 +1307,14 @@
         )
         return mark
 
-    mark = some_grads(0, out_first[0])
-    back.top(mark)
+    back.top()
+    mark = some_grads(0, *back.sent)
     moe = TokenSums(out_first, out_second).start(*back.sent)
     mark = some_grads(1, mark, *moe.sent)
     back = back.last(mark)
 
     grad_middle, grad_low, router_sum, gain_sum = route_back(
-        back, middle, x_piece, probs, cot_own, gain_two, router, waits=moe.came
+        back, middle, x_piece, probs, cot_own, gain_two, router, waits=[moe.came[0]]
     )
     low_pieces = gather_tp(grad_low)
     keep, give = output_back(low_pieces, output_pieces, places, [])
@@ -1332,10 +1332,10 @@
     terms, crossing = scatter_tp(parts)
     for_mate = combined([term[share:] for term in terms], 0)
     from_mate = over_z(for_mate, 1)
-    head_sums_at.along_z(moe.from_top)
+    head_sums_at.along_z(moe.from_top, from_mate)
     mates_low = over_z(held(low_pieces, bf16, [for_mate]), 1)
     mark = some_grads(2, mark, head_sums_at.sent)
-    moe = moe.last(head_sums_at.sent)
+    moe = moe.last(head_sums_at.came)
     low_slabs = paired(low_pieces, [mates_low], places, data_size)
     output_parts = weight_parts(
         low_slabs, [attended], places, False, waits=[head_sums_at.sent]
@@ -1347,14 +1347,14 @@
         gain_sums,
         places,
         data_size,
-        [head_sums_at.sent],
+        [],
     )
     grad_hidden = gather_tp(grad_hidden)
-    output_sums.along_z(mark)
-    mark = some_grads(3, mark, output_sums.sent)
-    head_sums_at.to_mate(output_sums.sent)
-    output_sums.to_mate(head_sums_at.sent)
-    total = reduce_all(*late)
+    mark = some_grads(3, mark, head_sums_at.sent)
+    came = head_sums_at.came
+    head_sums_at.to_mate(mark)
+    output_sums.along_z(head_sums_at.sent).to_mate()
+    total = reduce_all(*late, [came, mark])
     grad_hidden = absolute_tp(grad_hidden)
     hidden_out = absolute_tp(gather_tp(combined([middle, *moe], 0, sent=f32)))
     late = total[E + 8 :]

time: 613 us -> 593 us (0.967)
  waiting for transfers between devices: 262 us -> 253 us
    ppermute x124, waiting for transfers between devices: 262 us -> 253 us  [swap(): return lax.ppermute(values, ('dp', 'tp'), pairs)]
  transfers between devices with their start and end apart: 124 -> 124, of which waited for: 47 -> 45; matrix products, arithmetic and copies ran while one was open for 3% -> 2% of each run, Pallas kernels for 21% -> 23%
where the time goes in v5:
time: 593 us; the launch traced here: 583 us
  waiting for transfers between devices  253 us (43%)
  Pallas kernels  177 us (30%)
  starting transfers between devices  89.4 us (15%)
  local copies, waits for them, and re-layouts  46.8 us (8%)
  other arithmetic  14.2 us (2%)
    ppermute x124, waiting for transfers between devices, swap(): return lax.ppermute(values, ('dp', 'tp'), pairs)  253 us
    ppermute x124, starting transfers between devices, swap(): return lax.ppermute(values, ('dp', 'tp'), pairs)  89.4 us
    pallas_call x49, Pallas kernels, kernel_call(): pl.pallas_call(body, in_specs=[pl.BlockSpec(memory_space=pltpu.SMEM)] * l...  55.9 us
    pallas_call x3, Pallas kernels, per_expert(): pl.pallas_call(without(kernel, len(in_specs), len(waits)), grid=(experts,...  44 us
    unnamed x280, local copies, waits for them, and re-layouts  40.2 us
    pallas_call x4, Pallas kernels, expert_weight_grads(): pl.pallas_call(kernel, grid=(count,), in_specs=[block(rows // 2, width)]...  31.5 us
    pallas_call x4, Pallas kernels, tokens_of_slots(): pl.pallas_call(without(kernel, 2, len(waits)), grid=(sequences,), in_spec...  25.3 us
    pallas_call x3, Pallas kernels, rows_of_slots(): pl.pallas_call(without(kernel, 1 + len(flat), len(waits)), grid=(sequence...  20 us
  transfers between devices with their start and end apart: 124, of which 45 were waited for; matrix products, arithmetic and copies ran while one was open for 2% of the time, Pallas kernels for 23%

profile of v5, /device:TPU:0, one launch (start us, length us, event | category | flops | bytes accessed | tf_op | source)
XLA Modules:
  0.0 582.8 jit_solution(7680046553652687987)
XLA Ops:
  24.9 6.3 %collective-permute-done.2.refs_4_ = bf16[83,256]{1,0:T(8,128)(2,1)S(1)} collective-permute-done((bf16[83,256]{1,0:T(8,128)(2,1)S(1)}, bf16[83,256]{1,0:T(8,128)(2,1)S(1)}, u32[]{:S(2)}, u32[]{:S(2)}) %collective-permute-start.2) | collective-permute-done | bytes 42528 | tf_op jit(solution)/shard_map/ppermute | solution.py:34
  43.0 8.6 %collective-permute-done.48.refs_2_ = bf16[64,2048]{1,0:T(8,128)(2,1)S(1)} collective-permute-done((bf16[64,2048]{1,0:T(8,128)(2,1)S(1)}, bf16[64,2048]{1,0:T(8,128)(2,1)S(1)}, u32[]{:S(2)}, u32[]{:S(2)}) %collective-permute-start.48) | collective-permute-done | bytes 262176 | tf_op jit(solution)/shard_map/ppermute | solution.py:34
  67.1 16.7 %collective-permute-done.12.refs_4_.refs_6_ = bf16[256,768]{1,0:T(8,128)(2,1)S(1)} collective-permute-done((bf16[256,768]{1,0:T(8,128)(2,1)S(1)}, bf16[256,768]{1,0:T(8,128)(2,1)S(1)}, u32[]{:S(2)}, u32[]{:S(2)}) %collective-permute-start.12) | collective-permute-done | bytes 393248 | tf_op jit(solution)/shard_map/ppermute | solution.py:34
  85.4 6.8 %collective-permute-done.13.refs_5_.refs_1_.refs_7_ = bf16[256,768]{1,0:T(8,128)(2,1)S(1)} collective-permute-done((bf16[256,768]{1,0:T(8,128)(2,1)S(1)}, bf16[256,768]{1,0:T(8,128)(2,1)S(1)}, u32[]{:S(2)}, u32[]{:S(2)}) %collective-permute-start.13) | collective-permute-done | bytes 393248 | tf_op jit(solution)/shard_map/ppermute | solution.py:34
  95.8 8.4 %collective-permute-done.16.refs_8_.refs_10_ = bf16[256,768]{1,0:T(8,128)(2,1)S(1)} collective-permute-done((bf16[256,768]{1,0:T(8,128)(2,1)S(1)}, bf16[256,768]{1,0:T(8,128)(2,1)S(1)}, u32[]{:S(2)}, u32[]{:S(2)}) %collective-permute-start.16) | collective-permute-done | bytes 393248 | tf_op jit(solution)/shard_map/ppermute | solution.py:34
  104.3 8.0 %collective-permute-done.17.refs_9_.refs_11_ = bf16[256,768]{1,0:T(8,128)(2,1)S(1)} collective-permute-done((bf16[256,768]{1,0:T(8,128)(2,1)S(1)}, bf16[256,768]{1,0:T(8,128)(2,1)S(1)}, u32[]{:S(2)}, u32[]{:S(2)}) %collective-permute-start.17) | collective-permute-done | bytes 393248 | tf_op jit(solution)/shard_map/ppermute | solution.py:34
  123.9 14.1 %collective-permute-done.22.refs_9_.refs_5_.refs_7_ = bf16[512,256]{1,0:T(8,128)(2,1)S(1)} collective-permute-done((bf16[512,256]{1,0:T(8,128)(2,1)S(1)}, bf16[512,256]{1,0:T(8,128)(2,1)S(1)}, u32[]{:S(2)}, u32[]{:S(2)}) %collective-permute-start.22) | collective-permute-done | bytes 262176 | tf_op jit(solution)/shard_map/ppermute | solution.py:34
  147.2 5.6 collective-permute-done.27.refs_9_.refs_11_
  162.8 6.6 %collective-permute-done.31.refs_2_ = bf16[64,2048]{1,0:T(8,128)(2,1)S(1)} collective-permute-done((bf16[64,2048]{1,0:T(8,128)(2,1)S(1)}, bf16[64,2048]{1,0:T(8,128)(2,1)S(1)}, u32[]{:S(2)}, u32[]{:S(2)}) %collective-permute-start.31) | collective-permute-done | bytes 262176 | tf_op jit(solution)/shard_map/ppermute | solution.py:34
  172.6 8.2 %collective-permute-done.35.refs_5_.refs_0_ = bf16[64,2176]{1,0:T(8,128)(2,1)S(1)} collective-permute-done((bf16[64,2176]{1,0:T(8,128)(2,1)S(1)}, bf16[64,2176]{1,0:T(8,128)(2,1)S(1)}, u32[]{:S(2)}, u32[]{:S(2)}) %collective-permute-start.35) | collective-permute-done | bytes 278560 | tf_op jit(solution)/shard_map/ppermute | solution.py:34
  182.5 9.5 %rows_of_slots.3.refs_0_.refs_1_.cot_ref = bf16[8,384,2048]{2,1,0:T(8,128)(2,1)} custom-call(s32[8,8,256]{2,1,0:T(8,128)S(1)} %get-tuple-element.145.refs_0_, bf16[512,2048]{1,0:T(8,128)(2,1)S(1)} %held.7.refs_1_, bf16[512,2048]{1,0:T(8,128)(2,1)S(1)} %collective-permute-done.54.refs_2_, bf16[512,2048]{1,0:T(8,128)(2,1)} %copy-done.8, ...), custom_call_target="tpu_custom_call" | custom-call | flops 3221 | bytes 20 | tf_op jit(solution)/shard_map/rows_of_slots/pallas_call | solution.py:307
  215.5 10.6 %grad_of_hidden.1.refs_17_.refs_1_.refs_5_ = f32[8,384,256]{2,1,0:T(8,128)S(1)} custom-call(bf16[8,384,2048]{2,1,0:T(8,128)(2,1)} %rows_of_slots.3.refs_0_.refs_1_.cot_ref, bf16[8,256,2048]{2,1,0:T(8,128)(2,1)} %refs_1_.5), custom_call_target="tpu_custom_call" | custom-call | flops 3221 | bytes 24 | tf_op jit(solution)/shard_map/grad_of_hidden/pallas_call | solution.py:381
  278.8 21.9 %expert_step.1 = (bf16[8,384,2176]{2,1,0:T(8,128)(2,1)}, bf16[8,384,256]{2,1,0:T(8,128)(2,1)S(1)}, bf16[8,384,256]{2,1,0:T(8,128)(2,1)S(1)}, bf16[8,384,256]{2,1,0:T(8,128)(2,1)S(1)}) custom-call(s32[1]{0:T(128)} %bitcast.7.refs_0_, bf16[8,192,2176]{2,1,0:T(8,128)(2,1)} %rows_of_slots.4.refs_17_.refs_1_.a_ref, ...), custom_call_target="tpu_custom_call" | custom-call | flops 12884 | bytes 51 | tf_op jit(solution)/shard_map/expert_step/pallas_call | solution.py:381
  300.7 7.0 %tokens_of_slots.4 = (bf16[256,2176]{1,0:T(8,128)(2,1)S(1)}, bf16[256,2176]{1,0:T(8,128)(2,1)}, bf16[256,2176]{1,0:T(8,128)(2,1)S(1)}, bf16[256,2176]{1,0:T(8,128)(2,1)}) custom-call(s32[4,8,256]{2,1,0:T(8,128)S(1)} %get-tuple-element.254.refs_0_, bf16[8,384,2176]{2,1,0:T(8,128)(2,1)} %get-tuple-element.148.refs_1_), custom_call_target="tpu_custom_call" | custom-call | flops 1711 | bytes 11 | tf_op jit(solution)/shard_map/tokens_of_slots/pallas_call | solution.py:345
  307.7 6.2 %tokens_of_slots.5 = (bf16[256,2176]{1,0:T(8,128)(2,1)S(1)}, bf16[256,2176]{1,0:T(8,128)(2,1)}, bf16[256,2176]{1,0:T(8,128)(2,1)S(1)}, bf16[256,2176]{1,0:T(8,128)(2,1)S(1)}) custom-call(s32[4,8,256]{2,1,0:T(8,128)S(1)} %get-tuple-element.255.refs_0_, bf16[8,384,2176]{2,1,0:T(8,128)(2,1)} %get-tuple-element.148.refs_1_, ...), custom_call_target="tpu_custom_call" | custom-call | flops 1711 | bytes 11 | tf_op jit(solution)/shard_map/tokens_of_slots/pallas_call | solution.py:345
  323.1 11.5 %expert_out.1.refs_1_ = bf16[8,384,2048]{2,1,0:T(8,128)(2,1)} custom-call(bf16[8,384,256]{2,1,0:T(8,128)(2,1)S(1)} %get-tuple-element.147.refs_0_.act_ref, bf16[8,256,2048]{2,1,0:T(8,128)(2,1)} %refs_1_.5, bf16[128,2176]{1,0:T(8,128)(2,1)S(1)} %get-tuple-element.151.refs_2_, bf16[128,2176]{1,0:T(8,128)(2,1)} %get-tuple-element.154.refs_3_, ...), custom_call_target="tpu_custom_call" | custom-call | flops 3221 | bytes 22 | tf_op jit(solution)/shard_map/expert_out/pallas_call | solution.py:381
  335.4 5.9 %tokens_of_slots.6 = (bf16[256,2048]{1,0:T(8,128)(2,1)S(1)}, bf16[256,2048]{1,0:T(8,128)(2,1)}, bf16[256,2048]{1,0:T(8,128)(2,1)S(1)}, bf16[256,2048]{1,0:T(8,128)(2,1)S(1)}) custom-call(s32[4,8,256]{2,1,0:T(8,128)S(1)} %get-tuple-element.254.refs_0_, bf16[8,384,2048]{2,1,0:T(8,128)(2,1)} %expert_out.1.refs_1_), custom_call_target="tpu_custom_call" | custom-call | flops 1610 | bytes 10 | tf_op jit(solution)/shard_map/tokens_of_slots/pallas_call | solution.py:345
  349.6 6.1 %tokens_of_slots.7 = (bf16[256,2048]{1,0:T(8,128)(2,1)S(1)}, bf16[256,2048]{1,0:T(8,128)(2,1)}, bf16[256,2048]{1,0:T(8,128)(2,1)S(1)}, bf16[256,2048]{1,0:T(8,128)(2,1)S(1)}) custom-call(s32[4,8,256]{2,1,0:T(8,128)S(1)} %get-tuple-element.255.refs_0_, bf16[8,384,2048]{2,1,0:T(8,128)(2,1)} %expert_out.1.refs_1_, bf16[128,2176]{1,0:T(8,128)(2,1)S(1)} %combined.28.refs_2_, ...), custom_call_target="tpu_custom_call" | custom-call | flops 1610 | bytes 10 | tf_op jit(solution)/shard_map/tokens_of_slots/pallas_call | solution.py:345
  358.3 12.9 %collective-permute-done.81.refs_1_ = bf16[128,2176]{1,0:T(8,128)(2,1)S(1)} collective-permute-done((bf16[128,2176]{1,0:T(8,128)(2,1)S(1)}, bf16[128,2176]{1,0:T(8,128)(2,1)S(1)}, u32[]{:S(2)}, u32[]{:S(2)}) %collective-permute-start.81) | collective-permute-done | bytes 557088 | tf_op jit(solution)/shard_map/ppermute | solution.py:34
  378.4 7.9 %expert_weight_grads.4 = (f32[8,2048,256]{2,1,0:T(8,128)}, f32[8,2048,256]{2,1,0:T(8,128)}, f32[8,256,2048]{2,1,0:T(8,128)}, f32[8,128]{1,0:T(8,128)S(1)}) custom-call(bf16[8,192,2176]{2,1,0:T(8,128)(2,1)} %rows_of_slots.4.refs_17_.refs_1_.a_ref, bf16[8,192,2176]{2,1,0:T(8,128)(2,1)} %rows_of_slots.5.refs_2_.b_ref, ...), custom_call_target="tpu_custom_call" | custom-call | flops 2415 | bytes 19 | tf_op jit(solution)/shard_map/expert_weight_grads/pallas_call | solution.py:495
  386.6 7.8 %expert_weight_grads.5 = (f32[8,2048,256]{2,1,0:T(8,128)}, f32[8,2048,256]{2,1,0:T(8,128)}, f32[8,256,2048]{2,1,0:T(8,128)}, f32[8,128]{1,0:T(8,128)S(1)}) custom-call(bf16[8,192,2176]{2,1,0:T(8,128)(2,1)} %rows_of_slots.4.refs_17_.refs_1_.a_ref, ...), custom_call_target="tpu_custom_call", output_to_operand_aliasing={{0}: (6, {}), {1}: (7, {}), {2}: (8, {})} | custom-call | flops 2415 | bytes 19 | tf_op jit(solution)/shard_map/expert_weight_grads/pallas_call | solution.py:495
  401.3 8.6 %collective-permute-done.88.refs_1_ = bf16[64,2176]{1,0:T(8,128)(2,1)S(1)} collective-permute-done((bf16[64,2176]{1,0:T(8,128)(2,1)S(1)}, bf16[64,2176]{1,0:T(8,128)(2,1)S(1)}, u32[]{:S(2)}, u32[]{:S(2)}) %collective-permute-start.88) | collective-permute-done | bytes 278560 | tf_op jit(solution)/shard_map/ppermute | solution.py:34
  412.7 6.7 %collective-permute-done.91.refs_3_.refs_2_ = bf16[64,2048]{1,0:T(8,128)(2,1)S(1)} collective-permute-done((bf16[64,2048]{1,0:T(8,128)(2,1)S(1)}, bf16[64,2048]{1,0:T(8,128)(2,1)S(1)}, u32[]{:S(2)}, u32[]{:S(2)}) %collective-permute-start.91) | collective-permute-done | bytes 262176 | tf_op jit(solution)/shard_map/ppermute | solution.py:34
  461.0 11.8 %collective-permute-done.104.refs_2_ = bf16[128,2048]{1,0:T(8,128)(2,1)S(1)} collective-permute-done((bf16[128,2048]{1,0:T(8,128)(2,1)S(1)}, bf16[128,2048]{1,0:T(8,128)(2,1)S(1)}, u32[]{:S(2)}, u32[]{:S(2)}) %collective-permute-start.104) | collective-permute-done | bytes 524320 | tf_op jit(solution)/shard_map/ppermute | solution.py:34
  473.8 11.8 %collective-permute-done.97.refs_2_ = bf16[128,2048]{1,0:T(8,128)(2,1)S(1)} collective-permute-done((bf16[128,2048]{1,0:T(8,128)(2,1)S(1)}, bf16[128,2048]{1,0:T(8,128)(2,1)S(1)}, u32[]{:S(2)}, u32[]{:S(2)}) %collective-permute-start.97) | collective-permute-done | bytes 524320 | tf_op jit(solution)/shard_map/ppermute | solution.py:34
  485.6 5.5 collective-permute-done.105.refs_3_
  499.9 7.8 %expert_weight_grads.6 = (f32[8,2048,256]{2,1,0:T(8,128)}, f32[8,2048,256]{2,1,0:T(8,128)}, f32[8,256,2048]{2,1,0:T(8,128)}, f32[8,128]{1,0:T(8,128)S(1)}) custom-call(bf16[8,192,2176]{2,1,0:T(8,128)(2,1)} %rows_of_slots.4.refs_17_.refs_1_.a_ref, ...), custom_call_target="tpu_custom_call", output_to_operand_aliasing={{0}: (6, {}), {1}: (7, {}), {2}: (8, {})} | custom-call | flops 2415 | bytes 19 | tf_op jit(solution)/shard_map/expert_weight_grads/pallas_call | solution.py:495
  507.6 8.0 %expert_weight_grads.7 = (f32[8,2048,256]{2,1,0:T(8,128)}, f32[8,2048,256]{2,1,0:T(8,128)}, f32[8,256,2048]{2,1,0:T(8,128)}, f32[8,128]{1,0:T(8,128)S(1)}) custom-call(bf16[8,192,2176]{2,1,0:T(8,128)(2,1)} %rows_of_slots.4.refs_17_.refs_1_.a_ref, ...), custom_call_target="tpu_custom_call", output_to_operand_aliasing={{0}: (6, {}), {1}: (7, {}), {2}: (8, {})} | custom-call | flops 2415 | bytes 19 | tf_op jit(solution)/shard_map/expert_weight_grads/pallas_call | solution.py:495
  515.7 12.7 %collective-permute-done.106.refs_3_.refs_2_.refs_1_ = bf16[2,256,768]{2,1,0:T(8,128)(2,1)S(1)} collective-permute-done((bf16[2,256,768]{2,1,0:T(8,128)(2,1)S(1)}, bf16[2,256,768]{2,1,0:T(8,128)(2,1)S(1)}, u32[]{:S(2)}, u32[]{:S(2)}) %collective-permute-start.106) | collective-permute-done | bytes 786464 | tf_op jit(solution)/shard_map/ppermute | solution.py:34
  533.8 8.7 %collective-permute-done.115.refs_1_ = f32[2,112,256]{2,1,0:T(8,128)S(1)} collective-permute-done((f32[2,112,256]{2,1,0:T(8,128)S(1)}, f32[2,112,256]{2,1,0:T(8,128)S(1)}, u32[]{:S(2)}, u32[]{:S(2)}) %collective-permute-start.115) | collective-permute-done | bytes 229408 | tf_op jit(solution)/shard_map/ppermute | solution.py:34
  554.0 6.6 %collective-permute-done.121.refs_1_ = bf16[4,256,256]{2,1,0:T(8,128)(2,1)S(1)} collective-permute-done((bf16[4,256,256]{2,1,0:T(8,128)(2,1)S(1)}, bf16[4,256,256]{2,1,0:T(8,128)(2,1)S(1)}, u32[]{:S(2)}, u32[]{:S(2)}) %collective-permute-start.121) | collective-permute-done | bytes 524320 | tf_op jit(solution)/shard_map/ppermute | solution.py:34
  565.5 8.3 %collective-permute-done.122.refs_1_ = bf16[2,256,256]{2,1,0:T(8,128)(2,1)S(1)} collective-permute-done((bf16[2,256,256]{2,1,0:T(8,128)(2,1)S(1)}, bf16[2,256,256]{2,1,0:T(8,128)(2,1)S(1)}, u32[]{:S(2)}, u32[]{:S(2)}) %collective-permute-start.122) | collective-permute-done | bytes 262176 | tf_op jit(solution)/shard_map/ppermute | solution.py:34
  (601 shorter events, 286.4 us)
Async XLA Ops:
  59.0 24.8 %collective-permute-start.12 = (bf16[256,768]{1,0:T(8,128)(2,1)S(1)}, bf16[256,768]{1,0:T(8,128)(2,1)S(1)}, u32[]{:S(2)}, u32[]{:S(2)}) collective-permute-start(bf16[256,768]{1,0:T(8,128)(2,1)S(1)} %get-tuple-element.130.refs_2_.refs_4_), channel_id=1, source_target_pairs={{0,16},{1,17},{2,18},{3,19},{4,20},{5,21},{6,22},{7,23},{8,24},{9,... | collective-permute-start | bytes 1179656 | tf_op jit(solution)/shard_map/ppermute | solution.py:34
  64.7 106.3 %collective-permute-start.55 = (bf16[512,2048]{1,0:T(8,128)(2,1)S(1)}, bf16[512,2048]{1,0:T(8,128)(2,1)S(1)}, u32[]{:S(2)}, u32[]{:S(2)}) collective-permute-start(bf16[512,2048]{1,0:T(8,128)(2,1)S(1)} %held.7.refs_1_), channel_id=1, source_target_pairs={{0,2},{1,3},{2,0},{3,1},{4,6},{5,7},{6,4},{7,5},{8,10},{9,11},{10,... | collective-permute-start | bytes 6291464 | tf_op jit(solution)/shard_map/ppermute | solution.py:34
  67.1 25.1 %collective-permute-start.13 = (bf16[256,768]{1,0:T(8,128)(2,1)S(1)}, bf16[256,768]{1,0:T(8,128)(2,1)S(1)}, u32[]{:S(2)}, u32[]{:S(2)}) collective-permute-start(bf16[256,768]{1,0:T(8,128)(2,1)S(1)} %collective-permute-done.7.refs_9_.refs_3_.refs_5_), channel_id=1, source_target_pairs={{0,16},{1,17},{2,18},{3,19},{4,20},{5,21},{6,22},{7,23},{8,24},{9,... | collective-permute-start | bytes 1179656 | tf_op jit(solution)/shard_map/ppermute | solution.py:34
  67.1 26.6 %collective-permute-start.9 = (bf16[64,2048]{1,0:T(8,128)(2,1)S(1)}, bf16[64,2048]{1,0:T(8,128)(2,1)S(1)}, u32[]{:S(2)}, u32[]{:S(2)}) collective-permute-start(bf16[64,2048]{1,0:T(8,128)(2,1)S(1)} %collective-permute-done.8.refs_2_), channel_id=1, source_target_pairs={{0,1},{1,0},{2,3},{3,2},{4,5},{5,4},{6,7},{7,6},{8,9},{9,8},{10,11... | collective-permute-start | bytes 786440 | tf_op jit(solution)/shard_map/ppermute | solution.py:34
  94.3 26.6 %collective-permute-start.21 = (bf16[512,256]{1,0:T(8,128)(2,1)S(1)}, bf16[512,256]{1,0:T(8,128)(2,1)S(1)}, u32[]{:S(2)}, u32[]{:S(2)}) collective-permute-start(bf16[512,256]{1,0:T(8,128)(2,1)S(1)} %held.6.refs_7_.refs_3_.refs_5_), channel_id=1, source_target_pairs={{0,8},{1,9},{2,10},{3,11},{4,12},{5,13},{6,14},{7,15},{8,0},{9,1},... | collective-permute-start | bytes 786440 | tf_op jit(solution)/shard_map/ppermute | solution.py:34
  120.9 22.6 %collective-permute-start.23 = (bf16[512,256]{1,0:T(8,128)(2,1)S(1)}, bf16[512,256]{1,0:T(8,128)(2,1)S(1)}, u32[]{:S(2)}, u32[]{:S(2)}) collective-permute-start(bf16[512,256]{1,0:T(8,128)(2,1)S(1)} %collective-permute-done.21.refs_8_.refs_4_.refs_6_), channel_id=1, source_target_pairs={{0,16},{1,17},{2,18},{3,19},{4,20},{5,21},{6,22},{7,23},{8,24},{9,... | collective-permute-start | bytes 786440 | tf_op jit(solution)/shard_map/ppermute | solution.py:34
  121.0 25.8 %collective-permute-start.25 = (bf16[512,256]{1,0:T(8,128)(2,1)S(1)}, bf16[512,256]{1,0:T(8,128)(2,1)S(1)}, u32[]{:S(2)}, u32[]{:S(2)}) collective-permute-start(bf16[512,256]{1,0:T(8,128)(2,1)S(1)} %held.6.refs_7_.refs_3_.refs_5_), channel_id=1, source_target_pairs={{0,4},{1,5},{2,6},{3,7},{4,0},{5,1},{6,2},{7,3},{8,12},{9,13},{10,... | collective-permute-start | bytes 786440 | tf_op jit(solution)/shard_map/ppermute | solution.py:34
  171.7 25.0 %collective-permute-start.39 = (bf16[64,2176]{1,0:T(8,128)(2,1)S(1)}, bf16[64,2176]{1,0:T(8,128)(2,1)S(1)}, u32[]{:S(2)}, u32[]{:S(2)}) collective-permute-start(bf16[64,2176]{1,0:T(8,128)(2,1)S(1)} %get-tuple-element.146.refs_1_.refs_3_), channel_id=1, source_target_pairs={{0,4},{1,5},{2,6},{3,7},{4,0},{5,1},{6,2},{7,3},{8,12},{9,13},{10,... | collective-permute-start | bytes 835592 | tf_op jit(solution)/shard_map/ppermute | solution.py:34
  172.1 25.2 %collective-permute-start.33 = (bf16[64,2176]{1,0:T(8,128)(2,1)S(1)}, bf16[64,2176]{1,0:T(8,128)(2,1)S(1)}, u32[]{:S(2)}, u32[]{:S(2)}) collective-permute-start(bf16[64,2176]{1,0:T(8,128)(2,1)S(1)} %get-tuple-element.146.refs_1_.refs_3_), channel_id=1, source_target_pairs={{0,2},{1,3},{2,0},{3,1},{4,6},{5,7},{6,4},{7,5},{8,10},{9,11},{10,... | collective-permute-start | bytes 835592 | tf_op jit(solution)/shard_map/ppermute | solution.py:34
  241.1 32.3 %collective-permute-start.68 = (bf16[64,2176]{1,0:T(8,128)(2,1)}, bf16[64,2176]{1,0:T(8,128)(2,1)}, u32[]{:S(2)}, u32[]{:S(2)}) collective-permute-start(bf16[64,2176]{1,0:T(8,128)(2,1)} %collective-permute-done.67.refs_11_), channel_id=1, source_target_pairs={{0,1},{1,0},{2,3},{3,2},{4,5},{5,4},{6,7},{7,6},{8,9},{9,8},{10,11... | collective-permute-start | bytes 835592 | tf_op jit(solution)/shard_map/ppermute | solution.py:34
  241.9 31.6 %collective-permute-start.62 = (bf16[64,2176]{1,0:T(8,128)(2,1)}, bf16[64,2176]{1,0:T(8,128)(2,1)}, u32[]{:S(2)}, u32[]{:S(2)}) collective-permute-start(bf16[64,2176]{1,0:T(8,128)(2,1)} %held.10.refs_5_), channel_id=1, source_target_pairs={{0,1},{1,0},{2,3},{3,2},{4,5},{5,4},{6,7},{7,6},{8,9},{9,8},{10,11... | collective-permute-start | bytes 835592 | tf_op jit(solution)/shard_map/ppermute | solution.py:34
  243.1 30.4 %collective-permute-start.64 = (bf16[64,2176]{1,0:T(8,128)(2,1)}, bf16[64,2176]{1,0:T(8,128)(2,1)}, u32[]{:S(2)}, u32[]{:S(2)}) collective-permute-start(bf16[64,2176]{1,0:T(8,128)(2,1)} %collective-permute-done.63.refs_7_), channel_id=1, source_target_pairs={{0,1},{1,0},{2,3},{3,2},{4,5},{5,4},{6,7},{7,6},{8,9},{9,8},{10,11... | collective-permute-start | bytes 835592 | tf_op jit(solution)/shard_map/ppermute | solution.py:34
  248.3 25.2 %collective-permute-start.70 = (bf16[64,2176]{1,0:T(8,128)(2,1)}, bf16[64,2176]{1,0:T(8,128)(2,1)}, u32[]{:S(2)}, u32[]{:S(2)}) collective-permute-start(bf16[64,2176]{1,0:T(8,128)(2,1)} %collective-permute-done.69.refs_13_), channel_id=1, source_target_pairs={{0,1},{1,0},{2,3},{3,2},{4,5},{5,4},{6,7},{7,6},{8,9},{9,8},{10,11... | collective-permute-start | bytes 835592 | tf_op jit(solution)/shard_map/ppermute | solution.py:34
  315.0 30.8 %collective-permute-start.77 = (bf16[256,2176]{1,0:T(8,128)(2,1)}, bf16[256,2176]{1,0:T(8,128)(2,1)S(1)}, u32[]{:S(2)}, u32[]{:S(2)}) collective-permute-start(bf16[256,2176]{1,0:T(8,128)(2,1)} %get-tuple-element.160), channel_id=1, source_target_pairs={{0,1},{1,0},{2,3},{3,2},{4,5},{5,4},{6,7},{7,6},{8,9},{9,8},{10,11... | collective-permute-start | bytes 3342344 | tf_op jit(solution)/shard_map/ppermute | solution.py:34
  318.9 27.0 %collective-permute-start.78 = (bf16[256,2176]{1,0:T(8,128)(2,1)S(1)}, bf16[256,2176]{1,0:T(8,128)(2,1)S(1)}, u32[]{:S(2)}, u32[]{:S(2)}) collective-permute-start(bf16[256,2176]{1,0:T(8,128)(2,1)S(1)} %combined.27.refs_4_), channel_id=1, source_target_pairs={{0,2},{1,3},{2,0},{3,1},{4,6},{5,7},{6,4},{7,5},{8,10},{9,11},{10,... | collective-permute-start | bytes 3342344 | tf_op jit(solution)/shard_map/ppermute | solution.py:34
  321.7 21.5 %collective-permute-start.76 = (bf16[128,2176]{1,0:T(8,128)(2,1)}, bf16[128,2176]{1,0:T(8,128)(2,1)}, u32[]{:S(2)}, u32[]{:S(2)}) collective-permute-start(bf16[128,2176]{1,0:T(8,128)(2,1)} %get-tuple-element.154.refs_3_), channel_id=1, source_target_pairs={{0,4},{1,5},{2,6},{3,7},{4,0},{5,1},{6,2},{7,3},{8,12},{9,13},{10,... | collective-permute-start | bytes 1671176 | tf_op jit(solution)/shard_map/ppermute | solution.py:34
  343.2 31.4 %collective-permute-start.86 = (bf16[256,2048]{1,0:T(8,128)(2,1)}, bf16[256,2048]{1,0:T(8,128)(2,1)S(1)}, u32[]{:S(2)}, u32[]{:S(2)}) collective-permute-start(bf16[256,2048]{1,0:T(8,128)(2,1)} %get-tuple-element.174), channel_id=1, source_target_pairs={{0,1},{1,0},{2,3},{3,2},{4,5},{5,4},{6,7},{7,6},{8,9},{9,8},{10,11... | collective-permute-start | bytes 3145736 | tf_op jit(solution)/shard_map/ppermute | solution.py:34
  372.8 26.7 %collective-permute-start.85 = (bf16[128,2176]{1,0:T(8,128)(2,1)S(1)}, bf16[128,2176]{1,0:T(8,128)(2,1)}, u32[]{:S(2)}, u32[]{:S(2)}) collective-permute-start(bf16[128,2176]{1,0:T(8,128)(2,1)S(1)} %combined.30.refs_2_.refs_0_), channel_id=1, source_target_pairs={{0,16},{1,17},{2,18},{3,19},{4,20},{5,21},{6,22},{7,23},{8,24},{9,... | collective-permute-start | bytes 1671176 | tf_op jit(solution)/shard_map/ppermute | solution.py:34
  373.7 25.9 %collective-permute-start.84 = (bf16[128,2176]{1,0:T(8,128)(2,1)}, bf16[128,2176]{1,0:T(8,128)(2,1)}, u32[]{:S(2)}, u32[]{:S(2)}) collective-permute-start(bf16[128,2176]{1,0:T(8,128)(2,1)} %get-tuple-element.161.refs_3_), channel_id=1, source_target_pairs={{0,4},{1,5},{2,6},{3,7},{4,0},{5,1},{6,2},{7,3},{8,12},{9,13},{10,... | collective-permute-start | bytes 1671176 | tf_op jit(solution)/shard_map/ppermute | solution.py:34
  375.7 25.6 %collective-permute-start.89 = (bf16[128,2048]{1,0:T(8,128)(2,1)}, bf16[128,2048]{1,0:T(8,128)(2,1)S(1)}, u32[]{:S(2)}, u32[]{:S(2)}) collective-permute-start(bf16[128,2048]{1,0:T(8,128)(2,1)} %get-tuple-element.175.refs_4_), channel_id=1, source_target_pairs={{0,4},{1,5},{2,6},{3,7},{4,0},{5,1},{6,2},{7,3},{8,12},{9,13},{10,... | collective-permute-start | bytes 1572872 | tf_op jit(solution)/shard_map/ppermute | solution.py:34
  376.9 50.2 %collective-permute-start.79 = (bf16[256,2048]{1,0:T(8,128)(2,1)}, bf16[256,2048]{1,0:T(8,128)(2,1)S(1)}, u32[]{:S(2)}, u32[]{:S(2)}) collective-permute-start(bf16[256,2048]{1,0:T(8,128)(2,1)} %get-tuple-element.163), channel_id=1, source_target_pairs={{0,1},{1,0},{2,3},{3,2},{4,5},{5,4},{6,7},{7,6},{8,9},{9,8},{10,11... | collective-permute-start | bytes 3145736 | tf_op jit(solution)/shard_map/ppermute | solution.py:34
  377.3 49.8 %collective-permute-start.83 = (bf16[256,2048]{1,0:T(8,128)(2,1)S(1)}, bf16[256,2048]{1,0:T(8,128)(2,1)S(1)}, u32[]{:S(2)}, u32[]{:S(2)}) collective-permute-start(bf16[256,2048]{1,0:T(8,128)(2,1)S(1)} %combined.31.refs_6_), channel_id=1, source_target_pairs={{0,2},{1,3},{2,0},{3,1},{4,6},{5,7},{6,4},{7,5},{8,10},{9,11},{10,... | collective-permute-start | bytes 3145736 | tf_op jit(solution)/shard_map/ppermute | solution.py:34
  425.4 21.9 %collective-permute-start.95 = (bf16[128,2048]{1,0:T(8,128)(2,1)S(1)}, bf16[128,2048]{1,0:T(8,128)(2,1)S(1)}, u32[]{:S(2)}, u32[]{:S(2)}) collective-permute-start(bf16[128,2048]{1,0:T(8,128)(2,1)S(1)} %combined.36), channel_id=1, source_target_pairs={{0,2},{1,3},{2,0},{3,1},{4,6},{5,7},{6,4},{7,5},{8,10},{9,11},{10,... | collective-permute-start | bytes 1572872 | tf_op jit(solution)/shard_map/ppermute | solution.py:34
  450.8 40.3 %collective-permute-start.101 = (bf16[4,256,768]{2,1,0:T(8,128)(2,1)S(1)}, bf16[4,256,768]{2,1,0:T(8,128)(2,1)S(1)}, u32[]{:S(2)}, u32[]{:S(2)}) collective-permute-start(bf16[4,256,768]{2,1,0:T(8,128)(2,1)S(1)} %get-tuple-element.199.refs_12_), channel_id=1, source_target_pairs={{0,4},{1,5},{2,6},{3,7},{4,0},{5,1},{6,2},{7,3},{8,12},{9,13},{10,... | collective-permute-start | bytes 4718600 | tf_op jit(solution)/shard_map/ppermute | solution.py:34
  459.6 26.0 %collective-permute-start.97 = (bf16[128,2048]{1,0:T(8,128)(2,1)S(1)}, bf16[128,2048]{1,0:T(8,128)(2,1)S(1)}, u32[]{:S(2)}, u32[]{:S(2)}) collective-permute-start(bf16[128,2048]{1,0:T(8,128)(2,1)S(1)} %combined.37), channel_id=1, source_target_pairs={{0,16},{1,17},{2,18},{3,19},{4,20},{5,21},{6,22},{7,23},{8,24},{9,... | collective-permute-start | bytes 1572872 | tf_op jit(solution)/shard_map/ppermute | solution.py:34
  491.8 36.7 %collective-permute-start.106 = (bf16[2,256,768]{2,1,0:T(8,128)(2,1)S(1)}, bf16[2,256,768]{2,1,0:T(8,128)(2,1)S(1)}, u32[]{:S(2)}, u32[]{:S(2)}) collective-permute-start(bf16[2,256,768]{2,1,0:T(8,128)(2,1)S(1)} %get-tuple-element.204.refs_4_.refs_3_), channel_id=1, source_target_pairs={{0,16},{1,17},{2,18},{3,19},{4,20},{5,21},{6,22},{7,23},{8,24},{9,... | collective-permute-start | bytes 2359304 | tf_op jit(solution)/shard_map/ppermute | solution.py:34
  493.1 50.7 %collective-permute-start.120 = (bf16[256,2048]{1,0:T(8,128)(2,1)}, bf16[256,2048]{1,0:T(8,128)(2,1)}, u32[]{:S(2)}, u32[]{:S(2)}) collective-permute-start(bf16[256,2048]{1,0:T(8,128)(2,1)} %held.11), channel_id=1, source_target_pairs={{0,8},{1,9},{2,10},{3,11},{4,12},{5,13},{6,14},{7,15},{8,0},{9,1},... | collective-permute-start | bytes 3145736 | tf_op jit(solution)/shard_map/ppermute | solution.py:34
  497.2 32.0 %collective-permute-start.111 = (f32[64,2048]{1,0:T(8,128)}, f32[64,2048]{1,0:T(8,128)}, u32[]{:S(2)}, u32[]{:S(2)}) collective-permute-start(f32[64,2048]{1,0:T(8,128)} %get-tuple-element.208), channel_id=1, source_target_pairs={{0,2},{1,3},{2,0},{3,1},{4,6},{5,7},{6,4},{7,5},{8,10},{9,11},{10,... | collective-permute-start | bytes 1572872 | tf_op jit(solution)/shard_map/ppermute | solution.py:34
  529.1 23.0 %collective-permute-start.113 = (f32[64,2048]{1,0:T(8,128)}, f32[64,2048]{1,0:T(8,128)}, u32[]{:S(2)}, u32[]{:S(2)}) collective-permute-start(f32[64,2048]{1,0:T(8,128)} %get-tuple-element.208), channel_id=1, source_target_pairs={{0,1},{1,0},{2,3},{3,2},{4,5},{5,4},{6,7},{7,6},{8,9},{9,8},{10,11... | collective-permute-start | bytes 1572872 | tf_op jit(solution)/shard_map/ppermute | solution.py:34
  529.2 23.0 %collective-permute-start.112 = (f32[64,2048]{1,0:T(8,128)}, f32[64,2048]{1,0:T(8,128)}, u32[]{:S(2)}, u32[]{:S(2)}) collective-permute-start(f32[64,2048]{1,0:T(8,128)} %collective-permute-done.111), channel_id=1, source_target_pairs={{0,1},{1,0},{2,3},{3,2},{4,5},{5,4},{6,7},{7,6},{8,9},{9,8},{10,11... | collective-permute-start | bytes 1572872 | tf_op jit(solution)/shard_map/ppermute | solution.py:34
  548.5 25.5 %collective-permute-start.119 = (bf16[1,256,768]{2,1,0:T(8,128)(2,1)S(1)}, bf16[1,256,768]{2,1,0:T(8,128)(2,1)S(1)}, u32[]{:S(2)}, u32[]{:S(2)}) collective-permute-start(bf16[1,256,768]{2,1,0:T(8,128)(2,1)S(1)} %get-tuple-element.228.refs_2_), channel_id=1, source_target_pairs={{0,8},{1,9},{2,10},{3,11},{4,12},{5,13},{6,14},{7,15},{8,0},{9,1},... | collective-permute-start | bytes 1179656 | tf_op jit(solution)/shard_map/ppermute | solution.py:34
  550.8 25.3 %collective-permute-start.108 = (f32[64,2048]{1,0:T(8,128)S(1)}, f32[64,2048]{1,0:T(8,128)S(1)}, u32[]{:S(2)}, u32[]{:S(2)}) collective-permute-start(f32[64,2048]{1,0:T(8,128)S(1)} %combined.42), channel_id=1, source_target_pairs={{0,2},{1,3},{2,0},{3,1},{4,6},{5,7},{6,4},{7,5},{8,10},{9,11},{10,... | collective-permute-start | bytes 1572872 | tf_op jit(solution)/shard_map/ppermute | solution.py:34
  (232 other events, 3130.5 us)

commit v6 on v5

--- a/solution.py
+++ b/solution.py
@@ -1333,7 +1333,7 @@
     for_mate = combined([term[share:] for term in terms], 0)
     from_mate = over_z(for_mate, 1)
     head_sums_at.along_z(moe.from_top, from_mate)
-    mates_low = over_z(held(low_pieces, bf16, [for_mate]), 1)
+    mates_low = over_z(held(low_pieces, bf16, [inner]), 1)
     mark = some_grads(2, mark, head_sums_at.sent)
     moe = moe.last(head_sums_at.came)
     low_slabs = paired(low_pieces, [mates_low], places, data_size)

time: 593 us -> 595 us (level)
    unnamed x280 -> x284, local copies, waits for them, and re-layouts: 40.2 us -> 41.9 us
where the time goes in v6:
time: 595 us; the launch traced here: 585 us
  waiting for transfers between devices  249 us (42%)
  Pallas kernels  176 us (30%)
  starting transfers between devices  93.3 us (16%)
  local copies, waits for them, and re-layouts  48.6 us (8%)
  other arithmetic  14.1 us (2%)
    ppermute x124, waiting for transfers between devices, swap(): return lax.ppermute(values, ('dp', 'tp'), pairs)  249 us
    ppermute x124, starting transfers between devices, swap(): return lax.ppermute(values, ('dp', 'tp'), pairs)  93.3 us
    pallas_call x49, Pallas kernels, kernel_call(): pl.pallas_call(body, in_specs=[pl.BlockSpec(memory_space=pltpu.SMEM)] * l...  55.7 us
    pallas_call x3, Pallas kernels, per_expert(): pl.pallas_call(without(kernel, len(in_specs), len(waits)), grid=(experts,...  44 us
    unnamed x284, local copies, waits for them, and re-layouts  41.9 us
    pallas_call x4, Pallas kernels, expert_weight_grads(): pl.pallas_call(kernel, grid=(count,), in_specs=[block(rows // 2, width)]...  31.5 us
    pallas_call x4, Pallas kernels, tokens_of_slots(): pl.pallas_call(without(kernel, 2, len(waits)), grid=(sequences,), in_spec...  25.3 us
    pallas_call x3, Pallas kernels, rows_of_slots(): pl.pallas_call(without(kernel, 1 + len(flat), len(waits)), grid=(sequence...  19.9 us
  transfers between devices with their start and end apart: 124, of which 45 were waited for; matrix products, arithmetic and copies ran while one was open for 2% of the time, Pallas kernels for 23%

profile of v6, /device:TPU:0, one launch (start us, length us, event | category | flops | bytes accessed | tf_op | source)
XLA Modules:
  0.0 585.0 jit_solution(13618417363808728067)
XLA Ops:
  24.9 6.3 %collective-permute-done.2.refs_4_ = bf16[83,256]{1,0:T(8,128)(2,1)S(1)} collective-permute-done((bf16[83,256]{1,0:T(8,128)(2,1)S(1)}, bf16[83,256]{1,0:T(8,128)(2,1)S(1)}, u32[]{:S(2)}, u32[]{:S(2)}) %collective-permute-start.2) | collective-permute-done | bytes 42528 | tf_op jit(solution)/shard_map/ppermute | solution.py:34
  43.0 8.6 %collective-permute-done.48.refs_2_ = bf16[64,2048]{1,0:T(8,128)(2,1)S(1)} collective-permute-done((bf16[64,2048]{1,0:T(8,128)(2,1)S(1)}, bf16[64,2048]{1,0:T(8,128)(2,1)S(1)}, u32[]{:S(2)}, u32[]{:S(2)}) %collective-permute-start.48) | collective-permute-done | bytes 262176 | tf_op jit(solution)/shard_map/ppermute | solution.py:34
  67.1 16.7 %collective-permute-done.12.refs_4_.refs_6_ = bf16[256,768]{1,0:T(8,128)(2,1)S(1)} collective-permute-done((bf16[256,768]{1,0:T(8,128)(2,1)S(1)}, bf16[256,768]{1,0:T(8,128)(2,1)S(1)}, u32[]{:S(2)}, u32[]{:S(2)}) %collective-permute-start.12) | collective-permute-done | bytes 393248 | tf_op jit(solution)/shard_map/ppermute | solution.py:34
  85.4 6.8 %collective-permute-done.13.refs_5_.refs_1_.refs_7_ = bf16[256,768]{1,0:T(8,128)(2,1)S(1)} collective-permute-done((bf16[256,768]{1,0:T(8,128)(2,1)S(1)}, bf16[256,768]{1,0:T(8,128)(2,1)S(1)}, u32[]{:S(2)}, u32[]{:S(2)}) %collective-permute-start.13) | collective-permute-done | bytes 393248 | tf_op jit(solution)/shard_map/ppermute | solution.py:34
  95.8 8.4 %collective-permute-done.16.refs_8_.refs_10_ = bf16[256,768]{1,0:T(8,128)(2,1)S(1)} collective-permute-done((bf16[256,768]{1,0:T(8,128)(2,1)S(1)}, bf16[256,768]{1,0:T(8,128)(2,1)S(1)}, u32[]{:S(2)}, u32[]{:S(2)}) %collective-permute-start.16) | collective-permute-done | bytes 393248 | tf_op jit(solution)/shard_map/ppermute | solution.py:34
  104.3 8.0 %collective-permute-done.17.refs_9_.refs_11_ = bf16[256,768]{1,0:T(8,128)(2,1)S(1)} collective-permute-done((bf16[256,768]{1,0:T(8,128)(2,1)S(1)}, bf16[256,768]{1,0:T(8,128)(2,1)S(1)}, u32[]{:S(2)}, u32[]{:S(2)}) %collective-permute-start.17) | collective-permute-done | bytes 393248 | tf_op jit(solution)/shard_map/ppermute | solution.py:34
  123.9 14.1 %collective-permute-done.22.refs_9_.refs_5_.refs_7_ = bf16[512,256]{1,0:T(8,128)(2,1)S(1)} collective-permute-done((bf16[512,256]{1,0:T(8,128)(2,1)S(1)}, bf16[512,256]{1,0:T(8,128)(2,1)S(1)}, u32[]{:S(2)}, u32[]{:S(2)}) %collective-permute-start.22) | collective-permute-done | bytes 262176 | tf_op jit(solution)/shard_map/ppermute | solution.py:34
  147.2 5.6 collective-permute-done.27.refs_9_.refs_11_
  162.8 6.6 %collective-permute-done.31.refs_2_ = bf16[64,2048]{1,0:T(8,128)(2,1)S(1)} collective-permute-done((bf16[64,2048]{1,0:T(8,128)(2,1)S(1)}, bf16[64,2048]{1,0:T(8,128)(2,1)S(1)}, u32[]{:S(2)}, u32[]{:S(2)}) %collective-permute-start.31) | collective-permute-done | bytes 262176 | tf_op jit(solution)/shard_map/ppermute | solution.py:34
  172.6 8.2 %collective-permute-done.35.refs_5_.refs_0_ = bf16[64,2176]{1,0:T(8,128)(2,1)S(1)} collective-permute-done((bf16[64,2176]{1,0:T(8,128)(2,1)S(1)}, bf16[64,2176]{1,0:T(8,128)(2,1)S(1)}, u32[]{:S(2)}, u32[]{:S(2)}) %collective-permute-start.35) | collective-permute-done | bytes 278560 | tf_op jit(solution)/shard_map/ppermute | solution.py:34
  182.5 9.5 %rows_of_slots.3.refs_0_.refs_1_.cot_ref = bf16[8,384,2048]{2,1,0:T(8,128)(2,1)} custom-call(s32[8,8,256]{2,1,0:T(8,128)S(1)} %get-tuple-element.145.refs_0_, bf16[512,2048]{1,0:T(8,128)(2,1)S(1)} %held.7.refs_1_, bf16[512,2048]{1,0:T(8,128)(2,1)S(1)} %collective-permute-done.54.refs_2_, bf16[512,2048]{1,0:T(8,128)(2,1)} %copy-done.8, ...), custom_call_target="tpu_custom_call" | custom-call | flops 3221 | bytes 20 | tf_op jit(solution)/shard_map/rows_of_slots/pallas_call | solution.py:307
  215.4 10.6 %grad_of_hidden.1.refs_17_.refs_1_.refs_5_ = f32[8,384,256]{2,1,0:T(8,128)S(1)} custom-call(bf16[8,384,2048]{2,1,0:T(8,128)(2,1)} %rows_of_slots.3.refs_0_.refs_1_.cot_ref, bf16[8,256,2048]{2,1,0:T(8,128)(2,1)} %refs_1_.5), custom_call_target="tpu_custom_call" | custom-call | flops 3221 | bytes 24 | tf_op jit(solution)/shard_map/grad_of_hidden/pallas_call | solution.py:381
  273.5 5.3 rows_of_slots.5.refs_2_.b_ref
  278.8 21.9 %expert_step.1 = (bf16[8,384,2176]{2,1,0:T(8,128)(2,1)}, bf16[8,384,256]{2,1,0:T(8,128)(2,1)S(1)}, bf16[8,384,256]{2,1,0:T(8,128)(2,1)S(1)}, bf16[8,384,256]{2,1,0:T(8,128)(2,1)S(1)}) custom-call(s32[1]{0:T(128)} %bitcast.7.refs_0_, bf16[8,192,2176]{2,1,0:T(8,128)(2,1)} %rows_of_slots.4.refs_17_.refs_1_.a_ref, ...), custom_call_target="tpu_custom_call" | custom-call | flops 12884 | bytes 51 | tf_op jit(solution)/shard_map/expert_step/pallas_call | solution.py:381
  300.7 7.0 %tokens_of_slots.4 = (bf16[256,2176]{1,0:T(8,128)(2,1)S(1)}, bf16[256,2176]{1,0:T(8,128)(2,1)}, bf16[256,2176]{1,0:T(8,128)(2,1)S(1)}, bf16[256,2176]{1,0:T(8,128)(2,1)}) custom-call(s32[4,8,256]{2,1,0:T(8,128)S(1)} %get-tuple-element.254.refs_0_, bf16[8,384,2176]{2,1,0:T(8,128)(2,1)} %get-tuple-element.148.refs_1_), custom_call_target="tpu_custom_call" | custom-call | flops 1711 | bytes 11 | tf_op jit(solution)/shard_map/tokens_of_slots/pallas_call | solution.py:345
  307.7 6.2 %tokens_of_slots.5 = (bf16[256,2176]{1,0:T(8,128)(2,1)S(1)}, bf16[256,2176]{1,0:T(8,128)(2,1)}, bf16[256,2176]{1,0:T(8,128)(2,1)S(1)}, bf16[256,2176]{1,0:T(8,128)(2,1)S(1)}) custom-call(s32[4,8,256]{2,1,0:T(8,128)S(1)} %get-tuple-element.255.refs_0_, bf16[8,384,2176]{2,1,0:T(8,128)(2,1)} %get-tuple-element.148.refs_1_, ...), custom_call_target="tpu_custom_call" | custom-call | flops 1711 | bytes 11 | tf_op jit(solution)/shard_map/tokens_of_slots/pallas_call | solution.py:345
  323.1 11.5 %expert_out.1.refs_1_ = bf16[8,384,2048]{2,1,0:T(8,128)(2,1)} custom-call(bf16[8,384,256]{2,1,0:T(8,128)(2,1)S(1)} %get-tuple-element.147.refs_0_.act_ref, bf16[8,256,2048]{2,1,0:T(8,128)(2,1)} %refs_1_.5, bf16[128,2176]{1,0:T(8,128)(2,1)S(1)} %get-tuple-element.151.refs_2_, bf16[128,2176]{1,0:T(8,128)(2,1)} %get-tuple-element.154.refs_3_, ...), custom_call_target="tpu_custom_call" | custom-call | flops 3221 | bytes 22 | tf_op jit(solution)/shard_map/expert_out/pallas_call | solution.py:381
  335.4 5.9 %tokens_of_slots.6 = (bf16[256,2048]{1,0:T(8,128)(2,1)S(1)}, bf16[256,2048]{1,0:T(8,128)(2,1)}, bf16[256,2048]{1,0:T(8,128)(2,1)S(1)}, bf16[256,2048]{1,0:T(8,128)(2,1)S(1)}) custom-call(s32[4,8,256]{2,1,0:T(8,128)S(1)} %get-tuple-element.254.refs_0_, bf16[8,384,2048]{2,1,0:T(8,128)(2,1)} %expert_out.1.refs_1_), custom_call_target="tpu_custom_call" | custom-call | flops 1610 | bytes 10 | tf_op jit(solution)/shard_map/tokens_of_slots/pallas_call | solution.py:345
  349.6 6.1 %tokens_of_slots.7 = (bf16[256,2048]{1,0:T(8,128)(2,1)S(1)}, bf16[256,2048]{1,0:T(8,128)(2,1)}, bf16[256,2048]{1,0:T(8,128)(2,1)S(1)}, bf16[256,2048]{1,0:T(8,128)(2,1)S(1)}) custom-call(s32[4,8,256]{2,1,0:T(8,128)S(1)} %get-tuple-element.255.refs_0_, bf16[8,384,2048]{2,1,0:T(8,128)(2,1)} %expert_out.1.refs_1_, bf16[128,2176]{1,0:T(8,128)(2,1)S(1)} %combined.28.refs_2_, ...), custom_call_target="tpu_custom_call" | custom-call | flops 1610 | bytes 10 | tf_op jit(solution)/shard_map/tokens_of_slots/pallas_call | solution.py:345
  358.4 12.9 %collective-permute-done.81.refs_1_ = bf16[128,2176]{1,0:T(8,128)(2,1)S(1)} collective-permute-done((bf16[128,2176]{1,0:T(8,128)(2,1)S(1)}, bf16[128,2176]{1,0:T(8,128)(2,1)S(1)}, u32[]{:S(2)}, u32[]{:S(2)}) %collective-permute-start.81) | collective-permute-done | bytes 557088 | tf_op jit(solution)/shard_map/ppermute | solution.py:34
  379.2 7.9 %expert_weight_grads.4 = (f32[8,2048,256]{2,1,0:T(8,128)}, f32[8,2048,256]{2,1,0:T(8,128)}, f32[8,256,2048]{2,1,0:T(8,128)}, f32[8,128]{1,0:T(8,128)S(1)}) custom-call(bf16[8,192,2176]{2,1,0:T(8,128)(2,1)} %rows_of_slots.4.refs_17_.refs_1_.a_ref, bf16[8,192,2176]{2,1,0:T(8,128)(2,1)} %rows_of_slots.5.refs_2_.b_ref, ...), custom_call_target="tpu_custom_call" | custom-call | flops 2415 | bytes 19 | tf_op jit(solution)/shard_map/expert_weight_grads/pallas_call | solution.py:495
  387.5 7.8 %expert_weight_grads.5 = (f32[8,2048,256]{2,1,0:T(8,128)}, f32[8,2048,256]{2,1,0:T(8,128)}, f32[8,256,2048]{2,1,0:T(8,128)}, f32[8,128]{1,0:T(8,128)S(1)}) custom-call(bf16[8,192,2176]{2,1,0:T(8,128)(2,1)} %rows_of_slots.4.refs_17_.refs_1_.a_ref, ...), custom_call_target="tpu_custom_call", output_to_operand_aliasing={{0}: (6, {}), {1}: (7, {}), {2}: (8, {})} | custom-call | flops 2415 | bytes 19 | tf_op jit(solution)/shard_map/expert_weight_grads/pallas_call | solution.py:495
  401.2 8.6 %collective-permute-done.88.refs_1_ = bf16[64,2176]{1,0:T(8,128)(2,1)S(1)} collective-permute-done((bf16[64,2176]{1,0:T(8,128)(2,1)S(1)}, bf16[64,2176]{1,0:T(8,128)(2,1)S(1)}, u32[]{:S(2)}, u32[]{:S(2)}) %collective-permute-start.88) | collective-permute-done | bytes 278560 | tf_op jit(solution)/shard_map/ppermute | solution.py:34
  412.7 6.6 %collective-permute-done.91.refs_3_.refs_2_ = bf16[64,2048]{1,0:T(8,128)(2,1)S(1)} collective-permute-done((bf16[64,2048]{1,0:T(8,128)(2,1)S(1)}, bf16[64,2048]{1,0:T(8,128)(2,1)S(1)}, u32[]{:S(2)}, u32[]{:S(2)}) %collective-permute-start.91) | collective-permute-done | bytes 262176 | tf_op jit(solution)/shard_map/ppermute | solution.py:34
  462.7 10.2 %collective-permute-done.104.refs_2_ = bf16[128,2048]{1,0:T(8,128)(2,1)S(1)} collective-permute-done((bf16[128,2048]{1,0:T(8,128)(2,1)S(1)}, bf16[128,2048]{1,0:T(8,128)(2,1)S(1)}, u32[]{:S(2)}, u32[]{:S(2)}) %collective-permute-start.104) | collective-permute-done | bytes 524320 | tf_op jit(solution)/shard_map/ppermute | solution.py:34
  473.8 11.8 %collective-permute-done.97.refs_2_ = bf16[128,2048]{1,0:T(8,128)(2,1)S(1)} collective-permute-done((bf16[128,2048]{1,0:T(8,128)(2,1)S(1)}, bf16[128,2048]{1,0:T(8,128)(2,1)S(1)}, u32[]{:S(2)}, u32[]{:S(2)}) %collective-permute-start.97) | collective-permute-done | bytes 524320 | tf_op jit(solution)/shard_map/ppermute | solution.py:34
  485.6 17.0 %collective-permute-done.105.refs_3_ = bf16[64,2048]{1,0:T(8,128)(2,1)S(1)} collective-permute-done((bf16[64,2048]{1,0:T(8,128)(2,1)S(1)}, bf16[64,2048]{1,0:T(8,128)(2,1)S(1)}, u32[]{:S(2)}, u32[]{:S(2)}) %collective-permute-start.105) | collective-permute-done | bytes 262176 | tf_op jit(solution)/shard_map/ppermute | solution.py:34
  513.1 8.0 %expert_weight_grads.6 = (f32[8,2048,256]{2,1,0:T(8,128)}, f32[8,2048,256]{2,1,0:T(8,128)}, f32[8,256,2048]{2,1,0:T(8,128)}, f32[8,128]{1,0:T(8,128)S(1)}) custom-call(bf16[8,192,2176]{2,1,0:T(8,128)(2,1)} %rows_of_slots.4.refs_17_.refs_1_.a_ref, ...), custom_call_target="tpu_custom_call", output_to_operand_aliasing={{0}: (6, {}), {1}: (7, {}), {2}: (8, {})} | custom-call | flops 2415 | bytes 19 | tf_op jit(solution)/shard_map/expert_weight_grads/pallas_call | solution.py:495
  521.1 7.8 %expert_weight_grads.7 = (f32[8,2048,256]{2,1,0:T(8,128)}, f32[8,2048,256]{2,1,0:T(8,128)}, f32[8,256,2048]{2,1,0:T(8,128)}, f32[8,128]{1,0:T(8,128)S(1)}) custom-call(bf16[8,192,2176]{2,1,0:T(8,128)(2,1)} %rows_of_slots.4.refs_17_.refs_1_.a_ref, ...), custom_call_target="tpu_custom_call", output_to_operand_aliasing={{0}: (6, {}), {1}: (7, {}), {2}: (8, {})} | custom-call | flops 2415 | bytes 19 | tf_op jit(solution)/shard_map/expert_weight_grads/pallas_call | solution.py:495
  528.9 10.2 %collective-permute-done.106.refs_3_.refs_2_.refs_1_ = bf16[2,256,768]{2,1,0:T(8,128)(2,1)S(1)} collective-permute-done((bf16[2,256,768]{2,1,0:T(8,128)(2,1)S(1)}, bf16[2,256,768]{2,1,0:T(8,128)(2,1)S(1)}, u32[]{:S(2)}, u32[]{:S(2)}) %collective-permute-start.106) | collective-permute-done | bytes 786464 | tf_op jit(solution)/shard_map/ppermute | solution.py:34
  544.3 8.0 %collective-permute-done.115.refs_1_ = f32[2,112,256]{2,1,0:T(8,128)S(1)} collective-permute-done((f32[2,112,256]{2,1,0:T(8,128)S(1)}, f32[2,112,256]{2,1,0:T(8,128)S(1)}, u32[]{:S(2)}, u32[]{:S(2)}) %collective-permute-start.115) | collective-permute-done | bytes 229408 | tf_op jit(solution)/shard_map/ppermute | solution.py:34
  564.2 6.5 %collective-permute-done.122.refs_1_ = bf16[2,256,256]{2,1,0:T(8,128)(2,1)S(1)} collective-permute-done((bf16[2,256,256]{2,1,0:T(8,128)(2,1)S(1)}, bf16[2,256,256]{2,1,0:T(8,128)(2,1)S(1)}, u32[]{:S(2)}, u32[]{:S(2)}) %collective-permute-start.122) | collective-permute-done | bytes 262176 | tf_op jit(solution)/shard_map/ppermute | solution.py:34
  (605 shorter events, 285.3 us)
Async XLA Ops:
  59.0 24.8 %collective-permute-start.12 = (bf16[256,768]{1,0:T(8,128)(2,1)S(1)}, bf16[256,768]{1,0:T(8,128)(2,1)S(1)}, u32[]{:S(2)}, u32[]{:S(2)}) collective-permute-start(bf16[256,768]{1,0:T(8,128)(2,1)S(1)} %get-tuple-element.130.refs_2_.refs_4_), channel_id=1, source_target_pairs={{0,16},{1,17},{2,18},{3,19},{4,20},{5,21},{6,22},{7,23},{8,24},{9,... | collective-permute-start | bytes 1179656 | tf_op jit(solution)/shard_map/ppermute | solution.py:34
  64.7 106.3 %collective-permute-start.55 = (bf16[512,2048]{1,0:T(8,128)(2,1)S(1)}, bf16[512,2048]{1,0:T(8,128)(2,1)S(1)}, u32[]{:S(2)}, u32[]{:S(2)}) collective-permute-start(bf16[512,2048]{1,0:T(8,128)(2,1)S(1)} %held.7.refs_1_), channel_id=1, source_target_pairs={{0,2},{1,3},{2,0},{3,1},{4,6},{5,7},{6,4},{7,5},{8,10},{9,11},{10,... | collective-permute-start | bytes 6291464 | tf_op jit(solution)/shard_map/ppermute | solution.py:34
  67.1 25.1 %collective-permute-start.13 = (bf16[256,768]{1,0:T(8,128)(2,1)S(1)}, bf16[256,768]{1,0:T(8,128)(2,1)S(1)}, u32[]{:S(2)}, u32[]{:S(2)}) collective-permute-start(bf16[256,768]{1,0:T(8,128)(2,1)S(1)} %collective-permute-done.7.refs_9_.refs_3_.refs_5_), channel_id=1, source_target_pairs={{0,16},{1,17},{2,18},{3,19},{4,20},{5,21},{6,22},{7,23},{8,24},{9,... | collective-permute-start | bytes 1179656 | tf_op jit(solution)/shard_map/ppermute | solution.py:34
  67.1 26.6 %collective-permute-start.9 = (bf16[64,2048]{1,0:T(8,128)(2,1)S(1)}, bf16[64,2048]{1,0:T(8,128)(2,1)S(1)}, u32[]{:S(2)}, u32[]{:S(2)}) collective-permute-start(bf16[64,2048]{1,0:T(8,128)(2,1)S(1)} %collective-permute-done.8.refs_2_), channel_id=1, source_target_pairs={{0,1},{1,0},{2,3},{3,2},{4,5},{5,4},{6,7},{7,6},{8,9},{9,8},{10,11... | collective-permute-start | bytes 786440 | tf_op jit(solution)/shard_map/ppermute | solution.py:34
  94.3 26.6 %collective-permute-start.21 = (bf16[512,256]{1,0:T(8,128)(2,1)S(1)}, bf16[512,256]{1,0:T(8,128)(2,1)S(1)}, u32[]{:S(2)}, u32[]{:S(2)}) collective-permute-start(bf16[512,256]{1,0:T(8,128)(2,1)S(1)} %held.6.refs_7_.refs_3_.refs_5_), channel_id=1, source_target_pairs={{0,8},{1,9},{2,10},{3,11},{4,12},{5,13},{6,14},{7,15},{8,0},{9,1},... | collective-permute-start | bytes 786440 | tf_op jit(solution)/shard_map/ppermute | solution.py:34
  120.9 22.6 %collective-permute-start.23 = (bf16[512,256]{1,0:T(8,128)(2,1)S(1)}, bf16[512,256]{1,0:T(8,128)(2,1)S(1)}, u32[]{:S(2)}, u32[]{:S(2)}) collective-permute-start(bf16[512,256]{1,0:T(8,128)(2,1)S(1)} %collective-permute-done.21.refs_8_.refs_4_.refs_6_), channel_id=1, source_target_pairs={{0,16},{1,17},{2,18},{3,19},{4,20},{5,21},{6,22},{7,23},{8,24},{9,... | collective-permute-start | bytes 786440 | tf_op jit(solution)/shard_map/ppermute | solution.py:34
  121.0 25.8 %collective-permute-start.25 = (bf16[512,256]{1,0:T(8,128)(2,1)S(1)}, bf16[512,256]{1,0:T(8,128)(2,1)S(1)}, u32[]{:S(2)}, u32[]{:S(2)}) collective-permute-start(bf16[512,256]{1,0:T(8,128)(2,1)S(1)} %held.6.refs_7_.refs_3_.refs_5_), channel_id=1, source_target_pairs={{0,4},{1,5},{2,6},{3,7},{4,0},{5,1},{6,2},{7,3},{8,12},{9,13},{10,... | collective-permute-start | bytes 786440 | tf_op jit(solution)/shard_map/ppermute | solution.py:34
  171.7 24.9 %collective-permute-start.39 = (bf16[64,2176]{1,0:T(8,128)(2,1)S(1)}, bf16[64,2176]{1,0:T(8,128)(2,1)S(1)}, u32[]{:S(2)}, u32[]{:S(2)}) collective-permute-start(bf16[64,2176]{1,0:T(8,128)(2,1)S(1)} %get-tuple-element.146.refs_1_.refs_3_), channel_id=1, source_target_pairs={{0,4},{1,5},{2,6},{3,7},{4,0},{5,1},{6,2},{7,3},{8,12},{9,13},{10,... | collective-permute-start | bytes 835592 | tf_op jit(solution)/shard_map/ppermute | solution.py:34
  172.1 25.2 %collective-permute-start.33 = (bf16[64,2176]{1,0:T(8,128)(2,1)S(1)}, bf16[64,2176]{1,0:T(8,128)(2,1)S(1)}, u32[]{:S(2)}, u32[]{:S(2)}) collective-permute-start(bf16[64,2176]{1,0:T(8,128)(2,1)S(1)} %get-tuple-element.146.refs_1_.refs_3_), channel_id=1, source_target_pairs={{0,2},{1,3},{2,0},{3,1},{4,6},{5,7},{6,4},{7,5},{8,10},{9,11},{10,... | collective-permute-start | bytes 835592 | tf_op jit(solution)/shard_map/ppermute | solution.py:34
  241.1 32.3 %collective-permute-start.68 = (bf16[64,2176]{1,0:T(8,128)(2,1)}, bf16[64,2176]{1,0:T(8,128)(2,1)}, u32[]{:S(2)}, u32[]{:S(2)}) collective-permute-start(bf16[64,2176]{1,0:T(8,128)(2,1)} %collective-permute-done.67.refs_11_), channel_id=1, source_target_pairs={{0,1},{1,0},{2,3},{3,2},{4,5},{5,4},{6,7},{7,6},{8,9},{9,8},{10,11... | collective-permute-start | bytes 835592 | tf_op jit(solution)/shard_map/ppermute | solution.py:34
  241.8 31.6 %collective-permute-start.62 = (bf16[64,2176]{1,0:T(8,128)(2,1)}, bf16[64,2176]{1,0:T(8,128)(2,1)}, u32[]{:S(2)}, u32[]{:S(2)}) collective-permute-start(bf16[64,2176]{1,0:T(8,128)(2,1)} %held.10.refs_5_), channel_id=1, source_target_pairs={{0,1},{1,0},{2,3},{3,2},{4,5},{5,4},{6,7},{7,6},{8,9},{9,8},{10,11... | collective-permute-start | bytes 835592 | tf_op jit(solution)/shard_map/ppermute | solution.py:34
  243.1 30.4 %collective-permute-start.64 = (bf16[64,2176]{1,0:T(8,128)(2,1)}, bf16[64,2176]{1,0:T(8,128)(2,1)}, u32[]{:S(2)}, u32[]{:S(2)}) collective-permute-start(bf16[64,2176]{1,0:T(8,128)(2,1)} %collective-permute-done.63.refs_7_), channel_id=1, source_target_pairs={{0,1},{1,0},{2,3},{3,2},{4,5},{5,4},{6,7},{7,6},{8,9},{9,8},{10,11... | collective-permute-start | bytes 835592 | tf_op jit(solution)/shard_map/ppermute | solution.py:34
  248.3 25.2 %collective-permute-start.70 = (bf16[64,2176]{1,0:T(8,128)(2,1)}, bf16[64,2176]{1,0:T(8,128)(2,1)}, u32[]{:S(2)}, u32[]{:S(2)}) collective-permute-start(bf16[64,2176]{1,0:T(8,128)(2,1)} %collective-permute-done.69.refs_13_), channel_id=1, source_target_pairs={{0,1},{1,0},{2,3},{3,2},{4,5},{5,4},{6,7},{7,6},{8,9},{9,8},{10,11... | collective-permute-start | bytes 835592 | tf_op jit(solution)/shard_map/ppermute | solution.py:34
  315.0 30.9 %collective-permute-start.77 = (bf16[256,2176]{1,0:T(8,128)(2,1)}, bf16[256,2176]{1,0:T(8,128)(2,1)S(1)}, u32[]{:S(2)}, u32[]{:S(2)}) collective-permute-start(bf16[256,2176]{1,0:T(8,128)(2,1)} %get-tuple-element.160), channel_id=1, source_target_pairs={{0,1},{1,0},{2,3},{3,2},{4,5},{5,4},{6,7},{7,6},{8,9},{9,8},{10,11... | collective-permute-start | bytes 3342344 | tf_op jit(solution)/shard_map/ppermute | solution.py:34
  318.9 26.9 %collective-permute-start.78 = (bf16[256,2176]{1,0:T(8,128)(2,1)S(1)}, bf16[256,2176]{1,0:T(8,128)(2,1)S(1)}, u32[]{:S(2)}, u32[]{:S(2)}) collective-permute-start(bf16[256,2176]{1,0:T(8,128)(2,1)S(1)} %combined.27.refs_4_), channel_id=1, source_target_pairs={{0,2},{1,3},{2,0},{3,1},{4,6},{5,7},{6,4},{7,5},{8,10},{9,11},{10,... | collective-permute-start | bytes 3342344 | tf_op jit(solution)/shard_map/ppermute | solution.py:34
  343.3 31.4 %collective-permute-start.86 = (bf16[256,2048]{1,0:T(8,128)(2,1)}, bf16[256,2048]{1,0:T(8,128)(2,1)S(1)}, u32[]{:S(2)}, u32[]{:S(2)}) collective-permute-start(bf16[256,2048]{1,0:T(8,128)(2,1)} %get-tuple-element.174), channel_id=1, source_target_pairs={{0,1},{1,0},{2,3},{3,2},{4,5},{5,4},{6,7},{7,6},{8,9},{9,8},{10,11... | collective-permute-start | bytes 3145736 | tf_op jit(solution)/shard_map/ppermute | solution.py:34
  372.8 26.7 %collective-permute-start.85 = (bf16[128,2176]{1,0:T(8,128)(2,1)S(1)}, bf16[128,2176]{1,0:T(8,128)(2,1)}, u32[]{:S(2)}, u32[]{:S(2)}) collective-permute-start(bf16[128,2176]{1,0:T(8,128)(2,1)S(1)} %combined.30.refs_2_.refs_0_), channel_id=1, source_target_pairs={{0,16},{1,17},{2,18},{3,19},{4,20},{5,21},{6,22},{7,23},{8,24},{9,... | collective-permute-start | bytes 1671176 | tf_op jit(solution)/shard_map/ppermute | solution.py:34
  373.7 25.8 %collective-permute-start.84 = (bf16[128,2176]{1,0:T(8,128)(2,1)}, bf16[128,2176]{1,0:T(8,128)(2,1)}, u32[]{:S(2)}, u32[]{:S(2)}) collective-permute-start(bf16[128,2176]{1,0:T(8,128)(2,1)} %get-tuple-element.161.refs_3_), channel_id=1, source_target_pairs={{0,4},{1,5},{2,6},{3,7},{4,0},{5,1},{6,2},{7,3},{8,12},{9,13},{10,... | collective-permute-start | bytes 1671176 | tf_op jit(solution)/shard_map/ppermute | solution.py:34
  375.7 25.5 %collective-permute-start.89 = (bf16[128,2048]{1,0:T(8,128)(2,1)}, bf16[128,2048]{1,0:T(8,128)(2,1)S(1)}, u32[]{:S(2)}, u32[]{:S(2)}) collective-permute-start(bf16[128,2048]{1,0:T(8,128)(2,1)} %get-tuple-element.175.refs_4_), channel_id=1, source_target_pairs={{0,4},{1,5},{2,6},{3,7},{4,0},{5,1},{6,2},{7,3},{8,12},{9,13},{10,... | collective-permute-start | bytes 1572872 | tf_op jit(solution)/shard_map/ppermute | solution.py:34
  376.9 50.1 %collective-permute-start.79 = (bf16[256,2048]{1,0:T(8,128)(2,1)}, bf16[256,2048]{1,0:T(8,128)(2,1)S(1)}, u32[]{:S(2)}, u32[]{:S(2)}) collective-permute-start(bf16[256,2048]{1,0:T(8,128)(2,1)} %get-tuple-element.163), channel_id=1, source_target_pairs={{0,1},{1,0},{2,3},{3,2},{4,5},{5,4},{6,7},{7,6},{8,9},{9,8},{10,11... | collective-permute-start | bytes 3145736 | tf_op jit(solution)/shard_map/ppermute | solution.py:34
  378.3 48.7 %collective-permute-start.83 = (bf16[256,2048]{1,0:T(8,128)(2,1)S(1)}, bf16[256,2048]{1,0:T(8,128)(2,1)S(1)}, u32[]{:S(2)}, u32[]{:S(2)}) collective-permute-start(bf16[256,2048]{1,0:T(8,128)(2,1)S(1)} %combined.31.refs_6_), channel_id=1, source_target_pairs={{0,2},{1,3},{2,0},{3,1},{4,6},{5,7},{6,4},{7,5},{8,10},{9,11},{10,... | collective-permute-start | bytes 3145736 | tf_op jit(solution)/shard_map/ppermute | solution.py:34
  425.3 22.0 %collective-permute-start.95 = (bf16[128,2048]{1,0:T(8,128)(2,1)S(1)}, bf16[128,2048]{1,0:T(8,128)(2,1)S(1)}, u32[]{:S(2)}, u32[]{:S(2)}) collective-permute-start(bf16[128,2048]{1,0:T(8,128)(2,1)S(1)} %combined.36), channel_id=1, source_target_pairs={{0,2},{1,3},{2,0},{3,1},{4,6},{5,7},{6,4},{7,5},{8,10},{9,11},{10,... | collective-permute-start | bytes 1572872 | tf_op jit(solution)/shard_map/ppermute | solution.py:34
  450.9 51.7 %collective-permute-start.101 = (bf16[4,256,768]{2,1,0:T(8,128)(2,1)S(1)}, bf16[4,256,768]{2,1,0:T(8,128)(2,1)S(1)}, u32[]{:S(2)}, u32[]{:S(2)}) collective-permute-start(bf16[4,256,768]{2,1,0:T(8,128)(2,1)S(1)} %get-tuple-element.199.refs_12_), channel_id=1, source_target_pairs={{0,4},{1,5},{2,6},{3,7},{4,0},{5,1},{6,2},{7,3},{8,12},{9,13},{10,... | collective-permute-start | bytes 4718600 | tf_op jit(solution)/shard_map/ppermute | solution.py:34
  459.6 26.0 %collective-permute-start.97 = (bf16[128,2048]{1,0:T(8,128)(2,1)S(1)}, bf16[128,2048]{1,0:T(8,128)(2,1)S(1)}, u32[]{:S(2)}, u32[]{:S(2)}) collective-permute-start(bf16[128,2048]{1,0:T(8,128)(2,1)S(1)} %combined.37), channel_id=1, source_target_pairs={{0,16},{1,17},{2,18},{3,19},{4,20},{5,21},{6,22},{7,23},{8,24},{9,... | collective-permute-start | bytes 1572872 | tf_op jit(solution)/shard_map/ppermute | solution.py:34
  461.1 46.7 %collective-permute-start.120 = (bf16[256,2048]{1,0:T(8,128)(2,1)S(1)}, bf16[256,2048]{1,0:T(8,128)(2,1)S(1)}, u32[]{:S(2)}, u32[]{:S(2)}) collective-permute-start(bf16[256,2048]{1,0:T(8,128)(2,1)S(1)} %held.11), channel_id=1, source_target_pairs={{0,8},{1,9},{2,10},{3,11},{4,12},{5,13},{6,14},{7,15},{8,0},{9,1},... | collective-permute-start | bytes 3145736 | tf_op jit(solution)/shard_map/ppermute | solution.py:34
  473.1 29.4 %collective-permute-start.105 = (bf16[64,2048]{1,0:T(8,128)(2,1)S(1)}, bf16[64,2048]{1,0:T(8,128)(2,1)S(1)}, u32[]{:S(2)}, u32[]{:S(2)}) collective-permute-start(bf16[64,2048]{1,0:T(8,128)(2,1)S(1)} %combined.39), channel_id=1, source_target_pairs={{0,8},{1,9},{2,10},{3,11},{4,12},{5,13},{6,14},{7,15},{8,0},{9,1},... | collective-permute-start | bytes 786440 | tf_op jit(solution)/shard_map/ppermute | solution.py:34
  503.1 35.9 %collective-permute-start.106 = (bf16[2,256,768]{2,1,0:T(8,128)(2,1)S(1)}, bf16[2,256,768]{2,1,0:T(8,128)(2,1)S(1)}, u32[]{:S(2)}, u32[]{:S(2)}) collective-permute-start(bf16[2,256,768]{2,1,0:T(8,128)(2,1)S(1)} %get-tuple-element.204.refs_4_.refs_3_), channel_id=1, source_target_pairs={{0,16},{1,17},{2,18},{3,19},{4,20},{5,21},{6,22},{7,23},{8,24},{9,... | collective-permute-start | bytes 2359304 | tf_op jit(solution)/shard_map/ppermute | solution.py:34
  504.4 35.4 %collective-permute-start.111 = (f32[64,2048]{1,0:T(8,128)S(1)}, f32[64,2048]{1,0:T(8,128)}, u32[]{:S(2)}, u32[]{:S(2)}) collective-permute-start(f32[64,2048]{1,0:T(8,128)S(1)} %get-tuple-element.208), channel_id=1, source_target_pairs={{0,2},{1,3},{2,0},{3,1},{4,6},{5,7},{6,4},{7,5},{8,10},{9,11},{10,... | collective-permute-start | bytes 1572872 | tf_op jit(solution)/shard_map/ppermute | solution.py:34
  511.8 42.1 %collective-permute-start.121 = (bf16[4,256,256]{2,1,0:T(8,128)(2,1)}, bf16[4,256,256]{2,1,0:T(8,128)(2,1)}, u32[]{:S(2)}, u32[]{:S(2)}) collective-permute-start(bf16[4,256,256]{2,1,0:T(8,128)(2,1)} %get-tuple-element.231), channel_id=1, source_target_pairs={{0,4},{1,5},{2,6},{3,7},{4,0},{5,1},{6,2},{7,3},{8,12},{9,13},{10,... | collective-permute-start | bytes 1572872 | tf_op jit(solution)/shard_map/ppermute | solution.py:34
  539.8 22.7 %collective-permute-start.113 = (f32[64,2048]{1,0:T(8,128)S(1)}, f32[64,2048]{1,0:T(8,128)}, u32[]{:S(2)}, u32[]{:S(2)}) collective-permute-start(f32[64,2048]{1,0:T(8,128)S(1)} %get-tuple-element.208), channel_id=1, source_target_pairs={{0,1},{1,0},{2,3},{3,2},{4,5},{5,4},{6,7},{7,6},{8,9},{9,8},{10,11... | collective-permute-start | bytes 1572872 | tf_op jit(solution)/shard_map/ppermute | solution.py:34
  539.8 22.7 %collective-permute-start.112 = (f32[64,2048]{1,0:T(8,128)}, f32[64,2048]{1,0:T(8,128)}, u32[]{:S(2)}, u32[]{:S(2)}) collective-permute-start(f32[64,2048]{1,0:T(8,128)} %collective-permute-done.111), channel_id=1, source_target_pairs={{0,1},{1,0},{2,3},{3,2},{4,5},{5,4},{6,7},{7,6},{8,9},{9,8},{10,11... | collective-permute-start | bytes 1572872 | tf_op jit(solution)/shard_map/ppermute | solution.py:34
  553.9 24.7 %collective-permute-start.119 = (bf16[1,256,768]{2,1,0:T(8,128)(2,1)S(1)}, bf16[1,256,768]{2,1,0:T(8,128)(2,1)S(1)}, u32[]{:S(2)}, u32[]{:S(2)}) collective-permute-start(bf16[1,256,768]{2,1,0:T(8,128)(2,1)S(1)} %get-tuple-element.228.refs_2_), channel_id=1, source_target_pairs={{0,8},{1,9},{2,10},{3,11},{4,12},{5,13},{6,14},{7,15},{8,0},{9,1},... | collective-permute-start | bytes 1179656 | tf_op jit(solution)/shard_map/ppermute | solution.py:34
  (234 other events, 3194.9 us)
